TPU v7x, 32 devices: a whole 2x2x4 slice. The times are simulated.
32 devices in a mesh: dp: 4 (over z), seq: 8 (over y, x, core).
Axes of the slice: x: 2, y: 2, z: 4, core: 2. Of those that a mesh axis runs over, the one named last changes fastest.
Arguments:
- tokens: bfloat16 [32, 1024, 1024], P('dp', 'seq'), may hold values from -6 to 6
- ln1_gain: bfloat16 [1024], P(('dp', 'seq')), may hold values from 0.099609375 to 1.8984375
- ln1_shift: bfloat16 [1024], P(('dp', 'seq')), may hold values from -3 to 3
- ln2_gain: bfloat16 [1024], P(('dp', 'seq')), may hold values from 0.099609375 to 1.8984375
- ln2_shift: bfloat16 [1024], P(('dp', 'seq')), may hold values from -3 to 3
- qkv_weight: bfloat16 [1024, 3072], P(('dp', 'seq')), may hold values from -0.1875 to 0.1875
- qkv_bias: bfloat16 [3072], P(('dp', 'seq')), may hold values from -0.29882812 to 0.29882812
- out_weight: bfloat16 [1024, 1024], P(('dp', 'seq')), may hold values from -1.5 to 1.5
- out_bias: bfloat16 [1024], P(('dp', 'seq')), may hold values from -3 to 3
- in_weight: bfloat16 [1024, 4096], P(('dp', 'seq')), may hold values from -0.1875 to 0.1875
- in_bias: bfloat16 [4096], P(('dp', 'seq')), may hold values from -3 to 3
- down_weight: bfloat16 [4096, 1024], P(('dp', 'seq')), may hold values from -0.09375 to 0.09375
- down_bias: bfloat16 [1024], P(('dp', 'seq')), may hold values from -3 to 3
- cotangent: bfloat16 [32, 1024, 1024], P('dp', 'seq'), may hold values from -6 to 6
Outputs:
- output: bfloat16 [32, 1024, 1024], P('dp', 'seq')
- input_grad: float32 [32, 1024, 1024], P('dp', 'seq')
- ln1_gain_grad: float32 [1024], P(('dp', 'seq'))
- ln1_shift_grad: float32 [1024], P(('dp', 'seq'))
- ln2_gain_grad: float32 [1024], P(('dp', 'seq'))
- ln2_shift_grad: float32 [1024], P(('dp', 'seq'))
- qkv_weight_grad: float32 [1024, 3072], P(('dp', 'seq'))
- qkv_bias_grad: float32 [3072], P(('dp', 'seq'))
- out_weight_grad: float32 [1024, 1024], P(('dp', 'seq'))
- out_bias_grad: float32 [1024], P(('dp', 'seq'))
- in_weight_grad: float32 [1024, 4096], P(('dp', 'seq'))
- in_bias_grad: float32 [4096], P(('dp', 'seq'))
- down_weight_grad: float32 [4096, 1024], P(('dp', 'seq'))
- down_bias_grad: float32 [1024], P(('dp', 'seq'))
All inputs are finite; a program needn't handle non-finite values.
Results may differ from a plain program's by a relative error of at most 0.011.
Values may be sent and summed in bfloat16 or wider, within the bound.
No kernel may reach another device: no remote copies, remote signals or barrier semaphores. Data moves between devices by JAX's collectives and lax.ppermute only.
A program may use at most 192 MiB of HBM per device.

v0:
```python
import functools
import math

import jax
import jax.numpy as jnp
from jax import lax
from jax.experimental import pallas as pl
from jax.experimental.pallas import tpu as pltpu
from jax.sharding import Mesh
from jax.sharding import PartitionSpec as P


H = 16
HD = 64
ROT = 16
PAIR = 2 * HD
AXES = ("dp", "pl", "core")
CHIPS = ("dp", "pl")
BF = jnp.bfloat16
F32 = jnp.float32

epsilon = 1e-05


def dot_nn(left, right):
    return lax.dot_general(left, right, (((1,), (0,)), ((), ())), preferred_element_type=F32)


def dot_nt(left, right):
    return lax.dot_general(left, right, (((1,), (1,)), ((), ())), preferred_element_type=F32)


def dot_tn(left, right):
    return lax.dot_general(left, right, (((0,), (0,)), ((), ())), preferred_element_type=F32)


def rotary_lanes(length):
    lane = jnp.arange(PAIR, dtype=jnp.int32) % HD
    half = ROT // 2
    inverse = jnp.exp((lane % half).astype(F32) * (-2.0 * math.log(10000.0) / ROT))
    angles = jnp.arange(length, dtype=F32)[:, None] * inverse[None, :]
    turned = (lane < ROT)[None, :]
    first = (lane < half)[None, :]
    sines = jnp.sin(angles)
    return (
        jnp.where(turned, jnp.cos(angles), 1.0),
        jnp.where(first, -sines, 0.0),
        jnp.where(turned & ~first, sines, 0.0),
    )


def attention_kernel(
    block,
    qkv_ref,
    dc_ref,
    cos_ref,
    sin_a_ref,
    sin_b_ref,
    ctx_ref,
    dqkv_ref,
    q_s,
    k_s,
    km_s,
    vm_s,
    ctx_s,
    dq_s,
    dk_s,
    dv_s,
):
    length = qkv_ref.shape[1]
    half = ROT // 2
    factor = 1.0 / math.sqrt(HD)

    def turn(z, sign):
        swapped = pltpu.roll(z, PAIR - half, 1) * sin_a_ref[...] + pltpu.roll(z, half, 1) * sin_b_ref[...]
        return z * cos_ref[...] + sign * swapped

    q_s[...] = turn(qkv_ref[0, :, 0:PAIR].astype(F32), 1.0).astype(BF) * BF(factor)
    k_s[...] = turn(qkv_ref[0, :, PAIR : 2 * PAIR].astype(F32), 1.0).astype(BF)
    ctx_s[...] = jnp.zeros_like(ctx_s)
    dq_s[...] = jnp.zeros_like(dq_s)
    dk_s[...] = jnp.zeros_like(dk_s)
    dv_s[...] = jnp.zeros_like(dv_s)
    lane = lax.broadcasted_iota(jnp.int32, (1, PAIR), 1)

    def one_head(head, carry):
        chosen = ((lane >= head * HD) & (lane < head * HD + HD)).astype(BF)
        km_s[...] = k_s[...] * chosen
        vm_s[...] = qkv_ref[0, :, 2 * PAIR : 3 * PAIR] * chosen
        for i in range(length // block):
            lo, hi = i * block, (i + 1) * block
            queries = q_s[lo:hi, :] * chosen
            grads = dc_ref[0, lo:hi, :] * chosen
            scores = dot_nt(km_s[0:hi, :], queries)
            keys_at = lax.broadcasted_iota(jnp.int32, (block, block), 0)
            queries_at = lax.broadcasted_iota(jnp.int32, (block, block), 1)
            last = jnp.where(keys_at <= queries_at, scores[lo:hi, :], -1e30)
            scores = jnp.concatenate([scores[:lo, :], last], 0) if i else last
            highest = jnp.max(scores, axis=0, keepdims=True)
            weights = jnp.exp(scores - highest)
            weights = weights * (1.0 / jnp.sum(weights, axis=0, keepdims=True))
            low = weights.astype(BF)
            weight_grad = dot_nt(vm_s[0:hi, :], grads)
            mixed = jnp.sum(weights * weight_grad, axis=0, keepdims=True)
            score_grad = (weights * (weight_grad - mixed)).astype(BF)
            ctx_s[lo:hi, :] += dot_tn(low, vm_s[0:hi, :])
            dv_s[0:hi, :] += dot_nn(low, grads)
            dk_s[0:hi, :] += dot_nn(score_grad, queries)
            dq_s[lo:hi, :] += dot_tn(score_grad, km_s[0:hi, :])
        return carry

    lax.fori_loop(0, 2, one_head, 0)
    ctx_ref[0] = ctx_s[...].astype(BF)
    dqkv_ref[0, :, 0:PAIR] = turn(dq_s[...] * factor, -1.0).astype(BF)
    dqkv_ref[0, :, PAIR : 2 * PAIR] = turn(dk_s[...], -1.0).astype(BF)
    dqkv_ref[0, :, 2 * PAIR : 3 * PAIR] = dv_s[...].astype(BF)


def attention(qkv, context_grad, tables):
    seqs, length, width = qkv.shape
    pairs = width // (3 * PAIR)
    table = pl.BlockSpec((length, PAIR), lambda s, h: (0, 0))
    wide = pl.BlockSpec((1, length, 3 * PAIR), lambda s, h: (s, 0, h))
    slim = pl.BlockSpec((1, length, PAIR), lambda s, h: (s, 0, h))
    return pl.pallas_call(
        functools.partial(attention_kernel, math.gcd(length, 256)),
        out_shape=(
            jax.ShapeDtypeStruct((seqs, length, width // 3), BF),
            jax.ShapeDtypeStruct((seqs, length, width), BF),
        ),
        grid=(seqs, pairs),
        in_specs=[wide, slim, table, table, table],
        out_specs=(slim, wide),
        scratch_shapes=[pltpu.VMEM((length, PAIR), BF)] * 4 + [pltpu.VMEM((length, PAIR), F32)] * 4,
        cost_estimate=pl.CostEstimate(
            flops=seqs * pairs * 2 * 7 * length * length * PAIR,
            bytes_accessed=seqs * length * width * 6,
            transcendentals=seqs * pairs * length * length,
        ),
        compiler_params=pltpu.CompilerParams(vmem_limit_bytes=60 << 20),
    )(qkv, context_grad, *tables)


def norm_kernel(core_ref, mine_ref, theirs_ref, gains_ref, one_ref, two_ref, normed_ref):
    own = pl.program_id(2) == core_ref[0]
    x = jnp.where(own, mine_ref[0].astype(F32), theirs_ref[0].astype(F32))
    centred = x - jnp.mean(x, axis=-1, keepdims=True)
    normed = centred * lax.rsqrt(jnp.mean(centred * centred, axis=-1, keepdims=True) + epsilon)
    one_ref[...] = (normed * gains_ref[0:1, :] + gains_ref[1:2, :]).astype(BF)
    two_ref[...] = (normed * gains_ref[2:3, :] + gains_ref[3:4, :]).astype(BF)
    normed_ref[...] = normed.astype(BF)


def normalize(core, mine, theirs, gains, per_chip):
    blocks, rows, width = mine.shape
    planes = blocks // per_chip
    source = pl.BlockSpec((1, rows, width), lambda s, p, c, core: (p * per_chip + s, 0, 0))
    target = pl.BlockSpec((rows, width), lambda s, p, c, core: ((s * planes + p) * 2 + c, 0))
    shape = jax.ShapeDtypeStruct((2 * blocks * rows, width), BF)
    return pl.pallas_call(
        norm_kernel,
        out_shape=(shape, shape, shape),
        grid_spec=pltpu.PrefetchScalarGridSpec(
            num_scalar_prefetch=1,
            grid=(per_chip, planes, 2),
            in_specs=[source, source, pl.BlockSpec((4, width), lambda s, p, c, core: (0, 0))],
            out_specs=(target, target, target),
        ),
        cost_estimate=pl.CostEstimate(
            flops=20 * blocks * rows * width,
            bytes_accessed=20 * blocks * rows * width,
            transcendentals=0,
        ),
    )(core.reshape(1), mine, theirs, gains)


def dy_kernel(core_ref, mine_ref, theirs_ref, dy_ref):
    own = pl.program_id(2) == core_ref[0]
    dy_ref[...] = jnp.where(own, mine_ref[0].astype(F32), theirs_ref[0].astype(F32)).astype(BF)


def arrange_cotangent(core, mine, theirs, per_chip):
    blocks, rows, width = mine.shape
    planes = blocks // per_chip
    source = pl.BlockSpec((1, rows, width), lambda s, p, c, core: (p * per_chip + s, 0, 0))
    target = pl.BlockSpec((rows, width), lambda s, p, c, core: ((s * planes + p) * 2 + c, 0))
    count = 2 * blocks * rows
    return pl.pallas_call(
        dy_kernel,
        out_shape=jax.ShapeDtypeStruct((count, width), BF),
        grid_spec=pltpu.PrefetchScalarGridSpec(
            num_scalar_prefetch=1,
            grid=(per_chip, planes, 2),
            in_specs=[source, source],
            out_specs=target,
        ),
        cost_estimate=pl.CostEstimate(
            flops=count * width, bytes_accessed=6 * count * width, transcendentals=0
        ),
    )(core.reshape(1), mine, theirs)


def phi(u):
    density = jnp.exp(-0.5 * u * u) * (1.0 / math.sqrt(2.0 * math.pi))
    return 0.5 * (1.0 + lax.erf(u * math.sqrt(0.5))), density


def up_kernel(a_ref, low_ref, high_ref, bias_ref, z_ref, slope_ref):
    width = low_ref.shape[2]
    chunk = math.gcd(width, 512)
    a = a_ref[...]
    for half, w_ref in enumerate((low_ref, high_ref)):
        for start in range(0, width, chunk):
            weight = w_ref[:, :, start : start + chunk].reshape(a.shape[1], chunk)
            at = half * width + start
            u = dot_nn(a, weight) + bias_ref[:, at : at + chunk]
            cdf, density = phi(u)
            z_ref[:, at : at + chunk] = (u * cdf).astype(BF)
            slope_ref[:, at : at + chunk] = (cdf + u * density).astype(BF)


def half_specs(shared):
    chips, rows, width = shared.shape
    low = pl.BlockSpec((chips, rows // 4, width), lambda *i: (0, 0, 0))
    high = pl.BlockSpec((chips, rows // 4, width), lambda *i: (0, 1, 0))
    down = pl.BlockSpec((chips, rows // 2, width), lambda *i: (0, 1, 0))
    return low, high, down


def up_project(a, shared, bias, block):
    count, width = a.shape
    hidden = bias.shape[1]
    low, high, _ = half_specs(shared)
    wide = pl.BlockSpec((block, hidden), lambda i: (i, 0))
    shape = jax.ShapeDtypeStruct((count, hidden), BF)
    return pl.pallas_call(
        up_kernel,
        out_shape=(shape, shape),
        grid=(count // block,),
        in_specs=[
            pl.BlockSpec((block, width), lambda i: (i, 0)),
            low,
            high,
            pl.BlockSpec((1, hidden), lambda i: (0, 0)),
        ],
        out_specs=(wide, wide),
        cost_estimate=pl.CostEstimate(
            flops=2 * count * width * hidden,
            bytes_accessed=2 * (count * width + 2 * count * hidden + width * hidden),
            transcendentals=2 * count * hidden,
        ),
        compiler_params=pltpu.CompilerParams(vmem_limit_bytes=60 << 20),
    )(a, shared, shared, bias)


def dz_kernel(dy_ref, down_ref, slope_ref, du_ref, sum_ref):
    hidden = du_ref.shape[1]
    chunk = math.gcd(hidden, 512)
    width = dy_ref.shape[1]
    dy = dy_ref[...]
    _, rows, _ = down_ref.shape

    @pl.when(pl.program_id(0) == 0)
    def _():
        sum_ref[...] = jnp.zeros_like(sum_ref)

    for start in range(0, hidden, chunk):
        part = down_ref[start // rows : (start + chunk) // rows, :, :].reshape(chunk, width)
        slope = slope_ref[:, start : start + chunk].astype(F32)
        du = (dot_nt(dy, part) * slope).astype(BF)
        du_ref[:, start : start + chunk] = du
        sum_ref[:, start : start + chunk] += jnp.sum(du.astype(F32), 0, keepdims=True)


def down_pull(dy, shared, slope, block):
    count, width = dy.shape
    hidden = slope.shape[1]
    down = half_specs(shared)[2]
    wide = pl.BlockSpec((block, hidden), lambda i: (i, 0))
    return pl.pallas_call(
        dz_kernel,
        out_shape=(
            jax.ShapeDtypeStruct((count, hidden), BF),
            jax.ShapeDtypeStruct((1, hidden), F32),
        ),
        grid=(count // block,),
        in_specs=[pl.BlockSpec((block, width), lambda i: (i, 0)), down, wide],
        out_specs=(wide, pl.BlockSpec((1, hidden), lambda i: (0, 0))),
        cost_estimate=pl.CostEstimate(
            flops=2 * count * width * hidden,
            bytes_accessed=2 * (count * width + 2 * count * hidden + width * hidden),
            transcendentals=0,
        ),
        compiler_params=pltpu.CompilerParams(vmem_limit_bytes=60 << 20),
    )(dy, shared, slope)


def g_one_kernel(d_ref, w_ref, normed_ref, gain_ref, h_ref, sums_ref, bias_ref):
    @pl.when(pl.program_id(0) == 0)
    def _():
        sums_ref[...] = jnp.zeros_like(sums_ref)
        bias_ref[...] = jnp.zeros_like(bias_ref)

    d = d_ref[...]
    bias_ref[...] += jnp.sum(d.astype(F32), 0, keepdims=True)
    width = h_ref.shape[1]
    chunk = math.gcd(width, 512)
    for start in range(0, width, chunk):
        here = slice(start, start + chunk)
        g = dot_nt(d, w_ref[here, :])
        h_ref[:, here] = (g * gain_ref[:, here]).astype(BF)
        sums_ref[0:1, here] += jnp.sum(g * normed_ref[:, here].astype(F32), 0, keepdims=True)
        sums_ref[1:2, here] += jnp.sum(g, 0, keepdims=True)


def pull_one(d, weights, normed, gain, block):
    count, inner = d.shape
    width = gain.shape[1]
    return pl.pallas_call(
        g_one_kernel,
        out_shape=(
            jax.ShapeDtypeStruct((count, width), BF),
            jax.ShapeDtypeStruct((2, width), F32),
            jax.ShapeDtypeStruct((1, inner), F32),
        ),
        grid=(count // block,),
        in_specs=[
            pl.BlockSpec((block, inner), lambda i: (i, 0)),
            pl.BlockSpec((width, inner), lambda i: (0, 0)),
            pl.BlockSpec((block, width), lambda i: (i, 0)),
            pl.BlockSpec((1, width), lambda i: (0, 0)),
        ],
        out_specs=(
            pl.BlockSpec((block, width), lambda i: (i, 0)),
            pl.BlockSpec((2, width), lambda i: (0, 0)),
            pl.BlockSpec((1, inner), lambda i: (0, 0)),
        ),
        cost_estimate=pl.CostEstimate(
            flops=2 * count * width * inner,
            bytes_accessed=2 * count * (inner + 2 * width),
            transcendentals=0,
        ),
        compiler_params=pltpu.CompilerParams(vmem_limit_bytes=60 << 20),
    )(d, weights, normed, gain)


def split_rows(core, value_ref, kept_ref, sent_ref, cols, extra):
    planes, _, rows, _ = kept_ref.shape
    for p in range(planes):
        own = pl.ds(pl.multiple_of((2 * p + core) * rows, rows), rows)
        other = pl.ds(pl.multiple_of((2 * p + 1 - core) * rows, rows), rows)
        kept = value_ref[own, :]
        kept_ref[p, 0, :, cols] = kept if extra is None else kept + extra(p)
        sent_ref[p, 0, :, cols] = value_ref[other, :].astype(BF)


def g_two_kernel(
    core_ref, d_ref, low_ref, high_ref, normed_ref, gain_ref, h_ref, kept_ref, sent_ref, sums_ref, value_s
):
    @pl.when((pl.program_id(0) == 0) & (pl.program_id(1) == 0))
    def _():
        sums_ref[...] = jnp.zeros_like(sums_ref)

    _, rows, width = low_ref.shape
    chunk = value_s.shape[1]
    for start in range(0, width, chunk):
        here = slice(start, start + chunk)
        part = slice(start // rows, (start + chunk) // rows)
        g = dot_nt(d_ref[:, :width], low_ref[part, :, :].reshape(chunk, width))
        g += dot_nt(d_ref[:, width:], high_ref[part, :, :].reshape(chunk, width))
        value_s[...] = g * gain_ref[:, here] + h_ref[:, here].astype(F32)
        sums_ref[0:1, here] += jnp.sum(g * normed_ref[:, here].astype(F32), 0, keepdims=True)
        sums_ref[1:2, here] += jnp.sum(g, 0, keepdims=True)
        split_rows(core_ref[0], value_s, kept_ref, sent_ref, here, None)


def token_specs(planes, per_chip, rows, width, group):
    full = planes // group
    piece = pl.BlockSpec((group, 1, rows, width), lambda s, p, core: (p, s, 0, 0))

    def block(cols):
        return pl.BlockSpec((2 * group * rows, cols), lambda s, p, core: (s * full + p, 0))

    return (per_chip, full), piece, block


def pull_two(core, d, shared, normed, gain, h_one, planes, per_chip, rows):
    count, inner = d.shape
    width = gain.shape[1]
    group = math.gcd(planes, 2)
    grid, piece, block = token_specs(planes, per_chip, rows, width, group)
    low, high, _ = half_specs(shared)
    shape = (planes, per_chip, rows, width)
    return pl.pallas_call(
        g_two_kernel,
        out_shape=(
            jax.ShapeDtypeStruct(shape, F32),
            jax.ShapeDtypeStruct(shape, BF),
            jax.ShapeDtypeStruct((2, width), F32),
        ),
        grid_spec=pltpu.PrefetchScalarGridSpec(
            num_scalar_prefetch=1,
            grid=grid,
            in_specs=[
                block(inner),
                low,
                high,
                block(width),
                pl.BlockSpec((1, width), lambda s, p, core: (0, 0)),
                block(width),
            ],
            out_specs=(piece, piece, pl.BlockSpec((2, width), lambda s, p, core: (0, 0))),
            scratch_shapes=[pltpu.VMEM((2 * group * rows, math.gcd(width, 512)), F32)],
        ),
        cost_estimate=pl.CostEstimate(
            flops=2 * count * width * inner,
            bytes_accessed=2 * count * (inner + 4 * width),
            transcendentals=0,
        ),
        compiler_params=pltpu.CompilerParams(vmem_limit_bytes=60 << 20),
    )(core.reshape(1), d, shared, shared, normed, gain, h_one)


def out_kernel(
    core_ref, z_ref, down_ref, ctx_ref, out_ref, x_ref, bias_ref, kept_ref, sent_ref, value_s
):
    chips, rows, width = down_ref.shape
    chunk = value_s.shape[1]
    for start in range(0, width, chunk):
        here = slice(start, start + chunk)
        value_s[...] = dot_nn(z_ref[...], down_ref[:, :, here].reshape(chips * rows, chunk)) + dot_nn(
            ctx_ref[...], out_ref[:, here]
        )
        split_rows(
            core_ref[0],
            value_s,
            kept_ref,
            sent_ref,
            here,
            lambda p: x_ref[p, 0, :, here].astype(F32) + bias_ref[:, here],
        )


def out_project(core, z, shared, context, w_out, x_mine, bias, planes, per_chip, rows):
    count, hidden = z.shape
    inner, width = w_out.shape
    group = math.gcd(planes, 2)
    grid, piece, block = token_specs(planes, per_chip, rows, width, group)
    down = half_specs(shared)[2]
    shape = (planes, per_chip, rows, width)
    return pl.pallas_call(
        out_kernel,
        out_shape=(jax.ShapeDtypeStruct(shape, F32), jax.ShapeDtypeStruct(shape, BF)),
        grid_spec=pltpu.PrefetchScalarGridSpec(
            num_scalar_prefetch=1,
            grid=grid,
            in_specs=[
                block(hidden),
                down,
                block(inner),
                pl.BlockSpec((inner, width), lambda s, p, core: (0, 0)),
                piece,
                pl.BlockSpec((1, width), lambda s, p, core: (0, 0)),
            ],
            out_specs=(piece, piece),
            scratch_shapes=[pltpu.VMEM((2 * group * rows, math.gcd(width, 512)), F32)],
        ),
        cost_estimate=pl.CostEstimate(
            flops=2 * count * width * (hidden + inner),
            bytes_accessed=2 * count * (hidden + inner + 4 * width),
            transcendentals=0,
        ),
        compiler_params=pltpu.CompilerParams(vmem_limit_bytes=60 << 20),
    )(core.reshape(1), z, shared, context, w_out, x_mine.reshape(shape), bias)


def ordered(value, *before):
    return lax.optimization_barrier((value,) + before)[0]


def local(
    tokens,
    ln1_gain,
    ln1_shift,
    ln2_gain,
    ln2_shift,
    qkv_weight,
    qkv_bias,
    out_weight,
    out_bias,
    in_weight,
    in_bias,
    down_weight,
    down_bias,
    cotangent,
):
    planes = lax.axis_size("pl")
    chips = lax.axis_size("dp") * planes
    n = 2 * chips
    flat = (lax.axis_index("dp") * planes + lax.axis_index("pl")) * 2 + lax.axis_index("core")
    core = lax.axis_index("core")
    first_core = core == 0
    seqs, rows_here, width = tokens.shape
    per_chip = seqs // planes
    length = rows_here * planes * 2
    count = per_chip * length
    heads = H // 2
    qkv_cols = heads * 3 * HD
    ctx_cols = heads * HD
    hidden = in_weight.shape[1] // 2
    own_rows = qkv_weight.shape[0]

    def swap(value, mask):
        return lax.ppermute(value, AXES, [(i, i ^ mask) for i in range(n)])

    def in_core_order(own, other, axis):
        return jnp.where(
            first_core, jnp.concatenate([own, other], axis), jnp.concatenate([other, own], axis)
        )

    def pick(value, index, axis):
        return lax.dynamic_index_in_dim(value, index, axis, keepdims=False)

    qkv_halves = (
        qkv_weight.reshape(own_rows, 2, heads // 2, 2, 3, HD)
        .transpose(1, 0, 2, 4, 3, 5)
        .reshape(2, own_rows, qkv_cols)
    )
    out_halves = out_weight.reshape(own_rows, 2, ctx_cols).transpose(1, 0, 2)
    in_halves = (
        in_weight.reshape(own_rows, chips, 2, hidden // chips)
        .transpose(2, 0, 1, 3)
        .reshape(2, own_rows, hidden)
    )
    halves = jnp.concatenate([qkv_halves, out_halves, in_halves], 2)
    chip_rows = in_core_order(pick(halves, core, 0), swap(pick(halves, 1 - core, 0), 1), 0)
    first_cols = qkv_cols + ctx_cols
    first_all = lax.all_gather(chip_rows[:, :first_cols], CHIPS, axis=0, tiled=True)
    small = jnp.concatenate(
        [ln1_gain, ln1_shift, ln2_gain, ln2_shift, out_bias, down_bias, qkv_bias, in_bias]
    )
    small = jnp.broadcast_to(small[None, :], (n, small.shape[0]))
    small = ordered(small, chip_rows)
    small = lax.all_to_all(small, AXES, split_axis=0, concat_axis=0, tiled=True)
    small = small.astype(F32)
    part = width // n
    gain_one, shift_one, gain_two, shift_two, b_out, b_down = (
        small[:, i * part : (i + 1) * part].reshape(width) for i in range(6)
    )
    b_qkv = small[:, 6 * part : 9 * part].reshape(2, heads // 2, 2, 3, HD)
    b_qkv = pick(b_qkv, core, 0).transpose(0, 2, 1, 3).reshape(qkv_cols)
    b_in = pick(small[:, 9 * part :].reshape(chips, 2, hidden // chips), core, 1).reshape(hidden)

    second = jnp.concatenate(
        [
            chip_rows[:, first_cols : first_cols + width],
            chip_rows[:, first_cols + width :],
            down_weight,
        ],
        0,
    )
    shared = lax.all_gather(second[None], CHIPS, axis=0, tiled=True)
    other_rows = lax.dynamic_slice(first_all, ((1 - core) * ctx_cols, qkv_cols), (ctx_cols, ctx_cols))
    some_rows = lax.dynamic_slice(first_all, (core * ctx_cols, qkv_cols), (ctx_cols, ctx_cols))
    w_out = in_core_order(some_rows, swap(other_rows, 1), 1)
    w_qkv = first_all[:, :qkv_cols]

    def to_chip(value):
        mine = lax.all_to_all(value, "pl", split_axis=0, concat_axis=0, tiled=True)
        return mine, swap(mine, 1)

    def to_tokens(kept, sent):
        value = (kept + swap(sent, 1).astype(F32)).astype(BF)
        value = value.reshape(seqs, rows_here, width)
        return lax.all_to_all(value, "pl", split_axis=0, concat_axis=0, tiled=True)

    x_mine, x_theirs = to_chip(ordered(tokens, chip_rows))
    dy_mine, dy_theirs = to_chip(ordered(cotangent, x_mine))
    gains = jnp.stack([gain_one, shift_one, gain_two, shift_two])
    dy = arrange_cotangent(core, dy_mine, dy_theirs, per_chip)
    a_one, a_two, normed = normalize(core, x_mine, x_theirs, gains, per_chip)

    qkv = (dot_nn(a_one, w_qkv) + b_qkv).astype(BF)
    context_grad = dot_nt(dy, w_out).astype(BF)
    context, qkv_grad = attention(
        qkv.reshape(per_chip, length, qkv_cols),
        context_grad.reshape(per_chip, length, ctx_cols),
        rotary_lanes(length),
    )
    context = context.reshape(count, ctx_cols)
    qkv_grad = qkv_grad.reshape(count, qkv_cols)

    chip_bits = chips.bit_length() - 1
    plane_bits = planes.bit_length() - 1

    def scatter_sum(value, order):
        cols = value.shape[1]
        value = value.reshape((2,) * chip_bits + (value.shape[0] // chips, cols))
        left = list(range(chip_bits, 0, -1))
        for step, bit in enumerate(order):
            axis = left.index(bit)
            left.remove(bit)
            mine = (flat >> bit) & 1
            sent = swap(pick(value, 1 - mine, axis).astype(BF), 1 << bit)
            value = pick(value, mine, axis).astype(F32) + sent.astype(F32)
            if step < len(order) - 1:
                value = value.astype(BF)
        return value

    plane_up = list(range(1, plane_bits + 1))
    plane_down = plane_up[::-1]
    beyond = list(range(plane_bits + 1, chip_bits + 1))
    orders = {
        "sda": plane_up + beyond,
        "sdb": beyond + plane_down,
        "sia": plane_down + beyond,
        "sib": beyond + plane_up,
    }

    def scatter_two_ways(value, tag):
        cols = value.shape[1] // 2
        return jnp.concatenate(
            [
                scatter_sum(value[:, :cols], orders[tag + "a"]),
                scatter_sum(value[:, cols:], orders[tag + "b"]),
            ],
            1,
        )

    def own_rows_of(value):
        value = value.reshape(2, own_rows, value.shape[1])
        return in_core_order(
            pick(value, core, 0)[:, None], swap(pick(value, 1 - core, 0), 1)[:, None], 1
        )

    out_w_grad = dot_tn(context, dy).astype(BF)
    other_cols = lax.dynamic_slice_in_dim(out_w_grad, (1 - core) * ctx_cols, ctx_cols, 1)
    own_cols = lax.dynamic_slice_in_dim(out_w_grad, core * ctx_cols, ctx_cols, 1)
    out_w_grad = in_core_order(own_cols, swap(other_cols, 1), 0)
    qkv_w_grad = dot_tn(a_one, qkv_grad).astype(BF)
    first_grad = jnp.concatenate([qkv_w_grad, out_w_grad], 1)
    first_grad = lax.psum_scatter(first_grad, CHIPS, scatter_dimension=0, tiled=True)
    first_grad = own_rows_of(first_grad.astype(F32))
    qkv_w_grad = (
        first_grad[:, :, :qkv_cols]
        .reshape(own_rows, 2, heads // 2, 3, 2, HD)
        .transpose(0, 1, 2, 4, 3, 5)
        .reshape(own_rows, 2 * qkv_cols)
    )
    out_w_grad = first_grad[:, :, qkv_cols:].reshape(own_rows, width)
    block = math.gcd(count, 512)
    h_one, sums_one, qkv_b_grad = pull_one(qkv_grad, first_all, normed, gain_one[None], block)

    z, slope = up_project(a_two, shared, b_in[None], block)
    down_w_grad = dot_tn(z, dy).astype(BF)
    down_w_grad = scatter_two_ways(down_w_grad, "sd")
    du, in_b_grad = down_pull(dy, shared, slope, block)
    in_w_grad = dot_tn(a_two, du).astype(BF)
    in_w_grad = own_rows_of(scatter_two_ways(in_w_grad, "si"))
    in_w_grad = (
        in_w_grad.reshape(own_rows, 2, chips, hidden // chips)
        .transpose(0, 2, 1, 3)
        .reshape(own_rows, 2 * hidden)
    )
    kept, sent, sums_two = pull_two(
        core, du, shared, normed, gain_two[None], h_one, planes, per_chip, rows_here
    )
    combined = to_tokens(kept, sent)
    kept, sent = out_project(
        core, z, shared, context, w_out, x_mine, (b_out + b_down)[None], planes, per_chip, rows_here
    )
    output = to_tokens(kept, sent)

    x_here = tokens.astype(F32)
    mean_here = jnp.mean(x_here, axis=-1, keepdims=True)
    centred_here = x_here - mean_here
    scale_here = lax.rsqrt(jnp.mean(centred_here * centred_here, axis=-1, keepdims=True) + epsilon)
    normed_here = centred_here * scale_here
    combined = combined.astype(F32)
    pulled = (
        combined
        - jnp.mean(combined, axis=-1, keepdims=True)
        - normed_here * jnp.mean(combined * normed_here, axis=-1, keepdims=True)
    ) * scale_here
    dy_here = cotangent.astype(F32)
    input_grad = dy_here + pulled

    qkv_b_grad = (
        qkv_b_grad.reshape(heads // 2, 3, 2, HD)
        .transpose(0, 2, 1, 3)
        .reshape(qkv_cols)
    )
    nothing = jnp.zeros_like(qkv_b_grad)
    qkv_b_grad = in_core_order(qkv_b_grad, nothing, 0)
    in_b_grad = in_b_grad.reshape(chips, hidden // chips)
    in_b_grad = in_core_order(in_b_grad[:, None], jnp.zeros_like(in_b_grad)[:, None], 1)
    sums = [
        sums_one[0],
        sums_one[1],
        sums_two[0],
        sums_two[1],
        jnp.sum(dy_here, (0, 1)),
        qkv_b_grad,
        in_b_grad,
    ]
    sums = jnp.concatenate([value.reshape(n, -1) for value in sums], 1)
    sums = lax.all_to_all(sums, AXES, split_axis=0, concat_axis=0, tiled=True)
    sums = jnp.sum(sums, 0)
    b_grad = sums[4 * part : 5 * part]
    return (
        output,
        input_grad,
        sums[:part],
        sums[part : 2 * part],
        sums[2 * part : 3 * part],
        sums[3 * part : 4 * part],
        qkv_w_grad,
        sums[5 * part : 8 * part],
        out_w_grad,
        b_grad,
        in_w_grad,
        sums[8 * part :],
        down_w_grad,
        b_grad,
    )


def solution(mesh):
    split = Mesh(
        mesh.devices.reshape(mesh.shape["dp"], mesh.shape["seq"] // 2, 2),
        AXES,
    )
    rows = P("dp", ("pl", "core"), None)
    vector = P(AXES)
    matrix = P(AXES, None)
    return jax.shard_map(
        local,
        mesh=split,
        in_specs=(
            rows,
            vector,
            vector,
            vector,
            vector,
            matrix,
            vector,
            matrix,
            vector,
            matrix,
            vector,
            matrix,
            vector,
            rows,
        ),
        out_specs=(
            rows,
            rows,
            vector,
            vector,
            vector,
            vector,
            matrix,
            vector,
            matrix,
            vector,
            matrix,
            vector,
            matrix,
            vector,
        ),
        check_vma=False,
    )
```

profile of v0, /device:TPU:13, one launch (start us, length us, event | category | flops | bytes accessed | tf_op | source)
XLA Modules:
  0.0 521.2 jit_solution(13482751556327023854)
XLA Ops:
  9.4 1.5 reshape.252
  14.5 1.8 pad_maximum_fusion.2
  16.4 29.6 %all_to_all.38.mine_ref = bf16[8,128,1024]{2,1,0:T(8,128)(2,1)} all-to-all(bf16[8,128,1024]{2,1,0:T(8,128)(2,1)S(1)} %copy-done), channel_id=1, replica_groups=mesh['dp'=4,'pl'=4,'core'=2] {'pl'}, dimensions={0} | all-to-all | bytes 4194304 | tf_op jit(solution)/shard_map/all_to_all | solution.py:569
  46.0 4.7 all-to-all-start.2
  50.8 2.4 collective-permute-start.1
  53.2 31.2 %all-to-all-done.2.mine_ref = bf16[8,128,1024]{2,1,0:T(8,128)(2,1)} async-done(((bf16[8,128,1024]{2,1,0:T(8,128)(2,1)}), bf16[8,128,1024]{2,1,0:T(8,128)(2,1)}, u32[]{:S(2)}, u32[]{:S(2)}) %all-to-all-start.2) | async-done | bytes 2097184 | tf_op jit(solution)/shard_map/all_to_all | solution.py:569
  84.4 3.1 collective-permute-start.2
  87.9 3.0 fusion.22
  93.5 4.8 all-to-all-start.1
  99.1 4.6 all-to-all-done.1
  106.5 15.0 %shard_map.245 = (bf16[2048,1024]{1,0:T(8,128)(2,1)}, bf16[2048,1024]{1,0:T(8,128)(2,1)}, bf16[2048,1024]{1,0:T(8,128)(2,1)}) custom-call(s32[1]{0:T(128)} %bitcast.core_ref, bf16[8,128,1024]{2,1,0:T(8,128)(2,1)} %all_to_all.38.mine_ref, bf16[8,128,1024]{2,1,0:T(8,128)(2,1)} %collective-permute-done.1.theirs_ref, f32[4,1024]{1,0:T(4,128)} %pad_maximum_fusion.5.gains_ref), custom_call_target="tpu_custom_call" | custom-call | flops 20971520 | bytes 20971520 | tf_op jit(solution)/shard_map/pallas_call | solution.py:160
  121.5 11.0 %shard_map.247.dy_ref = bf16[2048,1024]{1,0:T(8,128)(2,1)} custom-call(s32[1]{0:T(128)} %bitcast.core_ref, bf16[8,128,1024]{2,1,0:T(8,128)(2,1)} %all-to-all-done.2.mine_ref, bf16[8,128,1024]{2,1,0:T(8,128)(2,1)} %collective-permute-done.2.theirs_ref), custom_call_target="tpu_custom_call" | custom-call | flops 2097152 | bytes 12582912 | tf_op jit(solution)/shard_map/pallas_call | solution.py:188
  134.6 12.0 %add_convert_fusion = bf16[2048,1536]{1,0:T(8,128)(2,1)} fusion(bf16[2048,1024]{1,0:T(8,128)(2,1)} %get-tuple-element.38, f32[1536]{0:T(1024)S(1)} %add.234, bf16[1024,2048]{1,0:T(8,128)(2,1)} %all-gather.4.cloned.1.call-done.w_ref), kind=kOutput, calls=%fused_computation | convolution fusion | flops 6448742400 | bytes 13637632 | tf_op jit(solution)/shard_map/dot_general | solution.py:26
  146.9 3.8 convolution_convert_fusion.3
  150.7 72.1 %shard_map.248 = (bf16[2,1024,512]{2,1,0:T(8,128)(2,1)}, bf16[2,1024,1536]{2,1,0:T(8,128)(2,1)}) custom-call(bf16[2,1024,1536]{2,1,0:T(8,128)(2,1)} %bitcast.201, bf16[2,1024,512]{2,1,0:T(8,128)(2,1)} %bitcast.204, f32[1024,128]{1,0:T(8,128)} %get-tuple-element.94.cos_ref, f32[1024,128]{1,0:T(8,128)} %get-tuple-element.93.sin_a_ref, ...), custom_call_target="tpu_custom_call" | custom-call | flops 15032385536 | bytes 18874368 | tf_op jit(solution)/shard_map/pallas_call | solution.py:125
  222.8 5.3 %convolution_convert_fusion.4 = bf16[512,1024]{1,0:T(8,128)(2,1)S(1)} fusion(bf16[2048,512]{1,0:T(8,128)(2,1)} %bitcast.202, bf16[2048,1024]{1,0:T(8,128)(2,1)} %shard_map.247.dy_ref), kind=kOutput, calls=%fused_computation.31 | convolution fusion | flops 2148007936 | bytes 7340032 | tf_op jit(solution)/shard_map/dot_general | solution.py:34
  229.3 7.1 %convolution_convert_fusion = bf16[1024,1536]{1,0:T(8,128)(2,1)S(1)} fusion(bf16[2048,1024]{1,0:T(8,128)(2,1)S(1)} %copy-done.37, bf16[2048,1536]{1,0:T(8,128)(2,1)S(1)} %bitcast.200), kind=kOutput, calls=%fused_computation.18 | convolution fusion | flops 6444023808 | bytes 13631488 | tf_op jit(solution)/shard_map/dot_general | solution.py:34
  236.4 11.6 %shard_map.251 = (bf16[2048,1024]{1,0:T(8,128)(2,1)}, f32[2,1024]{1,0:T(2,128)}, f32[1,1536]{1,0:T(1,128)}) custom-call(bf16[2048,1536]{1,0:T(8,128)(2,1)} %bitcast.199, bf16[1024,2048]{1,0:T(8,128)(2,1)} %all-gather.4.cloned.1.call-done.w_ref, bf16[2048,1024]{1,0:T(8,128)(2,1)} %get-tuple-element.45.normed_ref, f32[1,1024]{1,0:T(1,128)} %copy-done.25), custom_call_target="tpu_custom_call" | custom-call | flops 6442450944 | bytes 14680064 | tf_op jit(solution)/shard_map/pallas_call | solution.py:319
  251.1 1.8 maximum_select_fusion.1
  252.9 2.7 pad_maximum_fusion
  255.6 19.5 %shard_map.246 = (bf16[2048,2048]{1,0:T(8,128)(2,1)}, bf16[2048,2048]{1,0:T(8,128)(2,1)}) custom-call(bf16[2048,1024]{1,0:T(8,128)(2,1)} %get-tuple-element.36.a_ref, bf16[16,256,1024]{2,1,0:T(8,128)(2,1)} %bitcast.167, bf16[16,256,1024]{2,1,0:T(8,128)(2,1)} %bitcast.168, f32[1,2048]{1,0:T(1,128)} %fusion.23.bias_ref), custom_call_target="tpu_custom_call" | custom-call | flops 8589934592 | bytes 25165824 | tf_op jit(solution)/shard_map/pallas_call | solution.py:236
  275.2 13.1 %convolution_convert_fusion.2 = bf16[2048,1024]{1,0:T(8,128)(2,1)S(1)} fusion(bf16[2048,2048]{1,0:T(8,128)(2,1)} %get-tuple-element.37.z_ref, bf16[2048,1024]{1,0:T(8,128)(2,1)} %shard_map.247.dy_ref), kind=kOutput, calls=%fused_computation.20 | convolution fusion | flops 8592031744 | bytes 16777216 | tf_op jit(solution)/shard_map/dot_general | solution.py:34
  289.8 15.0 %shard_map.250 = (bf16[2048,2048]{1,0:T(8,128)(2,1)}, f32[1,2048]{1,0:T(1,128)}) custom-call(bf16[2048,1024]{1,0:T(8,128)(2,1)} %shard_map.247.dy_ref, bf16[16,256,1024]{2,1,0:T(8,128)(2,1)} %bitcast.169, bf16[2048,2048]{1,0:T(8,128)(2,1)} %get-tuple-element.43.slope_ref), custom_call_target="tpu_custom_call" | custom-call | flops 8589934592 | bytes 25165824 | tf_op jit(solution)/shard_map/pallas_call | solution.py:280
  304.8 12.9 %convolution_convert_fusion.1 = bf16[1024,2048]{1,0:T(8,128)(2,1)S(1)} fusion(bf16[2048,1024]{1,0:T(8,128)(2,1)} %get-tuple-element.36.a_ref, bf16[2048,2048]{1,0:T(8,128)(2,1)} %get-tuple-element.44.d_ref), kind=kOutput, calls=%fused_computation.19 | convolution fusion | flops 8592031744 | bytes 16777216 | tf_op jit(solution)/shard_map/dot_general | solution.py:34
  325.4 15.7 %shard_map.252 = (f32[4,2,128,1024]{3,2,1,0:T(8,128)}, bf16[4,2,128,1024]{3,2,1,0:T(8,128)(2,1)}, f32[2,1024]{1,0:T(2,128)}) custom-call(s32[1]{0:T(128)} %bitcast.core_ref, bf16[2048,2048]{1,0:T(8,128)(2,1)} %get-tuple-element.44.d_ref, bf16[16,256,1024]{2,1,0:T(8,128)(2,1)} %bitcast.170, bf16[16,256,1024]{2,1,0:T(8,128)(2,1)} %bitcast.171, ...), custom_call_target="tpu_custom_call" | custom-call | flops 8589934592 | bytes 25165824 | tf_op jit(solution)/shard_map/pallas_call | solution.py:394
  341.1 1.6 collective-permute-start.5
  342.6 16.8 %shard_map.249 = (f32[4,2,128,1024]{3,2,1,0:T(8,128)}, bf16[4,2,128,1024]{3,2,1,0:T(8,128)(2,1)}) custom-call(s32[1]{0:T(128)} %bitcast.core_ref, bf16[2048,2048]{1,0:T(8,128)(2,1)} %get-tuple-element.37.z_ref, bf16[16,256,1024]{2,1,0:T(8,128)(2,1)} %bitcast.172, bf16[2048,512]{1,0:T(8,128)(2,1)} %bitcast.203, bf16[512,1024]{1,0:T(8,128)(2,1)} %copy-done.17, ...), custom_call_target="tpu_custom_call" | custom-call | flops 10737418240 | bytes 27262976 | tf_op jit(solution)/shard_map/pallas_call | solution.py:451
  361.5 1.9 fusion.10
  364.7 1.6 fusion.11
  368.7 21.8 %collective-permute-start.9 = (bf16[2,2,64,1024]{3,2,0,1:T(8,128)(2,1)}, bf16[2,2,64,1024]{3,2,0,1:T(8,128)(2,1)}, u32[]{:S(2)}, u32[]{:S(2)}) collective-permute-start(bf16[2,2,64,1024]{3,2,0,1:T(8,128)(2,1)} %dynamic-slice_bitcast_fusion.5), channel_id=1, source_target_pairs={{0,2},{1,3},{2,0},{3,1},{4,6},{5,7},{6,4},{7,5},{8,10},{9,11},{10,... | collective-permute-start | bytes 1572872 | tf_op jit(solution)/shard_map/ppermute | solution.py:514
  390.5 1.5 fusion.8
  394.1 1.5 fusion.9
  397.5 4.6 collective-permute-done.9
  404.2 1.8 collective-permute-start.7
  408.8 7.7 %collective-permute-done.22 = bf16[2,2,128,512]{3,2,1,0:T(8,128)(2,1)} collective-permute-done((bf16[2,2,128,512]{3,2,1,0:T(8,128)(2,1)}, bf16[2,2,128,512]{3,2,1,0:T(8,128)(2,1)}, u32[]{:S(2)}, u32[]{:S(2)}) %collective-permute-start.22) | collective-permute-done | bytes 524320 | tf_op jit(solution)/shard_map/ppermute | solution.py:514
  417.7 3.9 collective-permute-start.10
  435.6 3.8 add_convert_fusion.1
  439.4 5.3 %all-to-all-start.4 = ((bf16[8,128,1024]{2,1,0:T(8,128)(2,1)}), bf16[8,128,1024]{2,1,0:T(8,128)(2,1)}, u32[]{:S(2)}, u32[]{:S(2)}) async-start(bf16[8,128,1024]{2,1,0:T(8,128)(2,1)} %bitcast.19), calls=%async_computation.4 | async-start | bytes 4194304 | tf_op jit(solution)/shard_map/all_to_all | solution.py:575
  444.9 5.0 collective-permute-start.16
  449.9 5.0 add_convert_fusion.2
  454.8 12.7 %all-to-all-done.4 = bf16[8,128,1024]{2,1,0:T(8,128)(2,1)} async-done(((bf16[8,128,1024]{2,1,0:T(8,128)(2,1)}), bf16[8,128,1024]{2,1,0:T(8,128)(2,1)}, u32[]{:S(2)}, u32[]{:S(2)}) %all-to-all-start.4) | async-done | bytes 2097184 | tf_op jit(solution)/shard_map/all_to_all | solution.py:575
  467.5 6.1 %all-to-all-start.3 = ((bf16[8,128,1024]{2,1,0:T(8,128)(2,1)}), bf16[8,128,1024]{2,1,0:T(8,128)(2,1)}, u32[]{:S(2)}, u32[]{:S(2)}) async-start(bf16[8,128,1024]{2,1,0:T(8,128)(2,1)} %bitcast.180), calls=%async_computation.3 | async-start | bytes 4194304 | tf_op jit(solution)/shard_map/all_to_all | solution.py:575
  476.1 3.5 convert_reduce_fusion
  479.7 4.4 convert_reduce_fusion.2
  485.0 12.0 %all-to-all-done.3 = bf16[8,128,1024]{2,1,0:T(8,128)(2,1)} async-done(((bf16[8,128,1024]{2,1,0:T(8,128)(2,1)}), bf16[8,128,1024]{2,1,0:T(8,128)(2,1)}, u32[]{:S(2)}, u32[]{:S(2)}) %all-to-all-start.3) | async-done | bytes 2097184 | tf_op jit(solution)/shard_map/all_to_all | solution.py:575
  497.0 6.8 %all-to-all-start.5 = ((f32[32,1,384]{2,1,0:T(1,128)}), f32[32,1,384]{2,1,0:T(1,128)S(1)}, u32[]{:S(2)}, u32[]{:S(2)}) async-start(f32[32,1,384]{2,1,0:T(1,128)} %copy.92), calls=%async_computation.5 | async-start | bytes 98304 | tf_op jit(solution)/shard_map/all_to_all | solution.py:707
  505.8 3.3 all-to-all-done.5
  511.3 3.1 copy.128
  (241 shorter events, 65.1 us)
Async XLA Ops:
  7.2 125.3 %all-gather.4.cloned.1.call-start = ((), (), s32[]{:S(2)}) async-start(), calls=%async_computation.7 | async-start | bytes 4456448 | tf_op jit(solution)/shard_map/all_gather | solution.py:538
  11.7 1.9 collective-permute-start
  14.4 241.2 %all-gather.6.cloned.1.call-start = ((), (), s32[]{:S(2)}) async-start(), calls=%async_computation.9 | async-start | bytes 8912896 | tf_op jit(solution)/shard_map/all_gather | solution.py:562
  16.3 34.3 %copy-start.28 = (bf16[32]{0:T(256)(128)(2,1)S(1)}, bf16[32]{0:T(256)(128)(2,1)}, u32[]{:S(2)}) copy-start(bf16[32]{0:T(256)(128)(2,1)} %param.15) | copy-start | bytes 196
  16.3 34.3 %copy-start.29 = (bf16[32]{0:T(256)(128)(2,1)S(1)}, bf16[32]{0:T(256)(128)(2,1)}, u32[]{:S(2)}) copy-start(bf16[32]{0:T(256)(128)(2,1)} %param.16) | copy-start | bytes 196
  16.3 34.3 %copy-start.30 = (bf16[32]{0:T(256)(128)(2,1)S(1)}, bf16[32]{0:T(256)(128)(2,1)}, u32[]{:S(2)}) copy-start(bf16[32]{0:T(256)(128)(2,1)} %param.17) | copy-start | bytes 196
  16.3 34.3 %copy-start.31 = (bf16[32]{0:T(256)(128)(2,1)S(1)}, bf16[32]{0:T(256)(128)(2,1)}, u32[]{:S(2)}) copy-start(bf16[32]{0:T(256)(128)(2,1)} %param.18) | copy-start | bytes 196
  16.4 34.3 %copy-start.32 = (bf16[32]{0:T(256)(128)(2,1)S(1)}, bf16[32]{0:T(256)(128)(2,1)}, u32[]{:S(2)}) copy-start(bf16[32]{0:T(256)(128)(2,1)} %param.22) | copy-start | bytes 196
  16.4 34.3 %copy-start.33 = (bf16[32]{0:T(256)(128)(2,1)S(1)}, bf16[32]{0:T(256)(128)(2,1)}, u32[]{:S(2)}) copy-start(bf16[32]{0:T(256)(128)(2,1)} %param.26) | copy-start | bytes 196
  16.4 34.3 %copy-start.34 = (bf16[96]{0:T(256)(128)(2,1)S(1)}, bf16[96]{0:T(256)(128)(2,1)}, u32[]{:S(2)}) copy-start(bf16[96]{0:T(256)(128)(2,1)} %param.20) | copy-start | bytes 580
  16.4 34.3 %copy-start.35 = (bf16[128]{0:T(256)(128)(2,1)S(1)}, bf16[128]{0:T(256)(128)(2,1)}, u32[]{:S(2)}) copy-start(bf16[128]{0:T(256)(128)(2,1)} %param.24) | copy-start | bytes 772
  46.0 38.5 %all-to-all-start.2 = ((bf16[8,128,1024]{2,1,0:T(8,128)(2,1)}), bf16[8,128,1024]{2,1,0:T(8,128)(2,1)}, u32[]{:S(2)}, u32[]{:S(2)}) async-start(bf16[8,128,1024]{2,1,0:T(8,128)(2,1)} %param.27), calls=%async_computation.2 | async-start | bytes 4194304 | tf_op jit(solution)/shard_map/all_to_all | solution.py:569
  50.8 55.6 %collective-permute-start.1 = (bf16[8,128,1024]{2,1,0:T(8,128)(2,1)}, bf16[8,128,1024]{2,1,0:T(8,128)(2,1)}, u32[]{:S(2)}, u32[]{:S(2)}) collective-permute-start(bf16[8,128,1024]{2,1,0:T(8,128)(2,1)} %all_to_all.38.mine_ref), channel_id=1, source_target_pairs={{0,1},{1,0},{2,3},{3,2},{4,5},{5,4},{6,7},{7,6},{8,9},{9,8},{10,11... | collective-permute-start | bytes 6291464 | tf_op jit(solution)/shard_map/ppermute | solution.py:514
  84.4 37.1 %collective-permute-start.2 = (bf16[8,128,1024]{2,1,0:T(8,128)(2,1)}, bf16[8,128,1024]{2,1,0:T(8,128)(2,1)}, u32[]{:S(2)}, u32[]{:S(2)}) collective-permute-start(bf16[8,128,1024]{2,1,0:T(8,128)(2,1)} %all-to-all-done.2.mine_ref), channel_id=1, source_target_pairs={{0,1},{1,0},{2,3},{3,2},{4,5},{5,4},{6,7},{7,6},{8,9},{9,8},{10,11... | collective-permute-start | bytes 6291464 | tf_op jit(solution)/shard_map/ppermute | solution.py:514
  93.5 10.2 %all-to-all-start.1 = ((bf16[32,2,208]{2,1,0:T(2,128)(2,1)}), bf16[32,2,208]{2,1,0:T(2,128)(2,1)S(1)}, u32[]{:S(2)}, u32[]{:S(2)}) async-start(bf16[32,2,208]{2,1,0:T(2,128)(2,1)} %reshape.325), calls=%async_computation.1 | async-start | bytes 65536 | tf_op jit(solution)/shard_map/all_to_all | solution.py:544
  98.3 298.2 %reduce-scatter.2.cloned.1.call-start = ((), (), s32[]{:S(2)}) async-start(), calls=%async_computation.8 | async-start | bytes 4456448 | tf_op jit(solution)/shard_map/reduce_scatter | solution.py:642
  105.0 27.5 %copy-start.24 = (f32[1,1024]{1,0:T(1,128)}, f32[1,1024]{1,0:T(1,128)S(1)}, u32[]{:S(2)}) copy-start(f32[1,1024]{1,0:T(1,128)S(1)} %stack_reshape.14.gain_ref) | copy-start | bytes 12292
  105.1 27.4 %copy-start.25 = (f32[1,1024]{1,0:T(1,128)}, f32[1,1024]{1,0:T(1,128)S(1)}, u32[]{:S(2)}) copy-start(f32[1,1024]{1,0:T(1,128)S(1)} %stack_reshape.12.gain_ref) | copy-start | bytes 12292
  133.8 12.8 %collective-permute-start.3 = (bf16[512,512]{1,0:T(8,128)(2,1)S(1)}, bf16[512,512]{1,0:T(8,128)(2,1)S(1)}, u32[]{:S(2)}, u32[]{:S(2)}) collective-permute-start(bf16[512,512]{1,0:T(8,128)(2,1)S(1)} %get-tuple-element.65), channel_id=1, source_target_pairs={{0,1},{1,0},{2,3},{3,2},{4,5},{5,4},{6,7},{7,6},{8,9},{9,8},{10,11... | collective-permute-start | bytes 1572872 | tf_op jit(solution)/shard_map/ppermute | solution.py:514
  229.2 21.8 %collective-permute-start.6 = (bf16[512,512]{1,0:T(8,128)(2,1)}, bf16[512,512]{1,0:T(8,128)(2,1)}, u32[]{:S(2)}, u32[]{:S(2)}) collective-permute-start(bf16[512,512]{1,0:T(8,128)(2,1)} %get-tuple-element.73), channel_id=1, source_target_pairs={{0,1},{1,0},{2,3},{3,2},{4,5},{5,4},{6,7},{7,6},{8,9},{9,8},{10,11... | collective-permute-start | bytes 1572872 | tf_op jit(solution)/shard_map/ppermute | solution.py:514
  321.7 39.8 %collective-permute-start.12 = (bf16[2,2,2,64,1024]{4,3,2,1,0:T(8,128)(2,1)}, bf16[2,2,2,64,1024]{4,3,2,1,0:T(8,128)(2,1)}, u32[]{:S(2)}, u32[]{:S(2)}) collective-permute-start(bf16[2,2,2,64,1024]{4,3,2,1,0:T(8,128)(2,1)} %dynamic-slice_bitcast_fusion.1), channel_id=1, source_target_pairs={{0,8},{1,9},{2,10},{3,11},{4,12},{5,13},{6,14},{7,15},{8,0},{9,1},... | collective-permute-start | bytes 3145736 | tf_op jit(solution)/shard_map/ppermute | solution.py:514
  322.8 41.6 %collective-permute-start.8 = (bf16[2,2,2,64,1024]{4,3,0,1,2:T(8,128)(2,1)}, bf16[2,2,2,64,1024]{4,3,0,1,2:T(8,128)(2,1)}, u32[]{:S(2)}, u32[]{:S(2)}) collective-permute-start(bf16[2,2,2,64,1024]{4,3,0,1,2:T(8,128)(2,1)} %bitcast.162), channel_id=1, source_target_pairs={{0,4},{1,5},{2,6},{3,7},{4,0},{5,1},{6,2},{7,3},{8,12},{9,13},{10,... | collective-permute-start | bytes 3145736 | tf_op jit(solution)/shard_map/ppermute | solution.py:514
  324.4 44.3 %collective-permute-start.21 = (bf16[2,2,2,128,512]{4,3,2,1,0:T(8,128)(2,1)}, bf16[2,2,2,128,512]{4,3,2,1,0:T(8,128)(2,1)}, u32[]{:S(2)}, u32[]{:S(2)}) collective-permute-start(bf16[2,2,2,128,512]{4,3,2,1,0:T(8,128)(2,1)} %dynamic-slice_bitcast_fusion), channel_id=1, source_target_pairs={{0,8},{1,9},{2,10},{3,11},{4,12},{5,13},{6,14},{7,15},{8,0},{9,1},... | collective-permute-start | bytes 3145736 | tf_op jit(solution)/shard_map/ppermute | solution.py:514
  325.2 67.7 %collective-permute-start.17 = (bf16[2,2,2,128,512]{4,3,0,1,2:T(8,128)(2,1)}, bf16[2,2,2,128,512]{4,3,0,1,2:T(8,128)(2,1)}, u32[]{:S(2)}, u32[]{:S(2)}) collective-permute-start(bf16[2,2,2,128,512]{4,3,0,1,2:T(8,128)(2,1)} %bitcast.161), channel_id=1, source_target_pairs={{0,2},{1,3},{2,0},{3,1},{4,6},{5,7},{6,4},{7,5},{8,10},{9,11},{10,... | collective-permute-start | bytes 3145736 | tf_op jit(solution)/shard_map/ppermute | solution.py:514
  341.1 93.8 %collective-permute-start.5 = (bf16[4,2,128,1024]{3,2,1,0:T(8,128)(2,1)}, bf16[4,2,128,1024]{3,2,1,0:T(8,128)(2,1)}, u32[]{:S(2)}, u32[]{:S(2)}) collective-permute-start(bf16[4,2,128,1024]{3,2,1,0:T(8,128)(2,1)} %get-tuple-element.49), channel_id=1, source_target_pairs={{0,1},{1,0},{2,3},{3,2},{4,5},{5,4},{6,7},{7,6},{8,9},{9,8},{10,11... | collective-permute-start | bytes 6291464 | tf_op jit(solution)/shard_map/ppermute | solution.py:514
  342.6 18.2 %copy-start.26 = (f32[1,2048]{1,0:T(1,128)S(1)}, f32[1,2048]{1,0:T(1,128)}, u32[]{:S(2)}) copy-start(f32[1,2048]{1,0:T(1,128)} %get-tuple-element.53) | copy-start | bytes 24580
  361.4 88.4 %collective-permute-start.4 = (bf16[4,2,128,1024]{3,2,1,0:T(8,128)(2,1)}, bf16[4,2,128,1024]{3,2,1,0:T(8,128)(2,1)}, u32[]{:S(2)}, u32[]{:S(2)}) collective-permute-start(bf16[4,2,128,1024]{3,2,1,0:T(8,128)(2,1)} %get-tuple-element.42), channel_id=1, source_target_pairs={{0,1},{1,0},{2,3},{3,2},{4,5},{5,4},{6,7},{7,6},{8,9},{9,8},{10,11... | collective-permute-start | bytes 6291464 | tf_op jit(solution)/shard_map/ppermute | solution.py:514
  364.4 39.8 %collective-permute-start.13 = (bf16[2,2,64,1024]{3,2,1,0:T(8,128)(2,1)}, bf16[2,2,64,1024]{3,2,1,0:T(8,128)(2,1)}, u32[]{:S(2)}, u32[]{:S(2)}) collective-permute-start(bf16[2,2,64,1024]{3,2,1,0:T(8,128)(2,1)} %dynamic-slice_bitcast_fusion.4), channel_id=1, source_target_pairs={{0,16},{1,17},{2,18},{3,19},{4,20},{5,21},{6,22},{7,23},{8,24},{9,... | collective-permute-start | bytes 1572872 | tf_op jit(solution)/shard_map/ppermute | solution.py:514
  366.3 29.3 %copy-start.5 = (bf16[2,2,2,64,1024]{4,3,0,1,2:T(8,128)(2,1)}, bf16[2,2,2,64,1024]{4,3,0,1,2:T(8,128)(2,1)S(1)}, u32[]{:S(2)}) copy-start(bf16[2,2,2,64,1024]{4,3,0,1,2:T(8,128)(2,1)S(1)} %fusion.11) | copy-start | bytes 3145732
  368.7 33.5 %collective-permute-start.9 = (bf16[2,2,64,1024]{3,2,0,1:T(8,128)(2,1)}, bf16[2,2,64,1024]{3,2,0,1:T(8,128)(2,1)}, u32[]{:S(2)}, u32[]{:S(2)}) collective-permute-start(bf16[2,2,64,1024]{3,2,0,1:T(8,128)(2,1)} %dynamic-slice_bitcast_fusion.5), channel_id=1, source_target_pairs={{0,2},{1,3},{2,0},{3,1},{4,6},{5,7},{6,4},{7,5},{8,10},{9,11},{10,... | collective-permute-start | bytes 1572872 | tf_op jit(solution)/shard_map/ppermute | solution.py:514
  392.9 23.6 %collective-permute-start.22 = (bf16[2,2,128,512]{3,2,1,0:T(8,128)(2,1)}, bf16[2,2,128,512]{3,2,1,0:T(8,128)(2,1)}, u32[]{:S(2)}, u32[]{:S(2)}) collective-permute-start(bf16[2,2,128,512]{3,2,1,0:T(8,128)(2,1)} %dynamic-slice_bitcast_fusion.2), channel_id=1, source_target_pairs={{0,16},{1,17},{2,18},{3,19},{4,20},{5,21},{6,22},{7,23},{8,24},{9,... | collective-permute-start | bytes 1572872 | tf_op jit(solution)/shard_map/ppermute | solution.py:514
  396.5 20.1 %copy-start.11 = (bf16[2,2,2,128,512]{4,3,2,1,0:T(8,128)(2,1)S(1)}, bf16[2,2,2,128,512]{4,3,2,1,0:T(8,128)(2,1)}, u32[]{:S(2)}) copy-start(bf16[2,2,2,128,512]{4,3,2,1,0:T(8,128)(2,1)} %copy-done.10) | copy-start | bytes 3145732
  402.2 15.6 %collective-permute-start.18 = (bf16[2,2,128,512]{3,2,0,1:T(8,128)(2,1)}, bf16[2,2,128,512]{3,2,0,1:T(8,128)(2,1)S(1)}, u32[]{:S(2)}, u32[]{:S(2)}) collective-permute-start(bf16[2,2,128,512]{3,2,0,1:T(8,128)(2,1)} %dynamic-slice_bitcast_fusion.3), channel_id=1, source_target_pairs={{0,4},{1,5},{2,6},{3,7},{4,0},{5,1},{6,2},{7,3},{8,12},{9,13},{10,... | collective-permute-start | bytes 1572872 | tf_op jit(solution)/shard_map/ppermute | solution.py:514
  404.1 20.1 %copy-start.12 = (bf16[2,2,64,1024]{3,2,0,1:T(8,128)(2,1)}, bf16[2,2,64,1024]{3,2,0,1:T(8,128)(2,1)S(1)}, u32[]{:S(2)}) copy-start(bf16[2,2,64,1024]{3,2,0,1:T(8,128)(2,1)S(1)} %fusion.15) | copy-start | bytes 1572868
  404.2 19.1 %collective-permute-start.7 = (f32[32,2048]{1,0:T(8,128)S(1)}, f32[32,2048]{1,0:T(8,128)S(1)}, u32[]{:S(2)}, u32[]{:S(2)}) collective-permute-start(f32[32,2048]{1,0:T(8,128)S(1)} %get-tuple-element.77), channel_id=1, source_target_pairs={{0,1},{1,0},{2,3},{3,2},{4,5},{5,4},{6,7},{7,6},{8,9},{9,8},{10,11... | collective-permute-start | bytes 786440 | tf_op jit(solution)/shard_map/ppermute | solution.py:514
  416.5 10.6 %collective-permute-start.14 = (bf16[2,64,1024]{2,1,0:T(8,128)(2,1)}, bf16[2,64,1024]{2,1,0:T(8,128)(2,1)}, u32[]{:S(2)}, u32[]{:S(2)}) collective-permute-start(bf16[2,64,1024]{2,1,0:T(8,128)(2,1)} %dynamic-slice_bitcast_fusion.9), channel_id=1, source_target_pairs={{0,2},{1,3},{2,0},{3,1},{4,6},{5,7},{6,4},{7,5},{8,10},{9,11},{10,... | collective-permute-start | bytes 786440 | tf_op jit(solution)/shard_map/ppermute | solution.py:514
  417.7 11.8 %collective-permute-start.10 = (bf16[2,64,1024]{2,1,0:T(8,128)(2,1)}, bf16[2,64,1024]{2,1,0:T(8,128)(2,1)}, u32[]{:S(2)}, u32[]{:S(2)}) collective-permute-start(bf16[2,64,1024]{2,1,0:T(8,128)(2,1)} %dynamic-slice_bitcast_fusion.10), channel_id=1, source_target_pairs={{0,8},{1,9},{2,10},{3,11},{4,12},{5,13},{6,14},{7,15},{8,0},{9,1},... | collective-permute-start | bytes 786440 | tf_op jit(solution)/shard_map/ppermute | solution.py:514
  423.2 7.4 %collective-permute-start.23 = (bf16[2,128,512]{2,1,0:T(8,128)(2,1)}, bf16[2,128,512]{2,1,0:T(8,128)(2,1)}, u32[]{:S(2)}, u32[]{:S(2)}) collective-permute-start(bf16[2,128,512]{2,1,0:T(8,128)(2,1)} %dynamic-slice_bitcast_fusion.6), channel_id=1, source_target_pairs={{0,4},{1,5},{2,6},{3,7},{4,0},{5,1},{6,2},{7,3},{8,12},{9,13},{10,... | collective-permute-start | bytes 786440 | tf_op jit(solution)/shard_map/ppermute | solution.py:514
  427.1 6.7 %collective-permute-start.19 = (bf16[2,128,512]{2,1,0:T(8,128)(2,1)}, bf16[2,128,512]{2,1,0:T(8,128)(2,1)S(1)}, u32[]{:S(2)}, u32[]{:S(2)}) collective-permute-start(bf16[2,128,512]{2,1,0:T(8,128)(2,1)} %dynamic-slice_bitcast_fusion.7), channel_id=1, source_target_pairs={{0,8},{1,9},{2,10},{3,11},{4,12},{5,13},{6,14},{7,15},{8,0},{9,1},... | collective-permute-start | bytes 786440 | tf_op jit(solution)/shard_map/ppermute | solution.py:514
  429.5 15.1 %collective-permute-start.15 = (bf16[64,1024]{1,0:T(8,128)(2,1)S(1)}, bf16[64,1024]{1,0:T(8,128)(2,1)S(1)}, u32[]{:S(2)}, u32[]{:S(2)}) collective-permute-start(bf16[64,1024]{1,0:T(8,128)(2,1)S(1)} %dynamic-slice_bitcast_fusion.17), channel_id=1, source_target_pairs={{0,4},{1,5},{2,6},{3,7},{4,0},{5,1},{6,2},{7,3},{8,12},{9,13},{10,... | collective-permute-start | bytes 393224 | tf_op jit(solution)/shard_map/ppermute | solution.py:514
  430.7 14.0 %collective-permute-start.11 = (bf16[64,1024]{1,0:T(8,128)(2,1)S(1)}, bf16[64,1024]{1,0:T(8,128)(2,1)S(1)}, u32[]{:S(2)}, u32[]{:S(2)}) collective-permute-start(bf16[64,1024]{1,0:T(8,128)(2,1)S(1)} %dynamic-slice_bitcast_fusion.18), channel_id=1, source_target_pairs={{0,16},{1,17},{2,18},{3,19},{4,20},{5,21},{6,22},{7,23},{8,24},{9,... | collective-permute-start | bytes 393224 | tf_op jit(solution)/shard_map/ppermute | solution.py:514
  433.9 15.9 %collective-permute-start.24 = (bf16[128,512]{1,0:T(8,128)(2,1)S(1)}, bf16[128,512]{1,0:T(8,128)(2,1)S(1)}, u32[]{:S(2)}, u32[]{:S(2)}) collective-permute-start(bf16[128,512]{1,0:T(8,128)(2,1)S(1)} %dynamic-slice_bitcast_fusion.15), channel_id=1, source_target_pairs={{0,2},{1,3},{2,0},{3,1},{4,6},{5,7},{6,4},{7,5},{8,10},{9,11},{10,... | collective-permute-start | bytes 393224 | tf_op jit(solution)/shard_map/ppermute | solution.py:514
  434.8 38.7 %collective-permute-start.20 = (bf16[128,512]{1,0:T(8,128)(2,1)S(1)}, bf16[128,512]{1,0:T(8,128)(2,1)S(1)}, u32[]{:S(2)}, u32[]{:S(2)}) collective-permute-start(bf16[128,512]{1,0:T(8,128)(2,1)S(1)} %dynamic-slice_bitcast_fusion.16), channel_id=1, source_target_pairs={{0,16},{1,17},{2,18},{3,19},{4,20},{5,21},{6,22},{7,23},{8,24},{9,... | collective-permute-start | bytes 393224 | tf_op jit(solution)/shard_map/ppermute | solution.py:514
  439.4 28.1 %all-to-all-start.4 = ((bf16[8,128,1024]{2,1,0:T(8,128)(2,1)}), bf16[8,128,1024]{2,1,0:T(8,128)(2,1)}, u32[]{:S(2)}, u32[]{:S(2)}) async-start(bf16[8,128,1024]{2,1,0:T(8,128)(2,1)} %bitcast.19), calls=%async_computation.4 | async-start | bytes 4194304 | tf_op jit(solution)/shard_map/all_to_all | solution.py:575
  444.9 29.9 %collective-permute-start.16 = (f32[32,2048]{1,0:T(8,128)S(1)}, f32[32,2048]{1,0:T(8,128)}, u32[]{:S(2)}, u32[]{:S(2)}) collective-permute-start(f32[32,2048]{1,0:T(8,128)S(1)} %get-tuple-element.75), channel_id=1, source_target_pairs={{0,1},{1,0},{2,3},{3,2},{4,5},{5,4},{6,7},{7,6},{8,9},{9,8},{10,11... | collective-permute-start | bytes 786440 | tf_op jit(solution)/shard_map/ppermute | solution.py:514
  454.8 21.2 %copy-start.1 = (bf16[8,128,1024]{2,1,0:T(8,128)(2,1)S(1)}, bf16[8,128,1024]{2,1,0:T(8,128)(2,1)}, u32[]{:S(2)}) copy-start(bf16[8,128,1024]{2,1,0:T(8,128)(2,1)} %param.14) | copy-start | bytes 6291460
  467.5 29.5 %all-to-all-start.3 = ((bf16[8,128,1024]{2,1,0:T(8,128)(2,1)}), bf16[8,128,1024]{2,1,0:T(8,128)(2,1)}, u32[]{:S(2)}, u32[]{:S(2)}) async-start(bf16[8,128,1024]{2,1,0:T(8,128)(2,1)} %bitcast.180), calls=%async_computation.3 | async-start | bytes 4194304 | tf_op jit(solution)/shard_map/all_to_all | solution.py:575
  497.0 12.1 %all-to-all-start.5 = ((f32[32,1,384]{2,1,0:T(1,128)}), f32[32,1,384]{2,1,0:T(1,128)S(1)}, u32[]{:S(2)}, u32[]{:S(2)}) async-start(f32[32,1,384]{2,1,0:T(1,128)} %copy.92), calls=%async_computation.5 | async-start | bytes 98304 | tf_op jit(solution)/shard_map/all_to_all | solution.py:707
  (24 other events, 148.5 us)
Sparse Core Ops, SparseCore 0:
  14.5 88.0 all-gather.3
  106.0 109.5 all-gather.5
  255.7 110.0 reduce-scatter.1
where the time goes:
time: 530 us; the launch traced here: 521 us
  Pallas kernels  177 us (33%)
  waiting for transfers between devices  80.3 us (15%)
  starting transfers between devices  77.7 us (15%)
  matrix products  54.2 us (10%)
  other arithmetic  47.8 us (9%)
  local copies, waits for them, and re-layouts  40 us (8%)
  blocking collectives  29.6 us (6%)
  between operations  15 us (3%)
    pallas_call x1, Pallas kernels, attention(): pl.pallas_call(functools.partial(attention_kernel, math.gcd(length, 256))...  72.1 us
    ppermute x25, starting transfers between devices, swap(): return lax.ppermute(value, AXES, [(i, i ^ mask) for i in range(n)])  49.7 us
    dot_general x4, matrix products, dot_tn(): lax.dot_general(left, right, (((0,), (0,)), ((), ())), preferred_element_...  38.4 us
    all_to_all x1, waiting for transfers between devices, to_chip(): mine = lax.all_to_all(value, 'pl', split_axis=0, concat_axis=0, tiled=True)  31.2 us
    all_to_all x1, blocking collectives, to_chip(): mine = lax.all_to_all(value, 'pl', split_axis=0, concat_axis=0, tiled=True)  29.6 us
    all_to_all x2, waiting for transfers between devices, to_tokens(): return lax.all_to_all(value, 'pl', split_axis=0, concat_axis=0, tiled=True)  24.7 us
    pallas_call x1, Pallas kernels, up_project(): pl.pallas_call(up_kernel, out_shape=(shape, shape), grid=(count // block,...  19.5 us
    pallas_call x1, Pallas kernels, out_project(): pl.pallas_call(out_kernel, out_shape=(jax.ShapeDtypeStruct(shape, F32), j...  16.8 us
  transfers between devices with their start and end apart: 33, of which 10 were waited for; matrix products, arithmetic and copies ran while one was open for 25% of the time, Pallas kernels for 34%

commit v1 on v0

--- a/solution.py
+++ b/solution.py
@@ -60,60 +60,74 @@
     dqkv_ref,
     q_s,
     k_s,
-    km_s,
-    vm_s,
-    ctx_s,
-    dq_s,
+    kt_s,
+    vt_s,
+    ctxt_s,
+    dqt_s,
     dk_s,
     dv_s,
 ):
     length = qkv_ref.shape[1]
     half = ROT // 2
     factor = 1.0 / math.sqrt(HD)
+    value_cols = slice(2 * PAIR, 3 * PAIR)
 
     def turn(z, sign):
         swapped = pltpu.roll(z, PAIR - half, 1) * sin_a_ref[...] + pltpu.roll(z, half, 1) * sin_b_ref[...]
         return z * cos_ref[...] + sign * swapped
 
     q_s[...] = turn(qkv_ref[0, :, 0:PAIR].astype(F32), 1.0).astype(BF) * BF(factor)
-    k_s[...] = turn(qkv_ref[0, :, PAIR : 2 * PAIR].astype(F32), 1.0).astype(BF)
-    ctx_s[...] = jnp.zeros_like(ctx_s)
-    dq_s[...] = jnp.zeros_like(dq_s)
+    keys = turn(qkv_ref[0, :, PAIR : 2 * PAIR].astype(F32), 1.0).astype(BF)
+    k_s[...] = keys
+    kt_s[...] = keys.T
+    vt_s[...] = qkv_ref[0, :, value_cols].T
     dk_s[...] = jnp.zeros_like(dk_s)
     dv_s[...] = jnp.zeros_like(dv_s)
     lane = lax.broadcasted_iota(jnp.int32, (1, PAIR), 1)
-
-    def one_head(head, carry):
-        chosen = ((lane >= head * HD) & (lane < head * HD + HD)).astype(BF)
-        km_s[...] = k_s[...] * chosen
-        vm_s[...] = qkv_ref[0, :, 2 * PAIR : 3 * PAIR] * chosen
-        for i in range(length // block):
-            lo, hi = i * block, (i + 1) * block
-            queries = q_s[lo:hi, :] * chosen
-            grads = dc_ref[0, lo:hi, :] * chosen
-            scores = dot_nt(km_s[0:hi, :], queries)
-            keys_at = lax.broadcasted_iota(jnp.int32, (block, block), 0)
-            queries_at = lax.broadcasted_iota(jnp.int32, (block, block), 1)
-            last = jnp.where(keys_at <= queries_at, scores[lo:hi, :], -1e30)
-            scores = jnp.concatenate([scores[:lo, :], last], 0) if i else last
-            highest = jnp.max(scores, axis=0, keepdims=True)
-            weights = jnp.exp(scores - highest)
-            weights = weights * (1.0 / jnp.sum(weights, axis=0, keepdims=True))
-            low = weights.astype(BF)
-            weight_grad = dot_nt(vm_s[0:hi, :], grads)
-            mixed = jnp.sum(weights * weight_grad, axis=0, keepdims=True)
-            score_grad = (weights * (weight_grad - mixed)).astype(BF)
-            ctx_s[lo:hi, :] += dot_tn(low, vm_s[0:hi, :])
-            dv_s[0:hi, :] += dot_nn(low, grads)
-            dk_s[0:hi, :] += dot_nn(score_grad, queries)
-            dq_s[lo:hi, :] += dot_tn(score_grad, km_s[0:hi, :])
-        return carry
-
-    lax.fori_loop(0, 2, one_head, 0)
-    ctx_ref[0] = ctx_s[...].astype(BF)
-    dqkv_ref[0, :, 0:PAIR] = turn(dq_s[...] * factor, -1.0).astype(BF)
+    keys_at = lax.broadcasted_iota(jnp.int32, (block, block), 0)
+    queries_at = lax.broadcasted_iota(jnp.int32, (block, block), 1)
+    chosen = [((lane >= h * HD) & (lane < h * HD + HD)).astype(BF) for h in range(2)]
+
+    def front(h, i):
+        lo, hi = i * block, (i + 1) * block
+        queries = q_s[lo:hi, :] * chosen[h]
+        grads = dc_ref[0, lo:hi, :] * chosen[h]
+        scores = dot_nt(k_s[0:hi, :], queries)
+        return scores, dot_nt(qkv_ref[0, 0:hi, value_cols], grads), queries, grads
+
+    def middle(i, scores, weight_grad, queries, grads):
+        lo, hi = i * block, (i + 1) * block
+        last = jnp.where(keys_at <= queries_at, scores[lo:hi, :], -1e30)
+        scores = jnp.concatenate([scores[:lo, :], last], 0) if i else last
+        weights = jnp.exp(scores - jnp.max(scores, axis=0, keepdims=True))
+        weights = weights * (1.0 / jnp.sum(weights, axis=0, keepdims=True))
+        mixed = jnp.sum(weights * weight_grad, axis=0, keepdims=True)
+        score_grad = (weights * (weight_grad - mixed)).astype(BF)
+        return weights.astype(BF), score_grad, queries, grads
+
+    def back(h, i, weights, score_grad, queries, grads):
+        lo, hi = i * block, (i + 1) * block
+        dims = slice(h * HD, h * HD + HD)
+        ctxt_s[dims, lo:hi] = dot_nn(vt_s[dims, 0:hi], weights)
+        dv_s[0:hi, :] += dot_nn(weights, grads)
+        dk_s[0:hi, :] += dot_nn(score_grad, queries)
+        dqt_s[dims, lo:hi] = dot_nn(kt_s[dims, 0:hi], score_grad)
+
+    order = [(h, i) for i in range(length // block) for h in range(2)]
+    ahead = front(*order[0])
+    behind = None
+    for step, (h, i) in enumerate(order):
+        following = front(*order[step + 1]) if step + 1 < len(order) else None
+        results = middle(i, *ahead)
+        if behind is not None:
+            back(*behind)
+        behind = (h, i, *results)
+        ahead = following
+    back(*behind)
+    ctx_ref[0] = ctxt_s[...].T.astype(BF)
+    dqkv_ref[0, :, 0:PAIR] = turn(dqt_s[...].T * factor, -1.0).astype(BF)
     dqkv_ref[0, :, PAIR : 2 * PAIR] = turn(dk_s[...], -1.0).astype(BF)
-    dqkv_ref[0, :, 2 * PAIR : 3 * PAIR] = dv_s[...].astype(BF)
+    dqkv_ref[0, :, value_cols] = dv_s[...].astype(BF)
 
 
 def attention(qkv, context_grad, tables):
@@ -131,7 +145,10 @@
         grid=(seqs, pairs),
         in_specs=[wide, slim, table, table, table],
         out_specs=(slim, wide),
-        scratch_shapes=[pltpu.VMEM((length, PAIR), BF)] * 4 + [pltpu.VMEM((length, PAIR), F32)] * 4,
+        scratch_shapes=[pltpu.VMEM((length, PAIR), BF)] * 2
+        + [pltpu.VMEM((PAIR, length), BF)] * 2
+        + [pltpu.VMEM((PAIR, length), F32)] * 2
+        + [pltpu.VMEM((length, PAIR), F32)] * 2,
         cost_estimate=pl.CostEstimate(
             flops=seqs * pairs * 2 * 7 * length * length * PAIR,
             bytes_accessed=seqs * length * width * 6,
@@ -141,63 +158,76 @@
     )(qkv, context_grad, *tables)
 
 
+def both_cores(core, rows, mine_ref, theirs_ref):
+    yield pl.ds(pl.multiple_of(core * rows, rows), rows), mine_ref[0]
+    yield pl.ds(pl.multiple_of((1 - core) * rows, rows), rows), theirs_ref[0]
+
+
 def norm_kernel(core_ref, mine_ref, theirs_ref, gains_ref, one_ref, two_ref, normed_ref):
-    own = pl.program_id(2) == core_ref[0]
-    x = jnp.where(own, mine_ref[0].astype(F32), theirs_ref[0].astype(F32))
-    centred = x - jnp.mean(x, axis=-1, keepdims=True)
-    normed = centred * lax.rsqrt(jnp.mean(centred * centred, axis=-1, keepdims=True) + epsilon)
-    one_ref[...] = (normed * gains_ref[0:1, :] + gains_ref[1:2, :]).astype(BF)
-    two_ref[...] = (normed * gains_ref[2:3, :] + gains_ref[3:4, :]).astype(BF)
-    normed_ref[...] = normed.astype(BF)
-
-
-def normalize(core, mine, theirs, gains, per_chip):
+    for at, value in both_cores(core_ref[0], mine_ref.shape[1], mine_ref, theirs_ref):
+        x = value.astype(F32)
+        centred = x - jnp.mean(x, axis=-1, keepdims=True)
+        normed = centred * lax.rsqrt(jnp.mean(centred * centred, axis=-1, keepdims=True) + epsilon)
+        one_ref[at, :] = (normed * gains_ref[0:1, :] + gains_ref[1:2, :]).astype(BF)
+        two_ref[at, :] = (normed * gains_ref[2:3, :] + gains_ref[3:4, :]).astype(BF)
+        normed_ref[at, :] = normed.astype(BF)
+
+
+def dy_kernel(core_ref, mine_ref, theirs_ref, dy_ref, sum_ref):
+    @pl.when((pl.program_id(0) == 0) & (pl.program_id(1) == 0))
+    def _():
+        sum_ref[...] = jnp.zeros_like(sum_ref)
+
+    sum_ref[...] += jnp.sum(mine_ref[0].astype(F32), 0, keepdims=True)
+    for at, value in both_cores(core_ref[0], mine_ref.shape[1], mine_ref, theirs_ref):
+        dy_ref[at, :] = value
+
+
+def on_pairs(kernel, outputs, core, mine, theirs, per_chip, extra=(), sums=0):
     blocks, rows, width = mine.shape
     planes = blocks // per_chip
-    source = pl.BlockSpec((1, rows, width), lambda s, p, c, core: (p * per_chip + s, 0, 0))
-    target = pl.BlockSpec((rows, width), lambda s, p, c, core: ((s * planes + p) * 2 + c, 0))
+    source = pl.BlockSpec((1, rows, width), lambda s, p, core: (p * per_chip + s, 0, 0))
+    target = pl.BlockSpec((2 * rows, width), lambda s, p, core: (s * planes + p, 0))
     shape = jax.ShapeDtypeStruct((2 * blocks * rows, width), BF)
+    whole = [pl.BlockSpec(value.shape, lambda s, p, core: (0, 0)) for value in extra]
     return pl.pallas_call(
-        norm_kernel,
-        out_shape=(shape, shape, shape),
+        kernel,
+        out_shape=(shape,) * outputs + (jax.ShapeDtypeStruct((1, width), F32),) * sums,
         grid_spec=pltpu.PrefetchScalarGridSpec(
             num_scalar_prefetch=1,
-            grid=(per_chip, planes, 2),
-            in_specs=[source, source, pl.BlockSpec((4, width), lambda s, p, c, core: (0, 0))],
-            out_specs=(target, target, target),
+            grid=(per_chip, planes),
+            in_specs=[source, source] + whole,
+            out_specs=(target,) * outputs
+            + (pl.BlockSpec((1, width), lambda s, p, core: (0, 0)),) * sums,
         ),
         cost_estimate=pl.CostEstimate(
             flops=20 * blocks * rows * width,
-            bytes_accessed=20 * blocks * rows * width,
+            bytes_accessed=(4 + 4 * outputs) * blocks * rows * width,
             transcendentals=0,
         ),
-    )(core.reshape(1), mine, theirs, gains)
-
-
-def dy_kernel(core_ref, mine_ref, theirs_ref, dy_ref):
-    own = pl.program_id(2) == core_ref[0]
-    dy_ref[...] = jnp.where(own, mine_ref[0].astype(F32), theirs_ref[0].astype(F32)).astype(BF)
-
-
-def arrange_cotangent(core, mine, theirs, per_chip):
-    blocks, rows, width = mine.shape
-    planes = blocks // per_chip
-    source = pl.BlockSpec((1, rows, width), lambda s, p, c, core: (p * per_chip + s, 0, 0))
-    target = pl.BlockSpec((rows, width), lambda s, p, c, core: ((s * planes + p) * 2 + c, 0))
-    count = 2 * blocks * rows
+    )(core.reshape(1), mine, theirs, *extra)
+
+
+def weave(first_core, own, other, chips):
+    rows, hidden = own.shape
+    block = hidden // chips
+
+    def kernel(first_ref, own_ref, other_ref, out_ref):
+        first = first_ref[0] == 1
+        for chip in range(chips):
+            here = slice(chip * block, (chip + 1) * block)
+            mine, theirs = own_ref[:, here], other_ref[:, here]
+            at = 2 * chip * block
+            out_ref[:, at : at + block] = jnp.where(first, mine, theirs)
+            out_ref[:, at + block : at + 2 * block] = jnp.where(first, theirs, mine)
+
+    whole = pl.BlockSpec(memory_space=pltpu.VMEM)
     return pl.pallas_call(
-        dy_kernel,
-        out_shape=jax.ShapeDtypeStruct((count, width), BF),
-        grid_spec=pltpu.PrefetchScalarGridSpec(
-            num_scalar_prefetch=1,
-            grid=(per_chip, planes, 2),
-            in_specs=[source, source],
-            out_specs=target,
-        ),
-        cost_estimate=pl.CostEstimate(
-            flops=count * width, bytes_accessed=6 * count * width, transcendentals=0
-        ),
-    )(core.reshape(1), mine, theirs)
+        kernel,
+        out_shape=jax.ShapeDtypeStruct((rows, 2 * hidden), own.dtype),
+        in_specs=[pl.BlockSpec(memory_space=pltpu.SMEM), whole, whole],
+        out_specs=whole,
+    )(first_core.astype(jnp.int32).reshape(1), own, other)
 
 
 def phi(u):
@@ -205,21 +235,26 @@
     return 0.5 * (1.0 + lax.erf(u * math.sqrt(0.5))), density
 
 
-def up_kernel(a_ref, low_ref, high_ref, bias_ref, z_ref, slope_ref):
-    width = low_ref.shape[2]
-    chunk = math.gcd(width, 512)
-    a = a_ref[...]
-    for half, w_ref in enumerate((low_ref, high_ref)):
-        for start in range(0, width, chunk):
-            weight = w_ref[:, :, start : start + chunk].reshape(a.shape[1], chunk)
-            at = half * width + start
-            u = dot_nn(a, weight) + bias_ref[:, at : at + chunk]
-            cdf, density = phi(u)
-            z_ref[:, at : at + chunk] = (u * cdf).astype(BF)
-            slope_ref[:, at : at + chunk] = (cdf + u * density).astype(BF)
-
-
-def half_specs(shared):
+def pipelined(chunks, first, second):
+    ahead = first(chunks[0])
+    for n, chunk in enumerate(chunks):
+        following = first(chunks[n + 1]) if n + 1 < len(chunks) else None
+        second(chunk, ahead)
+        ahead = following
+
+
+def starts(width, chunk=512):
+    chunk = math.gcd(width, chunk)
+    return [slice(at, at + chunk) for at in range(0, width, chunk)]
+
+
+def stacked(ref, rows, cols):
+    size = ref.shape[1]
+    part = ref[rows.start // size : rows.stop // size, :, cols]
+    return part.reshape(part.shape[0] * size, part.shape[2])
+
+
+def shared_specs(shared):
     chips, rows, width = shared.shape
     low = pl.BlockSpec((chips, rows // 4, width), lambda *i: (0, 0, 0))
     high = pl.BlockSpec((chips, rows // 4, width), lambda *i: (0, 1, 0))
@@ -227,10 +262,33 @@
     return low, high, down
 
 
+def up_kernel(a_ref, low_ref, high_ref, bias_ref, z_ref, slope_ref):
+    width = low_ref.shape[2]
+    everything = slice(0, a_ref.shape[1])
+    a = a_ref[...]
+    chunks = [
+        (w_ref, here, slice(half * width + here.start, half * width + here.stop))
+        for half, w_ref in enumerate((low_ref, high_ref))
+        for here in starts(width, 256)
+    ]
+
+    def product(chunk):
+        w_ref, here, there = chunk
+        return dot_nn(a, stacked(w_ref, everything, here)) + bias_ref[:, there]
+
+    def activate(chunk, u):
+        there = chunk[2]
+        cdf, density = phi(u)
+        z_ref[:, there] = (u * cdf).astype(BF)
+        slope_ref[:, there] = (cdf + u * density).astype(BF)
+
+    pipelined(chunks, product, activate)
+
+
 def up_project(a, shared, bias, block):
     count, width = a.shape
     hidden = bias.shape[1]
-    low, high, _ = half_specs(shared)
+    low, high, _ = shared_specs(shared)
     wide = pl.BlockSpec((block, hidden), lambda i: (i, 0))
     shape = jax.ShapeDtypeStruct((count, hidden), BF)
     return pl.pallas_call(
@@ -254,28 +312,27 @@
 
 
 def dz_kernel(dy_ref, down_ref, slope_ref, du_ref, sum_ref):
-    hidden = du_ref.shape[1]
-    chunk = math.gcd(hidden, 512)
-    width = dy_ref.shape[1]
     dy = dy_ref[...]
-    _, rows, _ = down_ref.shape
+    everything = slice(0, dy.shape[1])
 
     @pl.when(pl.program_id(0) == 0)
     def _():
         sum_ref[...] = jnp.zeros_like(sum_ref)
 
-    for start in range(0, hidden, chunk):
-        part = down_ref[start // rows : (start + chunk) // rows, :, :].reshape(chunk, width)
-        slope = slope_ref[:, start : start + chunk].astype(F32)
-        du = (dot_nt(dy, part) * slope).astype(BF)
-        du_ref[:, start : start + chunk] = du
-        sum_ref[:, start : start + chunk] += jnp.sum(du.astype(F32), 0, keepdims=True)
+    def product(here):
+        return dot_nt(dy, stacked(down_ref, here, everything))
+
+    def scale(here, dz):
+        du = (dz * slope_ref[:, here].astype(F32)).astype(BF)
+        du_ref[:, here] = du
+        sum_ref[:, here] += jnp.sum(du.astype(F32), 0, keepdims=True)
+
+    pipelined(starts(du_ref.shape[1]), product, scale)
 
 
 def down_pull(dy, shared, slope, block):
     count, width = dy.shape
     hidden = slope.shape[1]
-    down = half_specs(shared)[2]
     wide = pl.BlockSpec((block, hidden), lambda i: (i, 0))
     return pl.pallas_call(
         dz_kernel,
@@ -284,7 +341,11 @@
             jax.ShapeDtypeStruct((1, hidden), F32),
         ),
         grid=(count // block,),
-        in_specs=[pl.BlockSpec((block, width), lambda i: (i, 0)), down, wide],
+        in_specs=[
+            pl.BlockSpec((block, width), lambda i: (i, 0)),
+            shared_specs(shared)[2],
+            wide,
+        ],
         out_specs=(wide, pl.BlockSpec((1, hidden), lambda i: (0, 0))),
         cost_estimate=pl.CostEstimate(
             flops=2 * count * width * hidden,
@@ -302,15 +363,17 @@
         bias_ref[...] = jnp.zeros_like(bias_ref)
 
     d = d_ref[...]
-    bias_ref[...] += jnp.sum(d.astype(F32), 0, keepdims=True)
-    width = h_ref.shape[1]
-    chunk = math.gcd(width, 512)
-    for start in range(0, width, chunk):
-        here = slice(start, start + chunk)
-        g = dot_nt(d, w_ref[here, :])
+
+    def product(here):
+        return dot_nt(d, w_ref[here, :])
+
+    def scale(here, g):
         h_ref[:, here] = (g * gain_ref[:, here]).astype(BF)
         sums_ref[0:1, here] += jnp.sum(g * normed_ref[:, here].astype(F32), 0, keepdims=True)
         sums_ref[1:2, here] += jnp.sum(g, 0, keepdims=True)
+
+    pipelined(starts(h_ref.shape[1]), product, scale)
+    bias_ref[...] += jnp.sum(d.astype(F32), 0, keepdims=True)
 
 
 def pull_one(d, weights, normed, gain, block):
@@ -355,23 +418,37 @@
 
 
 def g_two_kernel(
-    core_ref, d_ref, low_ref, high_ref, normed_ref, gain_ref, h_ref, kept_ref, sent_ref, sums_ref, value_s
+    core_ref,
+    d_ref,
+    low_ref,
+    high_ref,
+    normed_ref,
+    gain_ref,
+    h_ref,
+    kept_ref,
+    sent_ref,
+    sums_ref,
+    value_s,
 ):
     @pl.when((pl.program_id(0) == 0) & (pl.program_id(1) == 0))
     def _():
         sums_ref[...] = jnp.zeros_like(sums_ref)
 
-    _, rows, width = low_ref.shape
-    chunk = value_s.shape[1]
-    for start in range(0, width, chunk):
-        here = slice(start, start + chunk)
-        part = slice(start // rows, (start + chunk) // rows)
-        g = dot_nt(d_ref[:, :width], low_ref[part, :, :].reshape(chunk, width))
-        g += dot_nt(d_ref[:, width:], high_ref[part, :, :].reshape(chunk, width))
+    width = low_ref.shape[2]
+    everything = slice(0, width)
+
+    def product(here):
+        return dot_nt(d_ref[:, :width], stacked(low_ref, here, everything)) + dot_nt(
+            d_ref[:, width:], stacked(high_ref, here, everything)
+        )
+
+    def scale(here, g):
         value_s[...] = g * gain_ref[:, here] + h_ref[:, here].astype(F32)
         sums_ref[0:1, here] += jnp.sum(g * normed_ref[:, here].astype(F32), 0, keepdims=True)
         sums_ref[1:2, here] += jnp.sum(g, 0, keepdims=True)
         split_rows(core_ref[0], value_s, kept_ref, sent_ref, here, None)
+
+    pipelined(starts(width), product, scale)
 
 
 def token_specs(planes, per_chip, rows, width, group):
@@ -389,7 +466,7 @@
     width = gain.shape[1]
     group = math.gcd(planes, 2)
     grid, piece, block = token_specs(planes, per_chip, rows, width, group)
-    low, high, _ = half_specs(shared)
+    low, high, _ = shared_specs(shared)
     shape = (planes, per_chip, rows, width)
     return pl.pallas_call(
         g_two_kernel,
@@ -424,13 +501,12 @@
 def out_kernel(
     core_ref, z_ref, down_ref, ctx_ref, out_ref, x_ref, bias_ref, kept_ref, sent_ref, value_s
 ):
-    chips, rows, width = down_ref.shape
-    chunk = value_s.shape[1]
-    for start in range(0, width, chunk):
-        here = slice(start, start + chunk)
-        value_s[...] = dot_nn(z_ref[...], down_ref[:, :, here].reshape(chips * rows, chunk)) + dot_nn(
-            ctx_ref[...], out_ref[:, here]
-        )
+    def product(here):
+        down = stacked(down_ref, slice(0, z_ref.shape[1]), here)
+        return dot_nn(z_ref[...], down) + dot_nn(ctx_ref[...], out_ref[:, here])
+
+    def split(here, value):
+        value_s[...] = value
         split_rows(
             core_ref[0],
             value_s,
@@ -440,13 +516,14 @@
             lambda p: x_ref[p, 0, :, here].astype(F32) + bias_ref[:, here],
         )
 
+    pipelined(starts(out_ref.shape[1]), product, split)
+
 
 def out_project(core, z, shared, context, w_out, x_mine, bias, planes, per_chip, rows):
     count, hidden = z.shape
     inner, width = w_out.shape
     group = math.gcd(planes, 2)
     grid, piece, block = token_specs(planes, per_chip, rows, width, group)
-    down = half_specs(shared)[2]
     shape = (planes, per_chip, rows, width)
     return pl.pallas_call(
         out_kernel,
@@ -456,7 +533,7 @@
             grid=grid,
             in_specs=[
                 block(hidden),
-                down,
+                shared_specs(shared)[2],
                 block(inner),
                 pl.BlockSpec((inner, width), lambda s, p, core: (0, 0)),
                 piece,
@@ -497,7 +574,6 @@
     planes = lax.axis_size("pl")
     chips = lax.axis_size("dp") * planes
     n = 2 * chips
-    flat = (lax.axis_index("dp") * planes + lax.axis_index("pl")) * 2 + lax.axis_index("core")
     core = lax.axis_index("core")
     first_core = core == 0
     seqs, rows_here, width = tokens.shape
@@ -551,6 +627,7 @@
     b_qkv = pick(b_qkv, core, 0).transpose(0, 2, 1, 3).reshape(qkv_cols)
     b_in = pick(small[:, 9 * part :].reshape(chips, 2, hidden // chips), core, 1).reshape(hidden)
 
+    deep = chips // planes
     second = jnp.concatenate(
         [
             chip_rows[:, first_cols : first_cols + width],
@@ -577,8 +654,10 @@
     x_mine, x_theirs = to_chip(ordered(tokens, chip_rows))
     dy_mine, dy_theirs = to_chip(ordered(cotangent, x_mine))
     gains = jnp.stack([gain_one, shift_one, gain_two, shift_two])
-    dy = arrange_cotangent(core, dy_mine, dy_theirs, per_chip)
-    a_one, a_two, normed = normalize(core, x_mine, x_theirs, gains, per_chip)
+    dy, dy_sum = on_pairs(dy_kernel, 1, core, dy_mine, dy_theirs, per_chip, sums=1)
+    a_one, a_two, normed = on_pairs(
+        norm_kernel, 3, core, x_mine, x_theirs, per_chip, (gains,)
+    )
 
     qkv = (dot_nn(a_one, w_qkv) + b_qkv).astype(BF)
     context_grad = dot_nt(dy, w_out).astype(BF)
@@ -590,48 +669,28 @@
     context = context.reshape(count, ctx_cols)
     qkv_grad = qkv_grad.reshape(count, qkv_cols)
 
-    chip_bits = chips.bit_length() - 1
-    plane_bits = planes.bit_length() - 1
-
-    def scatter_sum(value, order):
-        cols = value.shape[1]
-        value = value.reshape((2,) * chip_bits + (value.shape[0] // chips, cols))
-        left = list(range(chip_bits, 0, -1))
-        for step, bit in enumerate(order):
-            axis = left.index(bit)
-            left.remove(bit)
-            mine = (flat >> bit) & 1
-            sent = swap(pick(value, 1 - mine, axis).astype(BF), 1 << bit)
-            value = pick(value, mine, axis).astype(F32) + sent.astype(F32)
-            if step < len(order) - 1:
-                value = value.astype(BF)
-        return value
-
-    plane_up = list(range(1, plane_bits + 1))
-    plane_down = plane_up[::-1]
-    beyond = list(range(plane_bits + 1, chip_bits + 1))
-    orders = {
-        "sda": plane_up + beyond,
-        "sdb": beyond + plane_down,
-        "sia": plane_down + beyond,
-        "sib": beyond + plane_up,
-    }
-
-    def scatter_two_ways(value, tag):
-        cols = value.shape[1] // 2
-        return jnp.concatenate(
-            [
-                scatter_sum(value[:, :cols], orders[tag + "a"]),
-                scatter_sum(value[:, cols:], orders[tag + "b"]),
-            ],
-            1,
-        )
+    plane_here = lax.axis_index("pl")
+    deep_here = lax.axis_index("dp")
+
+    def direct_sum(value, axis, size, here, stride, final):
+        total = pick(value, here, axis).astype(F32)
+        for k in range(1, size):
+            total += swap(pick(value, here ^ k, axis), k * stride).astype(F32)
+        return total if final else total.astype(BF)
+
+    def plane_then_deep(value):
+        value = value.reshape(deep, planes, value.shape[0] // chips, value.shape[1])
+        value = direct_sum(value, 1, planes, plane_here, 2, False)
+        return direct_sum(value, 0, deep, deep_here, 2 * planes, True)
+
+    def deep_then_plane(value):
+        value = value.reshape(deep, planes, value.shape[0] // chips, value.shape[1])
+        value = direct_sum(value, 0, deep, deep_here, 2 * planes, False)
+        return direct_sum(value, 0, planes, plane_here, 2, True)
 
     def own_rows_of(value):
         value = value.reshape(2, own_rows, value.shape[1])
-        return in_core_order(
-            pick(value, core, 0)[:, None], swap(pick(value, 1 - core, 0), 1)[:, None], 1
-        )
+        return pick(value, core, 0), swap(pick(value, 1 - core, 0), 1)
 
     out_w_grad = dot_tn(context, dy).astype(BF)
     other_cols = lax.dynamic_slice_in_dim(out_w_grad, (1 - core) * ctx_cols, ctx_cols, 1)
@@ -639,8 +698,12 @@
     out_w_grad = in_core_order(own_cols, swap(other_cols, 1), 0)
     qkv_w_grad = dot_tn(a_one, qkv_grad).astype(BF)
     first_grad = jnp.concatenate([qkv_w_grad, out_w_grad], 1)
-    first_grad = lax.psum_scatter(first_grad, CHIPS, scatter_dimension=0, tiled=True)
-    first_grad = own_rows_of(first_grad.astype(F32))
+    first_grad = first_grad.reshape(deep, planes, 2 * own_rows, first_cols).transpose(1, 0, 2, 3)
+    first_grad = lax.all_to_all(first_grad, "pl", split_axis=0, concat_axis=0, tiled=True)
+    first_grad = jnp.sum(first_grad.astype(F32), 0).astype(BF)
+    first_grad = direct_sum(first_grad, 0, deep, deep_here, 2 * planes, True)
+    first_own, first_other = own_rows_of(first_grad)
+    first_grad = in_core_order(first_own[:, None], first_other[:, None], 1)
     qkv_w_grad = (
         first_grad[:, :, :qkv_cols]
         .reshape(own_rows, 2, heads // 2, 3, 2, HD)
@@ -653,15 +716,18 @@
 
     z, slope = up_project(a_two, shared, b_in[None], block)
     down_w_grad = dot_tn(z, dy).astype(BF)
-    down_w_grad = scatter_two_ways(down_w_grad, "sd")
+    down_w_grad = plane_then_deep(down_w_grad)
     du, in_b_grad = down_pull(dy, shared, slope, block)
     in_w_grad = dot_tn(a_two, du).astype(BF)
-    in_w_grad = own_rows_of(scatter_two_ways(in_w_grad, "si"))
-    in_w_grad = (
-        in_w_grad.reshape(own_rows, 2, chips, hidden // chips)
-        .transpose(0, 2, 1, 3)
-        .reshape(own_rows, 2 * hidden)
-    )
+    in_w_grad = jnp.concatenate(
+        [
+            plane_then_deep(in_w_grad[:, : hidden // 2]),
+            deep_then_plane(in_w_grad[:, hidden // 2 :]),
+        ],
+        1,
+    )
+    in_w_own, in_w_other = own_rows_of(in_w_grad)
+    in_w_grad = weave(first_core, in_w_own, in_w_other, chips)
     kept, sent, sums_two = pull_two(
         core, du, shared, normed, gain_two[None], h_one, planes, per_chip, rows_here
     )
@@ -699,7 +765,7 @@
         sums_one[1],
         sums_two[0],
         sums_two[1],
-        jnp.sum(dy_here, (0, 1)),
+        dy_sum,
         qkv_b_grad,
         in_b_grad,
     ]

time: 530 us -> 554 us (1.045)
  the two profiles are of different devices: /device:TPU:13 before, /device:TPU:0 now
where the time goes in v1:
time: 554 us; the launch traced here: 545 us
  waiting for transfers between devices  167 us (30%)
  Pallas kernels  140 us (25%)
  starting transfers between devices  55.8 us (10%)
  matrix products  52.1 us (9%)
  other arithmetic  42.5 us (8%)
  local copies, waits for them, and re-layouts  40 us (7%)
  blocking collectives  32.7 us (6%)
  between operations  15 us (3%)
    ppermute x30, waiting for transfers between devices, swap(): return lax.ppermute(value, AXES, [(i, i ^ mask) for i in range(n)])  78.7 us
    all_to_all x1, waiting for transfers between devices, local(): lax.all_to_all(first_grad, 'pl', split_axis=0, concat_axis=0, tiled=True)  47.1 us
    pallas_call x1, Pallas kernels, attention(): pl.pallas_call(functools.partial(attention_kernel, math.gcd(length, 256))...  43.8 us
    dot_general x4, matrix products, dot_tn(): lax.dot_general(left, right, (((0,), (0,)), ((), ())), preferred_element_...  36.7 us
    all_to_all x1, waiting for transfers between devices, to_chip(): mine = lax.all_to_all(value, 'pl', split_axis=0, concat_axis=0, tiled=True)  34.2 us
    all_to_all x1, blocking collectives, to_chip(): mine = lax.all_to_all(value, 'pl', split_axis=0, concat_axis=0, tiled=True)  32.7 us
    ppermute x30, starting transfers between devices, swap(): return lax.ppermute(value, AXES, [(i, i ^ mask) for i in range(n)])  28.2 us
    pallas_call x1, Pallas kernels, up_project(): pl.pallas_call(up_kernel, out_shape=(shape, shape), grid=(count // block,...  19.5 us
  transfers between devices with their start and end apart: 38, of which 17 were waited for; matrix products, arithmetic and copies ran while one was open for 17% of the time, Pallas kernels for 19%

profile of v1, /device:TPU:0, one launch (start us, length us, event | category | flops | bytes accessed | tf_op | source)
XLA Modules:
  0.0 545.1 jit_solution(1509904114806720625)
XLA Ops:
  14.2 32.7 %all_to_all.43.mine_ref = bf16[8,128,1024]{2,1,0:T(8,128)(2,1)} all-to-all(bf16[8,128,1024]{2,1,0:T(8,128)(2,1)S(1)} %copy-done), channel_id=1, replica_groups=mesh['dp'=4,'pl'=4,'core'=2] {'pl'}, dimensions={0} | all-to-all | bytes 4194304 | tf_op jit(solution)/shard_map/all_to_all | solution.py:646
  47.0 4.6 all-to-all-start.2
  52.6 34.2 %all-to-all-done.2.mine_ref = bf16[8,128,1024]{2,1,0:T(8,128)(2,1)} async-done(((bf16[8,128,1024]{2,1,0:T(8,128)(2,1)}), bf16[8,128,1024]{2,1,0:T(8,128)(2,1)}, u32[]{:S(2)}, u32[]{:S(2)}) %all-to-all-start.2) | async-done | bytes 2097184 | tf_op jit(solution)/shard_map/all_to_all | solution.py:646
  88.9 4.7 all-to-all-start.1
  93.6 3.0 fusion.23
  96.5 4.5 all-to-all-done.1
  102.5 9.7 %shard_map.245 = (bf16[2048,1024]{1,0:T(8,128)(2,1)}, bf16[2048,1024]{1,0:T(8,128)(2,1)}, bf16[2048,1024]{1,0:T(8,128)(2,1)}) custom-call(s32[1]{0:T(128)} %bitcast.core_ref, bf16[8,128,1024]{2,1,0:T(8,128)(2,1)} %all_to_all.43.mine_ref, bf16[8,128,1024]{2,1,0:T(8,128)(2,1)} %collective-permute-done.1.theirs_ref, f32[4,1024]{1,0:T(4,128)} %pad_maximum_fusion.4.gains_ref), custom_call_target="tpu_custom_call" | custom-call | flops 20971520 | bytes 16777216 | tf_op jit(solution)/shard_map/pallas_call | solution.py:193
  112.2 6.7 %shard_map.247 = (bf16[2048,1024]{1,0:T(8,128)(2,1)}, f32[1,1024]{1,0:T(1,128)}) custom-call(s32[1]{0:T(128)} %bitcast.core_ref, bf16[8,128,1024]{2,1,0:T(8,128)(2,1)} %all-to-all-done.2.mine_ref, bf16[8,128,1024]{2,1,0:T(8,128)(2,1)} %collective-permute-done.2.theirs_ref), custom_call_target="tpu_custom_call" | custom-call | flops 20971520 | bytes 8388608 | tf_op jit(solution)/shard_map/pallas_call | solution.py:193
  120.4 11.6 %add_convert_fusion = bf16[2048,1536]{1,0:T(8,128)(2,1)} fusion(bf16[2048,1024]{1,0:T(8,128)(2,1)} %get-tuple-element.40, f32[1536]{0:T(1024)S(1)} %add.226, bf16[1024,2048]{1,0:T(8,128)(2,1)} %all-gather.4.cloned.1.call-done.w_ref), kind=kOutput, calls=%fused_computation | convolution fusion | flops 6448742400 | bytes 13637632 | tf_op jit(solution)/shard_map/dot_general | solution.py:26
  132.3 3.8 convolution_convert_fusion.3
  136.1 43.8 %shard_map.248 = (bf16[2,1024,512]{2,1,0:T(8,128)(2,1)}, bf16[2,1024,1536]{2,1,0:T(8,128)(2,1)}) custom-call(bf16[2,1024,1536]{2,1,0:T(8,128)(2,1)} %bitcast.186, bf16[2,1024,512]{2,1,0:T(8,128)(2,1)} %bitcast.189, f32[1024,128]{1,0:T(8,128)} %get-tuple-element.111.cos_ref, f32[1024,128]{1,0:T(8,128)} %get-tuple-element.110.sin_a_ref, ...), custom_call_target="tpu_custom_call" | custom-call | flops 15032385536 | bytes 18874368 | tf_op jit(solution)/shard_map/pallas_call | solution.py:139
  179.8 5.3 convolution_convert_fusion.4
  185.8 7.1 %convolution_convert_fusion = bf16[1024,1536]{1,0:T(8,128)(2,1)S(1)} fusion(bf16[2048,1024]{1,0:T(8,128)(2,1)S(1)} %copy-done.27, bf16[2048,1536]{1,0:T(8,128)(2,1)S(1)} %bitcast.185), kind=kOutput, calls=%fused_computation.18 | convolution fusion | flops 6444023808 | bytes 13631488 | tf_op jit(solution)/shard_map/dot_general | solution.py:34
  194.0 2.3 copy.102
  196.4 5.1 all-to-all-start.6
  202.5 47.1 %all-to-all-done.6 = bf16[4,4,64,2048]{3,2,1,0:T(8,128)(2,1)} async-done(((bf16[4,4,64,2048]{3,2,1,0:T(8,128)(2,1)}), bf16[4,4,64,2048]{3,2,1,0:T(8,128)(2,1)}, u32[]{:S(2)}, u32[]{:S(2)}) %all-to-all-start.6) | async-done | bytes 4194336 | tf_op jit(solution)/shard_map/all_to_all | solution.py:702
  249.6 3.1 reduce_sum.62
  259.7 6.7 %collective-permute-done.7 = bf16[64,2048]{1,0:T(8,128)(2,1)} collective-permute-done((bf16[64,2048]{1,0:T(8,128)(2,1)}, bf16[64,2048]{1,0:T(8,128)(2,1)}, u32[]{:S(2)}, u32[]{:S(2)}) %collective-permute-start.7) | collective-permute-done | bytes 262176 | tf_op jit(solution)/shard_map/ppermute | solution.py:590
  266.3 2.3 collective-permute-done.9
  268.6 11.0 %collective-permute-done.8 = bf16[64,2048]{1,0:T(8,128)(2,1)} collective-permute-done((bf16[64,2048]{1,0:T(8,128)(2,1)S(1)}, bf16[64,2048]{1,0:T(8,128)(2,1)}, u32[]{:S(2)}, u32[]{:S(2)}) %collective-permute-start.8) | collective-permute-done | bytes 262176 | tf_op jit(solution)/shard_map/ppermute | solution.py:590
  281.0 11.6 %shard_map.251 = (bf16[2048,1024]{1,0:T(8,128)(2,1)}, f32[2,1024]{1,0:T(2,128)}, f32[1,1536]{1,0:T(1,128)}) custom-call(bf16[2048,1536]{1,0:T(8,128)(2,1)} %bitcast.184, bf16[1024,2048]{1,0:T(8,128)(2,1)} %all-gather.4.cloned.1.call-done.w_ref, bf16[2048,1024]{1,0:T(8,128)(2,1)} %get-tuple-element.48.normed_ref, f32[1,1024]{1,0:T(1,128)} %copy-done.13), custom_call_target="tpu_custom_call" | custom-call | flops 6442450944 | bytes 14680064 | tf_op jit(solution)/shard_map/pallas_call | solution.py:382
  295.3 19.5 %shard_map.246 = (bf16[2048,2048]{1,0:T(8,128)(2,1)}, bf16[2048,2048]{1,0:T(8,128)(2,1)}) custom-call(bf16[2048,1024]{1,0:T(8,128)(2,1)} %get-tuple-element.38.a_ref, bf16[16,256,1024]{2,1,0:T(8,128)(2,1)} %bitcast.149, bf16[16,256,1024]{2,1,0:T(8,128)(2,1)} %bitcast.150, f32[1,2048]{1,0:T(1,128)} %fusion.28.bias_ref), custom_call_target="tpu_custom_call" | custom-call | flops 8589934592 | bytes 25165824 | tf_op jit(solution)/shard_map/pallas_call | solution.py:294
  314.8 15.0 %shard_map.250 = (bf16[2048,2048]{1,0:T(8,128)(2,1)}, f32[1,2048]{1,0:T(1,128)}) custom-call(bf16[2048,1024]{1,0:T(8,128)(2,1)} %get-tuple-element.42.dy_ref, bf16[16,256,1024]{2,1,0:T(8,128)(2,1)} %bitcast.151, bf16[2048,2048]{1,0:T(8,128)(2,1)} %get-tuple-element.46.slope_ref), custom_call_target="tpu_custom_call" | custom-call | flops 8589934592 | bytes 25165824 | tf_op jit(solution)/shard_map/pallas_call | solution.py:337
  329.8 14.6 %convolution_convert_fusion.2 = bf16[2048,1024]{1,0:T(8,128)(2,1)} fusion(bf16[2048,2048]{1,0:T(8,128)(2,1)} %get-tuple-element.39.z_ref, bf16[2048,1024]{1,0:T(8,128)(2,1)} %get-tuple-element.42.dy_ref), kind=kOutput, calls=%fused_computation.20 | convolution fusion | flops 8592031744 | bytes 16777216 | tf_op jit(solution)/shard_map/dot_general | solution.py:34
  344.4 9.6 %convolution_convert_fusion.1 = bf16[1024,2048]{1,0:T(8,128)(2,1)S(1)} fusion(bf16[2048,1024]{1,0:T(8,128)(2,1)S(1)} %copy-done.25, bf16[2048,2048]{1,0:T(8,128)(2,1)S(1)} %copy-done.1), kind=kOutput, calls=%fused_computation.19 | convolution fusion | flops 8592031744 | bytes 16777216 | tf_op jit(solution)/shard_map/dot_general | solution.py:34
  359.3 15.7 %shard_map.252 = (f32[4,2,128,1024]{3,2,1,0:T(8,128)}, bf16[4,2,128,1024]{3,2,1,0:T(8,128)(2,1)}, f32[2,1024]{1,0:T(2,128)}) custom-call(s32[1]{0:T(128)} %bitcast.core_ref, bf16[2048,2048]{1,0:T(8,128)(2,1)} %get-tuple-element.47.d_ref, bf16[16,256,1024]{2,1,0:T(8,128)(2,1)} %bitcast.152, bf16[16,256,1024]{2,1,0:T(8,128)(2,1)} %bitcast.153, ...), custom_call_target="tpu_custom_call" | custom-call | flops 8589934592 | bytes 25165824 | tf_op jit(solution)/shard_map/pallas_call | solution.py:471
  376.7 4.1 all-to-all-start.5
  380.8 2.9 collective-permute-start.18
  383.7 2.5 dynamic-slice_bitcast_fusion.8
  389.6 16.8 %shard_map.249 = (f32[4,2,128,1024]{3,2,1,0:T(8,128)}, bf16[4,2,128,1024]{3,2,1,0:T(8,128)(2,1)}) custom-call(s32[1]{0:T(128)} %bitcast.core_ref, bf16[2048,2048]{1,0:T(8,128)(2,1)} %get-tuple-element.39.z_ref, bf16[16,256,1024]{2,1,0:T(8,128)(2,1)} %bitcast.154, bf16[2048,512]{1,0:T(8,128)(2,1)} %bitcast.188, bf16[512,1024]{1,0:T(8,128)(2,1)} %copy-done.7, ...), custom_call_target="tpu_custom_call" | custom-call | flops 10737418240 | bytes 27262976 | tf_op jit(solution)/shard_map/pallas_call | solution.py:528
  406.4 2.1 collective-permute-done.18
  408.5 1.9 fusion.14
  416.8 1.9 fusion.17
  427.7 3.8 add_convert_fusion.1
  435.1 4.4 all-to-all-start.4
  443.6 5.4 collective-permute-done.24
  449.0 22.5 %collective-permute-done.26 = bf16[4,128,1024]{2,1,0:T(8,128)(2,1)} collective-permute-done((bf16[4,128,1024]{2,1,0:T(8,128)(2,1)}, bf16[4,128,1024]{2,1,0:T(8,128)(2,1)}, u32[]{:S(2)}, u32[]{:S(2)}) %collective-permute-start.26) | collective-permute-done | bytes 1048608 | tf_op jit(solution)/shard_map/ppermute | solution.py:590
  471.5 13.2 %collective-permute-done.25 = bf16[4,128,1024]{2,1,0:T(8,128)(2,1)} collective-permute-done((bf16[4,128,1024]{2,1,0:T(8,128)(2,1)}, bf16[4,128,1024]{2,1,0:T(8,128)(2,1)}, u32[]{:S(2)}, u32[]{:S(2)}) %collective-permute-start.25) | collective-permute-done | bytes 1048608 | tf_op jit(solution)/shard_map/ppermute | solution.py:590
  484.7 3.1 fusion.11
  487.9 4.1 add_convert_fusion.2
  492.0 2.0 all-to-all-done.4
  494.0 4.7 all-to-all-start.3
  511.4 1.9 shard_map.253
  514.5 9.7 %collective-permute-done.28 = bf16[128,1024]{1,0:T(8,128)(2,1)} collective-permute-done((bf16[128,1024]{1,0:T(8,128)(2,1)}, bf16[128,1024]{1,0:T(8,128)(2,1)}, u32[]{:S(2)}, u32[]{:S(2)}) %collective-permute-start.28) | collective-permute-done | bytes 262176 | tf_op jit(solution)/shard_map/ppermute | solution.py:590
  524.3 2.1 fusion.19
  526.4 3.4 convert_reduce_fusion
  529.8 4.6 fusion.5
  534.9 3.1 copy.110
  (209 shorter events, 75.0 us)
Async XLA Ops:
  7.2 111.8 %all-gather.4.cloned.1.call-start = ((), (), s32[]{:S(2)}) async-start(), calls=%async_computation.7 | async-start | bytes 4456448 | tf_op jit(solution)/shard_map/all_gather | solution.py:614
  11.7 1.7 collective-permute-start
  46.9 39.8 %copy-start.17 = (bf16[32]{0:T(256)(128)(2,1)S(1)}, bf16[32]{0:T(256)(128)(2,1)}, u32[]{:S(2)}) copy-start(bf16[32]{0:T(256)(128)(2,1)} %param.16) | copy-start | bytes 196
  46.9 39.8 %copy-start.18 = (bf16[32]{0:T(256)(128)(2,1)S(1)}, bf16[32]{0:T(256)(128)(2,1)}, u32[]{:S(2)}) copy-start(bf16[32]{0:T(256)(128)(2,1)} %param.17) | copy-start | bytes 196
  46.9 39.9 %copy-start.19 = (bf16[32]{0:T(256)(128)(2,1)S(1)}, bf16[32]{0:T(256)(128)(2,1)}, u32[]{:S(2)}) copy-start(bf16[32]{0:T(256)(128)(2,1)} %param.18) | copy-start | bytes 196
  46.9 39.9 %copy-start.20 = (bf16[32]{0:T(256)(128)(2,1)S(1)}, bf16[32]{0:T(256)(128)(2,1)}, u32[]{:S(2)}) copy-start(bf16[32]{0:T(256)(128)(2,1)} %param.22) | copy-start | bytes 196
  46.9 39.9 %copy-start.21 = (bf16[32]{0:T(256)(128)(2,1)S(1)}, bf16[32]{0:T(256)(128)(2,1)}, u32[]{:S(2)}) copy-start(bf16[32]{0:T(256)(128)(2,1)} %param.26) | copy-start | bytes 196
  47.0 39.9 %copy-start.22 = (bf16[96]{0:T(256)(128)(2,1)S(1)}, bf16[96]{0:T(256)(128)(2,1)}, u32[]{:S(2)}) copy-start(bf16[96]{0:T(256)(128)(2,1)} %param.20) | copy-start | bytes 580
  47.0 39.9 %copy-start.23 = (bf16[128]{0:T(256)(128)(2,1)S(1)}, bf16[128]{0:T(256)(128)(2,1)}, u32[]{:S(2)}) copy-start(bf16[128]{0:T(256)(128)(2,1)} %param.24) | copy-start | bytes 772
  47.0 39.8 %all-to-all-start.2 = ((bf16[8,128,1024]{2,1,0:T(8,128)(2,1)}), bf16[8,128,1024]{2,1,0:T(8,128)(2,1)}, u32[]{:S(2)}, u32[]{:S(2)}) async-start(bf16[8,128,1024]{2,1,0:T(8,128)(2,1)} %param.27), calls=%async_computation.2 | async-start | bytes 4194304 | tf_op jit(solution)/shard_map/all_to_all | solution.py:646
  51.6 243.7 %all-gather.6.cloned.1.call-start = ((), (), s32[]{:S(2)}) async-start(), calls=%async_computation.8 | async-start | bytes 8912896 | tf_op jit(solution)/shard_map/all_gather | solution.py:639
  52.5 50.0 %collective-permute-start.1 = (bf16[8,128,1024]{2,1,0:T(8,128)(2,1)}, bf16[8,128,1024]{2,1,0:T(8,128)(2,1)}, u32[]{:S(2)}, u32[]{:S(2)}) collective-permute-start(bf16[8,128,1024]{2,1,0:T(8,128)(2,1)} %all_to_all.43.mine_ref), channel_id=1, source_target_pairs={{0,1},{1,0},{2,3},{3,2},{4,5},{5,4},{6,7},{7,6},{8,9},{9,8},{10,11... | collective-permute-start | bytes 6291464 | tf_op jit(solution)/shard_map/ppermute | solution.py:590
  86.8 25.5 %collective-permute-start.2 = (bf16[8,128,1024]{2,1,0:T(8,128)(2,1)}, bf16[8,128,1024]{2,1,0:T(8,128)(2,1)}, u32[]{:S(2)}, u32[]{:S(2)}) collective-permute-start(bf16[8,128,1024]{2,1,0:T(8,128)(2,1)} %all-to-all-done.2.mine_ref), channel_id=1, source_target_pairs={{0,1},{1,0},{2,3},{3,2},{4,5},{5,4},{6,7},{7,6},{8,9},{9,8},{10,11... | collective-permute-start | bytes 6291464 | tf_op jit(solution)/shard_map/ppermute | solution.py:590
  88.9 12.2 %all-to-all-start.1 = ((bf16[32,2,208]{2,1,0:T(2,128)(2,1)}), bf16[32,2,208]{2,1,0:T(2,128)(2,1)S(1)}, u32[]{:S(2)}, u32[]{:S(2)}) async-start(bf16[32,2,208]{2,1,0:T(2,128)(2,1)} %reshape.294), calls=%async_computation.1 | async-start | bytes 65536 | tf_op jit(solution)/shard_map/all_to_all | solution.py:620
  120.3 11.7 %collective-permute-start.3 = (bf16[512,512]{1,0:T(8,128)(2,1)S(1)}, bf16[512,512]{1,0:T(8,128)(2,1)S(1)}, u32[]{:S(2)}, u32[]{:S(2)}) collective-permute-start(bf16[512,512]{1,0:T(8,128)(2,1)S(1)} %get-tuple-element.70), channel_id=1, source_target_pairs={{0,1},{1,0},{2,3},{3,2},{4,5},{5,4},{6,7},{7,6},{8,9},{9,8},{10,11... | collective-permute-start | bytes 1572872 | tf_op jit(solution)/shard_map/ppermute | solution.py:590
  185.3 7.6 %collective-permute-start.6 = (bf16[512,512]{1,0:T(8,128)(2,1)S(1)}, bf16[512,512]{1,0:T(8,128)(2,1)S(1)}, u32[]{:S(2)}, u32[]{:S(2)}) collective-permute-start(bf16[512,512]{1,0:T(8,128)(2,1)S(1)} %get-tuple-element.84), channel_id=1, source_target_pairs={{0,1},{1,0},{2,3},{3,2},{4,5},{5,4},{6,7},{7,6},{8,9},{9,8},{10,11... | collective-permute-start | bytes 1572872 | tf_op jit(solution)/shard_map/ppermute | solution.py:590
  196.4 53.3 %all-to-all-start.6 = ((bf16[4,4,64,2048]{3,2,1,0:T(8,128)(2,1)}), bf16[4,4,64,2048]{3,2,1,0:T(8,128)(2,1)}, u32[]{:S(2)}, u32[]{:S(2)}) async-start(bf16[4,4,64,2048]{3,2,1,0:T(8,128)(2,1)} %bitcast.155), calls=%async_computation.6 | async-start | bytes 8388608 | tf_op jit(solution)/shard_map/all_to_all | solution.py:702
  201.8 57.1 %copy-start.15 = (f32[1,1024]{1,0:T(1,128)S(1)}, f32[1,1024]{1,0:T(1,128)}, u32[]{:S(2)}) copy-start(f32[1,1024]{1,0:T(1,128)} %get-tuple-element.55) | copy-start | bytes 12292
  253.6 12.8 %collective-permute-start.7 = (bf16[64,2048]{1,0:T(8,128)(2,1)}, bf16[64,2048]{1,0:T(8,128)(2,1)}, u32[]{:S(2)}, u32[]{:S(2)}) collective-permute-start(bf16[64,2048]{1,0:T(8,128)(2,1)} %get-tuple-element.80), channel_id=1, source_target_pairs={{0,8},{1,9},{2,10},{3,11},{4,12},{5,13},{6,14},{7,15},{8,0},{9,1},... | collective-permute-start | bytes 786440 | tf_op jit(solution)/shard_map/ppermute | solution.py:590
  253.8 14.8 %collective-permute-start.9 = (bf16[64,2048]{1,0:T(8,128)(2,1)}, bf16[64,2048]{1,0:T(8,128)(2,1)}, u32[]{:S(2)}, u32[]{:S(2)}) collective-permute-start(bf16[64,2048]{1,0:T(8,128)(2,1)} %get-tuple-element.81), channel_id=1, source_target_pairs={{0,24},{1,25},{2,26},{3,27},{4,28},{5,29},{6,30},{7,31},{8,16},{9,... | collective-permute-start | bytes 786440 | tf_op jit(solution)/shard_map/ppermute | solution.py:590
  255.4 24.2 %collective-permute-start.8 = (bf16[64,2048]{1,0:T(8,128)(2,1)S(1)}, bf16[64,2048]{1,0:T(8,128)(2,1)}, u32[]{:S(2)}, u32[]{:S(2)}) collective-permute-start(bf16[64,2048]{1,0:T(8,128)(2,1)S(1)} %get-tuple-element.82), channel_id=1, source_target_pairs={{0,16},{1,17},{2,18},{3,19},{4,20},{5,21},{6,22},{7,23},{8,24},{9,... | collective-permute-start | bytes 786440 | tf_op jit(solution)/shard_map/ppermute | solution.py:590
  280.9 13.5 %collective-permute-start.10 = (f32[32,2048]{1,0:T(8,128)S(1)}, f32[32,2048]{1,0:T(8,128)S(1)}, u32[]{:S(2)}, u32[]{:S(2)}) collective-permute-start(f32[32,2048]{1,0:T(8,128)S(1)} %get-tuple-element.94), channel_id=1, source_target_pairs={{0,1},{1,0},{2,3},{3,2},{4,5},{5,4},{6,7},{7,6},{8,9},{9,8},{10,11... | collective-permute-start | bytes 786440 | tf_op jit(solution)/shard_map/ppermute | solution.py:590
  358.1 29.5 %collective-permute-start.17 = (bf16[4,64,1024]{2,1,0:T(8,128)(2,1)}, bf16[4,64,1024]{2,1,0:T(8,128)(2,1)}, u32[]{:S(2)}, u32[]{:S(2)}) collective-permute-start(bf16[4,64,1024]{2,1,0:T(8,128)(2,1)} %get-tuple-element.74), channel_id=1, source_target_pairs={{0,8},{1,9},{2,10},{3,11},{4,12},{5,13},{6,14},{7,15},{8,0},{9,1},... | collective-permute-start | bytes 1572872 | tf_op jit(solution)/shard_map/ppermute | solution.py:590
  358.1 31.0 %collective-permute-start.19 = (bf16[4,64,1024]{2,1,0:T(8,128)(2,1)S(1)}, bf16[4,64,1024]{2,1,0:T(8,128)(2,1)}, u32[]{:S(2)}, u32[]{:S(2)}) collective-permute-start(bf16[4,64,1024]{2,1,0:T(8,128)(2,1)S(1)} %get-tuple-element.75), channel_id=1, source_target_pairs={{0,24},{1,25},{2,26},{3,27},{4,28},{5,29},{6,30},{7,31},{8,16},{9,... | collective-permute-start | bytes 1572872 | tf_op jit(solution)/shard_map/ppermute | solution.py:590
  376.7 58.4 %all-to-all-start.5 = ((f32[32,1,384]{2,1,0:T(1,128)}), f32[32,1,384]{2,1,0:T(1,128)S(1)}, u32[]{:S(2)}, u32[]{:S(2)}) async-start(f32[32,1,384]{2,1,0:T(1,128)} %copy.85), calls=%async_computation.5 | async-start | bytes 98304 | tf_op jit(solution)/shard_map/all_to_all | solution.py:773
  380.8 27.6 %collective-permute-start.18 = (bf16[4,64,1024]{2,1,0:T(8,128)(2,1)S(1)}, bf16[4,64,1024]{2,1,0:T(8,128)(2,1)}, u32[]{:S(2)}, u32[]{:S(2)}) collective-permute-start(bf16[4,64,1024]{2,1,0:T(8,128)(2,1)S(1)} %get-tuple-element.76), channel_id=1, source_target_pairs={{0,16},{1,17},{2,18},{3,19},{4,20},{5,21},{6,22},{7,23},{8,24},{9,... | collective-permute-start | bytes 1572872 | tf_op jit(solution)/shard_map/ppermute | solution.py:590
  383.7 42.5 %collective-permute-start.5 = (bf16[4,2,128,1024]{3,2,1,0:T(8,128)(2,1)}, bf16[4,2,128,1024]{3,2,1,0:T(8,128)(2,1)}, u32[]{:S(2)}, u32[]{:S(2)}) collective-permute-start(bf16[4,2,128,1024]{3,2,1,0:T(8,128)(2,1)} %get-tuple-element.52), channel_id=1, source_target_pairs={{0,1},{1,0},{2,3},{3,2},{4,5},{5,4},{6,7},{7,6},{8,9},{9,8},{10,11... | collective-permute-start | bytes 6291464 | tf_op jit(solution)/shard_map/ppermute | solution.py:590
  386.1 24.3 %collective-permute-start.11 = (bf16[4,64,1024]{2,1,0:T(8,128)(2,1)}, bf16[4,64,1024]{2,1,0:T(8,128)(2,1)}, u32[]{:S(2)}, u32[]{:S(2)}) collective-permute-start(bf16[4,64,1024]{2,1,0:T(8,128)(2,1)} %get-tuple-element.71), channel_id=1, source_target_pairs={{0,2},{1,3},{2,0},{3,1},{4,6},{5,7},{6,4},{7,5},{8,10},{9,11},{10,... | collective-permute-start | bytes 1572872 | tf_op jit(solution)/shard_map/ppermute | solution.py:590
  387.6 25.4 %collective-permute-start.13 = (bf16[4,64,1024]{2,1,0:T(8,128)(2,1)}, bf16[4,64,1024]{2,1,0:T(8,128)(2,1)}, u32[]{:S(2)}, u32[]{:S(2)}) collective-permute-start(bf16[4,64,1024]{2,1,0:T(8,128)(2,1)} %get-tuple-element.72), channel_id=1, source_target_pairs={{0,6},{1,7},{2,4},{3,5},{4,2},{5,3},{6,0},{7,1},{8,14},{9,15},{10,... | collective-permute-start | bytes 1572872 | tf_op jit(solution)/shard_map/ppermute | solution.py:590
  389.1 25.4 %collective-permute-start.12 = (bf16[4,64,1024]{2,1,0:T(8,128)(2,1)S(1)}, bf16[4,64,1024]{2,1,0:T(8,128)(2,1)S(1)}, u32[]{:S(2)}, u32[]{:S(2)}) collective-permute-start(bf16[4,64,1024]{2,1,0:T(8,128)(2,1)S(1)} %get-tuple-element.73), channel_id=1, source_target_pairs={{0,4},{1,5},{2,6},{3,7},{4,0},{5,1},{6,2},{7,3},{8,12},{9,13},{10,... | collective-permute-start | bytes 1572872 | tf_op jit(solution)/shard_map/ppermute | solution.py:590
  408.5 79.4 %collective-permute-start.4 = (bf16[4,2,128,1024]{3,2,1,0:T(8,128)(2,1)}, bf16[4,2,128,1024]{3,2,1,0:T(8,128)(2,1)}, u32[]{:S(2)}, u32[]{:S(2)}) collective-permute-start(bf16[4,2,128,1024]{3,2,1,0:T(8,128)(2,1)} %get-tuple-element.45), channel_id=1, source_target_pairs={{0,1},{1,0},{2,3},{3,2},{4,5},{5,4},{6,7},{7,6},{8,9},{9,8},{10,11... | collective-permute-start | bytes 6291464 | tf_op jit(solution)/shard_map/ppermute | solution.py:590
  410.4 8.9 %collective-permute-start.20 = (bf16[64,1024]{1,0:T(8,128)(2,1)S(1)}, bf16[64,1024]{1,0:T(8,128)(2,1)S(1)}, u32[]{:S(2)}, u32[]{:S(2)}) collective-permute-start(bf16[64,1024]{1,0:T(8,128)(2,1)S(1)} %get-tuple-element.90), channel_id=1, source_target_pairs={{0,2},{1,3},{2,0},{3,1},{4,6},{5,7},{6,4},{7,5},{8,10},{9,11},{10,... | collective-permute-start | bytes 393224 | tf_op jit(solution)/shard_map/ppermute | solution.py:590
  413.0 9.6 %collective-permute-start.22 = (bf16[64,1024]{1,0:T(8,128)(2,1)S(1)}, bf16[64,1024]{1,0:T(8,128)(2,1)S(1)}, u32[]{:S(2)}, u32[]{:S(2)}) collective-permute-start(bf16[64,1024]{1,0:T(8,128)(2,1)S(1)} %get-tuple-element.91), channel_id=1, source_target_pairs={{0,6},{1,7},{2,4},{3,5},{4,2},{5,3},{6,0},{7,1},{8,14},{9,15},{10,... | collective-permute-start | bytes 393224 | tf_op jit(solution)/shard_map/ppermute | solution.py:590
  415.3 7.9 %collective-permute-start.21 = (bf16[64,1024]{1,0:T(8,128)(2,1)S(1)}, bf16[64,1024]{1,0:T(8,128)(2,1)}, u32[]{:S(2)}, u32[]{:S(2)}) collective-permute-start(bf16[64,1024]{1,0:T(8,128)(2,1)S(1)} %get-tuple-element.92), channel_id=1, source_target_pairs={{0,4},{1,5},{2,6},{3,7},{4,0},{5,1},{6,2},{7,3},{8,12},{9,13},{10,... | collective-permute-start | bytes 393224 | tf_op jit(solution)/shard_map/ppermute | solution.py:590
  419.4 5.3 collective-permute-start.14
  422.7 26.3 %collective-permute-start.24 = (bf16[4,128,1024]{2,1,0:T(8,128)(2,1)}, bf16[4,128,1024]{2,1,0:T(8,128)(2,1)}, u32[]{:S(2)}, u32[]{:S(2)}) collective-permute-start(bf16[4,128,1024]{2,1,0:T(8,128)(2,1)} %get-tuple-element.64), channel_id=1, source_target_pairs={{0,2},{1,3},{2,0},{3,1},{4,6},{5,7},{6,4},{7,5},{8,10},{9,11},{10,... | collective-permute-start | bytes 3145736 | tf_op jit(solution)/shard_map/ppermute | solution.py:590
  423.2 48.3 %collective-permute-start.26 = (bf16[4,128,1024]{2,1,0:T(8,128)(2,1)}, bf16[4,128,1024]{2,1,0:T(8,128)(2,1)}, u32[]{:S(2)}, u32[]{:S(2)}) collective-permute-start(bf16[4,128,1024]{2,1,0:T(8,128)(2,1)} %get-tuple-element.65), channel_id=1, source_target_pairs={{0,6},{1,7},{2,4},{3,5},{4,2},{5,3},{6,0},{7,1},{8,14},{9,15},{10,... | collective-permute-start | bytes 3145736 | tf_op jit(solution)/shard_map/ppermute | solution.py:590
  424.7 60.1 %collective-permute-start.25 = (bf16[4,128,1024]{2,1,0:T(8,128)(2,1)}, bf16[4,128,1024]{2,1,0:T(8,128)(2,1)}, u32[]{:S(2)}, u32[]{:S(2)}) collective-permute-start(bf16[4,128,1024]{2,1,0:T(8,128)(2,1)} %get-tuple-element.66), channel_id=1, source_target_pairs={{0,4},{1,5},{2,6},{3,7},{4,0},{5,1},{6,2},{7,3},{8,12},{9,13},{10,... | collective-permute-start | bytes 3145736 | tf_op jit(solution)/shard_map/ppermute | solution.py:590
  426.2 6.9 %collective-permute-start.16 = (bf16[64,1024]{1,0:T(8,128)(2,1)S(1)}, bf16[64,1024]{1,0:T(8,128)(2,1)S(1)}, u32[]{:S(2)}, u32[]{:S(2)}) collective-permute-start(bf16[64,1024]{1,0:T(8,128)(2,1)S(1)} %get-tuple-element.88), channel_id=1, source_target_pairs={{0,24},{1,25},{2,26},{3,27},{4,28},{5,29},{6,30},{7,31},{8,16},{9,... | collective-permute-start | bytes 393224 | tf_op jit(solution)/shard_map/ppermute | solution.py:590
  433.7 7.6 %collective-permute-start.15 = (bf16[64,1024]{1,0:T(8,128)(2,1)}, bf16[64,1024]{1,0:T(8,128)(2,1)}, u32[]{:S(2)}, u32[]{:S(2)}) collective-permute-start(bf16[64,1024]{1,0:T(8,128)(2,1)} %get-tuple-element.89), channel_id=1, source_target_pairs={{0,16},{1,17},{2,18},{3,19},{4,20},{5,21},{6,22},{7,23},{8,24},{9,... | collective-permute-start | bytes 393224 | tf_op jit(solution)/shard_map/ppermute | solution.py:590
  435.1 52.8 %copy-start.10 = (f32[32,1,384]{2,1,0:T(1,128)}, f32[32,1,384]{2,1,0:T(1,128)S(1)}, u32[]{:S(2)}) copy-start(f32[32,1,384]{2,1,0:T(1,128)S(1)} %all-to-all-done.5) | copy-start | bytes 147460
  435.1 58.9 %all-to-all-start.4 = ((bf16[8,128,1024]{2,1,0:T(8,128)(2,1)}), bf16[8,128,1024]{2,1,0:T(8,128)(2,1)}, u32[]{:S(2)}, u32[]{:S(2)}) async-start(bf16[8,128,1024]{2,1,0:T(8,128)(2,1)} %bitcast.163), calls=%async_computation.4 | async-start | bytes 4194304 | tf_op jit(solution)/shard_map/all_to_all | solution.py:652
  440.5 47.3 %copy-start.3 = (f32[4,2,128,1024]{3,2,1,0:T(8,128)S(1)}, f32[4,2,128,1024]{3,2,1,0:T(8,128)}, u32[]{:S(2)}) copy-start(f32[4,2,128,1024]{3,2,1,0:T(8,128)} %get-tuple-element.44) | copy-start | bytes 12582916
  443.6 67.8 %collective-permute-start.23 = (f32[32,2048]{1,0:T(8,128)}, f32[32,2048]{1,0:T(8,128)}, u32[]{:S(2)}, u32[]{:S(2)}) collective-permute-start(f32[32,2048]{1,0:T(8,128)} %get-tuple-element.85), channel_id=1, source_target_pairs={{0,1},{1,0},{2,3},{3,2},{4,5},{5,4},{6,7},{7,6},{8,9},{9,8},{10,11... | collective-permute-start | bytes 786440 | tf_op jit(solution)/shard_map/ppermute | solution.py:590
  494.0 35.8 %all-to-all-start.3 = ((bf16[8,128,1024]{2,1,0:T(8,128)(2,1)}), bf16[8,128,1024]{2,1,0:T(8,128)(2,1)}, u32[]{:S(2)}, u32[]{:S(2)}) async-start(bf16[8,128,1024]{2,1,0:T(8,128)(2,1)} %bitcast.162), calls=%async_computation.3 | async-start | bytes 4194304 | tf_op jit(solution)/shard_map/all_to_all | solution.py:652
  499.6 13.7 %collective-permute-start.27 = (bf16[128,1024]{1,0:T(8,128)(2,1)}, bf16[128,1024]{1,0:T(8,128)(2,1)}, u32[]{:S(2)}, u32[]{:S(2)}) collective-permute-start(bf16[128,1024]{1,0:T(8,128)(2,1)} %get-tuple-element.77), channel_id=1, source_target_pairs={{0,8},{1,9},{2,10},{3,11},{4,12},{5,13},{6,14},{7,15},{8,0},{9,1},... | collective-permute-start | bytes 786440 | tf_op jit(solution)/shard_map/ppermute | solution.py:590
  500.5 14.1 %collective-permute-start.29 = (bf16[128,1024]{1,0:T(8,128)(2,1)}, bf16[128,1024]{1,0:T(8,128)(2,1)}, u32[]{:S(2)}, u32[]{:S(2)}) collective-permute-start(bf16[128,1024]{1,0:T(8,128)(2,1)} %get-tuple-element.78), channel_id=1, source_target_pairs={{0,24},{1,25},{2,26},{3,27},{4,28},{5,29},{6,30},{7,31},{8,16},{9,... | collective-permute-start | bytes 786440 | tf_op jit(solution)/shard_map/ppermute | solution.py:590
  501.4 22.9 %collective-permute-start.28 = (bf16[128,1024]{1,0:T(8,128)(2,1)}, bf16[128,1024]{1,0:T(8,128)(2,1)}, u32[]{:S(2)}, u32[]{:S(2)}) collective-permute-start(bf16[128,1024]{1,0:T(8,128)(2,1)} %get-tuple-element.79), channel_id=1, source_target_pairs={{0,16},{1,17},{2,18},{3,19},{4,20},{5,21},{6,22},{7,23},{8,24},{9,... | collective-permute-start | bytes 786440 | tf_op jit(solution)/shard_map/ppermute | solution.py:590
  (20 other events, 265.1 us)
Sparse Core Ops, SparseCore 0:
  14.3 91.6 all-gather.3
  109.4 110.6 all-gather.5

commit v2 on v1

--- a/solution.py
+++ b/solution.py
@@ -208,8 +208,8 @@
     )(core.reshape(1), mine, theirs, *extra)
 
 
-def weave(first_core, own, other, chips):
-    rows, hidden = own.shape
+def weave(first_core, own, other, chips, hidden):
+    rows = own.shape[0]
     block = hidden // chips
 
     def kernel(first_ref, own_ref, other_ref, out_ref):
@@ -714,24 +714,41 @@
     block = math.gcd(count, 512)
     h_one, sums_one, qkv_b_grad = pull_one(qkv_grad, first_all, normed, gain_one[None], block)
 
+    qkv_b_grad = (
+        qkv_b_grad.reshape(heads // 2, 3, 2, HD).transpose(0, 2, 1, 3).reshape(qkv_cols)
+    )
+    qkv_b_grad = in_core_order(qkv_b_grad, jnp.zeros_like(qkv_b_grad), 0)
+    sums = [sums_one[0], sums_one[1], dy_sum, qkv_b_grad]
+    sums = jnp.concatenate([value.reshape(n, -1) for value in sums], 1)
+    sums = lax.all_to_all(sums, AXES, split_axis=0, concat_axis=0, tiled=True)
+    sums = jnp.sum(sums, 0)
+
     z, slope = up_project(a_two, shared, b_in[None], block)
     down_w_grad = dot_tn(z, dy).astype(BF)
     down_w_grad = plane_then_deep(down_w_grad)
     du, in_b_grad = down_pull(dy, shared, slope, block)
     in_w_grad = dot_tn(a_two, du).astype(BF)
+    kept, sent, sums_two = pull_two(
+        core, du, shared, normed, gain_two[None], h_one, planes, per_chip, rows_here
+    )
+    combined = to_tokens(kept, sent)
+    per_row = hidden // width
+    riders = jnp.concatenate(
+        [sums_two.T, in_b_grad.reshape(width, per_row), jnp.zeros((width, PAIR - 2 - per_row), F32)], 1
+    )
     in_w_grad = jnp.concatenate(
         [
-            plane_then_deep(in_w_grad[:, : hidden // 2]),
-            deep_then_plane(in_w_grad[:, hidden // 2 :]),
+            plane_then_deep(in_w_grad[:, : 3 * hidden // 4]),
+            deep_then_plane(
+                jnp.concatenate([in_w_grad[:, 3 * hidden // 4 :], riders.astype(BF)], 1)
+            ),
         ],
         1,
     )
+    in_b_grad = in_w_grad[:, hidden + 2 : hidden + 2 + per_row].reshape(hidden // chips)
     in_w_own, in_w_other = own_rows_of(in_w_grad)
-    in_w_grad = weave(first_core, in_w_own, in_w_other, chips)
-    kept, sent, sums_two = pull_two(
-        core, du, shared, normed, gain_two[None], h_one, planes, per_chip, rows_here
-    )
-    combined = to_tokens(kept, sent)
+    ln2_grads = (in_w_own + in_w_other)[:, hidden : hidden + 2]
+    in_w_grad = weave(first_core, in_w_own, in_w_other, chips, hidden)
     kept, sent = out_project(
         core, z, shared, context, w_out, x_mine, (b_out + b_down)[None], planes, per_chip, rows_here
     )
@@ -751,41 +768,20 @@
     dy_here = cotangent.astype(F32)
     input_grad = dy_here + pulled
 
-    qkv_b_grad = (
-        qkv_b_grad.reshape(heads // 2, 3, 2, HD)
-        .transpose(0, 2, 1, 3)
-        .reshape(qkv_cols)
-    )
-    nothing = jnp.zeros_like(qkv_b_grad)
-    qkv_b_grad = in_core_order(qkv_b_grad, nothing, 0)
-    in_b_grad = in_b_grad.reshape(chips, hidden // chips)
-    in_b_grad = in_core_order(in_b_grad[:, None], jnp.zeros_like(in_b_grad)[:, None], 1)
-    sums = [
-        sums_one[0],
-        sums_one[1],
-        sums_two[0],
-        sums_two[1],
-        dy_sum,
-        qkv_b_grad,
-        in_b_grad,
-    ]
-    sums = jnp.concatenate([value.reshape(n, -1) for value in sums], 1)
-    sums = lax.all_to_all(sums, AXES, split_axis=0, concat_axis=0, tiled=True)
-    sums = jnp.sum(sums, 0)
-    b_grad = sums[4 * part : 5 * part]
+    b_grad = sums[2 * part : 3 * part]
     return (
         output,
         input_grad,
         sums[:part],
         sums[part : 2 * part],
-        sums[2 * part : 3 * part],
-        sums[3 * part : 4 * part],
+        ln2_grads[:, 0],
+        ln2_grads[:, 1],
         qkv_w_grad,
-        sums[5 * part : 8 * part],
+        sums[3 * part :],
         out_w_grad,
         b_grad,
         in_w_grad,
-        sums[8 * part :],
+        in_b_grad,
         down_w_grad,
         b_grad,
     )

time: 554 us -> 560 us (1.011)
    all_to_all x1, waiting for transfers between devices: 47.1 us -> 33.2 us  [local(): lax.all_to_all(first_grad, 'pl', split_axis=0, concat_axis=0, tiled=True)]
    ppermute x30, waiting for transfers between devices: 78.7 us -> 88.2 us  [swap(): return lax.ppermute(value, AXES, [(i, i ^ mask) for i in range(n)])]
    all_to_all x1, starting transfers between devices: 4.13 us -> 11 us  [local(): sums = lax.all_to_all(sums, AXES, split_axis=0, concat_axis=0, tiled=True)]
  transfers between devices with their start and end apart: 38 -> 38, of which waited for: 17 -> 14; matrix products, arithmetic and copies ran while one was open for 17% -> 19% of each run, Pallas kernels for 19% -> 16%
where the time goes in v2:
time: 560 us; the launch traced here: 551 us
  waiting for transfers between devices  165 us (29%)
  Pallas kernels  141 us (25%)
  starting transfers between devices  60.8 us (11%)
  matrix products  54.9 us (10%)
  other arithmetic  43.2 us (8%)
  local copies, waits for them, and re-layouts  37.8 us (7%)
  blocking collectives  32.7 us (6%)
  between operations  15.3 us (3%)
    ppermute x30, waiting for transfers between devices, swap(): return lax.ppermute(value, AXES, [(i, i ^ mask) for i in range(n)])  88.2 us
    pallas_call x1, Pallas kernels, attention(): pl.pallas_call(functools.partial(attention_kernel, math.gcd(length, 256))...  43.8 us
    dot_general x4, matrix products, dot_tn(): lax.dot_general(left, right, (((0,), (0,)), ((), ())), preferred_element_...  39.6 us
    all_to_all x1, waiting for transfers between devices, to_chip(): mine = lax.all_to_all(value, 'pl', split_axis=0, concat_axis=0, tiled=True)  34.2 us
    all_to_all x1, waiting for transfers between devices, local(): lax.all_to_all(first_grad, 'pl', split_axis=0, concat_axis=0, tiled=True)  33.2 us
    all_to_all x1, blocking collectives, to_chip(): mine = lax.all_to_all(value, 'pl', split_axis=0, concat_axis=0, tiled=True)  32.7 us
    ppermute x30, starting transfers between devices, swap(): return lax.ppermute(value, AXES, [(i, i ^ mask) for i in range(n)])  26.6 us
    pallas_call x1, Pallas kernels, up_project(): pl.pallas_call(up_kernel, out_shape=(shape, shape), grid=(count // block,...  19.5 us
  transfers between devices with their start and end apart: 38, of which 14 were waited for; matrix products, arithmetic and copies ran while one was open for 19% of the time, Pallas kernels for 16%

profile of v2, /device:TPU:0, one launch (start us, length us, event | category | flops | bytes accessed | tf_op | source)
XLA Modules:
  0.0 550.8 jit_solution(607964872612563061)
XLA Ops:
  14.2 32.7 %all_to_all.43.mine_ref = bf16[8,128,1024]{2,1,0:T(8,128)(2,1)} all-to-all(bf16[8,128,1024]{2,1,0:T(8,128)(2,1)S(1)} %copy-done), channel_id=1, replica_groups=mesh['dp'=4,'pl'=4,'core'=2] {'pl'}, dimensions={0} | all-to-all | bytes 4194304 | tf_op jit(solution)/shard_map/all_to_all | solution.py:646
  47.0 4.6 all-to-all-start.2
  52.6 34.2 %all-to-all-done.2.mine_ref = bf16[8,128,1024]{2,1,0:T(8,128)(2,1)} async-done(((bf16[8,128,1024]{2,1,0:T(8,128)(2,1)}), bf16[8,128,1024]{2,1,0:T(8,128)(2,1)}, u32[]{:S(2)}, u32[]{:S(2)}) %all-to-all-start.2) | async-done | bytes 2097184 | tf_op jit(solution)/shard_map/all_to_all | solution.py:646
  88.9 4.7 all-to-all-start.1
  93.6 3.0 fusion.23
  96.6 4.5 all-to-all-done.1
  102.5 9.7 %shard_map.245 = (bf16[2048,1024]{1,0:T(8,128)(2,1)}, bf16[2048,1024]{1,0:T(8,128)(2,1)}, bf16[2048,1024]{1,0:T(8,128)(2,1)}) custom-call(s32[1]{0:T(128)} %bitcast.core_ref, bf16[8,128,1024]{2,1,0:T(8,128)(2,1)} %all_to_all.43.mine_ref, bf16[8,128,1024]{2,1,0:T(8,128)(2,1)} %collective-permute-done.1.theirs_ref, f32[4,1024]{1,0:T(4,128)} %pad_maximum_fusion.5.gains_ref), custom_call_target="tpu_custom_call" | custom-call | flops 20971520 | bytes 16777216 | tf_op jit(solution)/shard_map/pallas_call | solution.py:193
  112.2 6.7 %shard_map.247 = (bf16[2048,1024]{1,0:T(8,128)(2,1)}, f32[1,1024]{1,0:T(1,128)}) custom-call(s32[1]{0:T(128)} %bitcast.core_ref, bf16[8,128,1024]{2,1,0:T(8,128)(2,1)} %all-to-all-done.2.mine_ref, bf16[8,128,1024]{2,1,0:T(8,128)(2,1)} %collective-permute-done.2.theirs_ref), custom_call_target="tpu_custom_call" | custom-call | flops 20971520 | bytes 8388608 | tf_op jit(solution)/shard_map/pallas_call | solution.py:193
  120.4 11.6 %add_convert_fusion = bf16[2048,1536]{1,0:T(8,128)(2,1)} fusion(bf16[2048,1024]{1,0:T(8,128)(2,1)} %get-tuple-element.40, f32[1536]{0:T(1024)S(1)} %add.227, bf16[1024,2048]{1,0:T(8,128)(2,1)} %all-gather.4.cloned.1.call-done.w_ref), kind=kOutput, calls=%fused_computation | convolution fusion | flops 6448742400 | bytes 13637632 | tf_op jit(solution)/shard_map/dot_general | solution.py:26
  132.3 3.8 convolution_convert_fusion.3
  136.1 43.8 %shard_map.248 = (bf16[2,1024,512]{2,1,0:T(8,128)(2,1)}, bf16[2,1024,1536]{2,1,0:T(8,128)(2,1)}) custom-call(bf16[2,1024,1536]{2,1,0:T(8,128)(2,1)} %bitcast.179, bf16[2,1024,512]{2,1,0:T(8,128)(2,1)} %bitcast.182, f32[1024,128]{1,0:T(8,128)} %get-tuple-element.107.cos_ref, f32[1024,128]{1,0:T(8,128)} %get-tuple-element.106.sin_a_ref, ...), custom_call_target="tpu_custom_call" | custom-call | flops 15032385536 | bytes 18874368 | tf_op jit(solution)/shard_map/pallas_call | solution.py:139
  179.9 5.3 convolution_convert_fusion.4
  185.8 7.1 %convolution_convert_fusion = bf16[1024,1536]{1,0:T(8,128)(2,1)S(1)} fusion(bf16[2048,1024]{1,0:T(8,128)(2,1)S(1)} %copy-done.24, bf16[2048,1536]{1,0:T(8,128)(2,1)S(1)} %bitcast.178), kind=kOutput, calls=%fused_computation.18 | convolution fusion | flops 6444023808 | bytes 13631488 | tf_op jit(solution)/shard_map/dot_general | solution.py:34
  194.1 2.4 copy.91
  196.5 4.9 all-to-all-start.6
  203.9 11.5 %shard_map.251 = (bf16[2048,1024]{1,0:T(8,128)(2,1)}, f32[2,1024]{1,0:T(2,128)}, f32[1,1536]{1,0:T(1,128)}) custom-call(bf16[2048,1536]{1,0:T(8,128)(2,1)} %bitcast.177, bf16[1024,2048]{1,0:T(8,128)(2,1)} %all-gather.4.cloned.1.call-done.w_ref, bf16[2048,1024]{1,0:T(8,128)(2,1)} %get-tuple-element.48.normed_ref, f32[1,1024]{1,0:T(1,128)} %copy-done.9), custom_call_target="tpu_custom_call" | custom-call | flops 6442450944 | bytes 14680064 | tf_op jit(solution)/shard_map/pallas_call | solution.py:382
  216.3 33.2 %all-to-all-done.6 = bf16[4,4,64,2048]{3,2,1,0:T(8,128)(2,1)} async-done(((bf16[4,4,64,2048]{3,2,1,0:T(8,128)(2,1)}), bf16[4,4,64,2048]{3,2,1,0:T(8,128)(2,1)}, u32[]{:S(2)}, u32[]{:S(2)}) %all-to-all-start.6) | async-done | bytes 4194336 | tf_op jit(solution)/shard_map/all_to_all | solution.py:702
  249.5 3.1 reduce_sum.62
  258.0 11.0 %all-to-all-start.5 = ((f32[32,1,192]{2,1,0:T(1,128)}), f32[32,1,192]{2,1,0:T(1,128)S(1)}, u32[]{:S(2)}, u32[]{:S(2)}) async-start(f32[32,1,192]{2,1,0:T(1,128)} %all_to_all.33), calls=%async_computation.5 | async-start | bytes 65536 | tf_op jit(solution)/shard_map/all_to_all | solution.py:723
  269.1 11.0 %collective-permute-done.21 = bf16[64,2048]{1,0:T(8,128)(2,1)} collective-permute-done((bf16[64,2048]{1,0:T(8,128)(2,1)S(1)}, bf16[64,2048]{1,0:T(8,128)(2,1)}, u32[]{:S(2)}, u32[]{:S(2)}) %collective-permute-start.21) | collective-permute-done | bytes 262176 | tf_op jit(solution)/shard_map/ppermute | solution.py:590
  288.9 19.5 %shard_map.246 = (bf16[2048,2048]{1,0:T(8,128)(2,1)}, bf16[2048,2048]{1,0:T(8,128)(2,1)}) custom-call(bf16[2048,1024]{1,0:T(8,128)(2,1)} %get-tuple-element.38.a_ref, bf16[16,256,1024]{2,1,0:T(8,128)(2,1)} %bitcast.144, bf16[16,256,1024]{2,1,0:T(8,128)(2,1)} %bitcast.145, f32[1,2048]{1,0:T(1,128)} %fusion.28.bias_ref), custom_call_target="tpu_custom_call" | custom-call | flops 8589934592 | bytes 25165824 | tf_op jit(solution)/shard_map/pallas_call | solution.py:294
  308.4 15.0 %shard_map.250 = (bf16[2048,2048]{1,0:T(8,128)(2,1)}, f32[1,2048]{1,0:T(1,128)}) custom-call(bf16[2048,1024]{1,0:T(8,128)(2,1)} %get-tuple-element.42.dy_ref, bf16[16,256,1024]{2,1,0:T(8,128)(2,1)} %bitcast.146, bf16[2048,2048]{1,0:T(8,128)(2,1)} %get-tuple-element.46.slope_ref), custom_call_target="tpu_custom_call" | custom-call | flops 8589934592 | bytes 25165824 | tf_op jit(solution)/shard_map/pallas_call | solution.py:337
  323.4 14.0 %convolution_convert_fusion.1 = bf16[1024,2048]{1,0:T(8,128)(2,1)} fusion(bf16[2048,1024]{1,0:T(8,128)(2,1)} %get-tuple-element.38.a_ref, bf16[2048,2048]{1,0:T(8,128)(2,1)} %get-tuple-element.47.d_ref), kind=kOutput, calls=%fused_computation.19 | convolution fusion | flops 8592031744 | bytes 16777216 | tf_op jit(solution)/shard_map/dot_general | solution.py:34
  337.4 15.9 %shard_map.252 = (f32[4,2,128,1024]{3,2,1,0:T(8,128)}, bf16[4,2,128,1024]{3,2,1,0:T(8,128)(2,1)}, f32[2,1024]{1,0:T(2,128)}) custom-call(s32[1]{0:T(128)} %bitcast.core_ref, bf16[2048,2048]{1,0:T(8,128)(2,1)} %get-tuple-element.47.d_ref, bf16[16,256,1024]{2,1,0:T(8,128)(2,1)} %bitcast.147, bf16[16,256,1024]{2,1,0:T(8,128)(2,1)} %bitcast.148, ...), custom_call_target="tpu_custom_call" | custom-call | flops 8589934592 | bytes 25165824 | tf_op jit(solution)/shard_map/pallas_call | solution.py:471
  358.7 13.0 %convolution_convert_fusion.2 = bf16[2048,1024]{1,0:T(8,128)(2,1)} fusion(bf16[2048,2048]{1,0:T(8,128)(2,1)} %get-tuple-element.39.z_ref, bf16[2048,1024]{1,0:T(8,128)(2,1)S(1)} %copy-done.23), kind=kOutput, calls=%fused_computation.20 | convolution fusion | flops 8592031744 | bytes 16777216 | tf_op jit(solution)/shard_map/dot_general | solution.py:34
  372.0 2.4 collective-permute-start.13
  379.4 17.0 %shard_map.249 = (f32[4,2,128,1024]{3,2,1,0:T(8,128)}, bf16[4,2,128,1024]{3,2,1,0:T(8,128)(2,1)}) custom-call(s32[1]{0:T(128)} %bitcast.core_ref, bf16[2048,2048]{1,0:T(8,128)(2,1)} %get-tuple-element.39.z_ref, bf16[16,256,1024]{2,1,0:T(8,128)(2,1)} %bitcast.149, bf16[2048,512]{1,0:T(8,128)(2,1)} %bitcast.181, bf16[512,1024]{1,0:T(8,128)(2,1)} %copy-done.6, ...), custom_call_target="tpu_custom_call" | custom-call | flops 10737418240 | bytes 27262976 | tf_op jit(solution)/shard_map/pallas_call | solution.py:528
  396.4 3.7 dynamic-slice_bitcast_fusion.2
  402.7 11.7 %collective-permute-done.8 = bf16[4,64,1536]{2,1,0:T(8,128)(2,1)} collective-permute-done((bf16[4,64,1536]{2,1,0:T(8,128)(2,1)}, bf16[4,64,1536]{2,1,0:T(8,128)(2,1)}, u32[]{:S(2)}, u32[]{:S(2)}) %collective-permute-start.8) | collective-permute-done | bytes 786464 | tf_op jit(solution)/shard_map/ppermute | solution.py:590
  416.4 2.2 fusion.14
  420.3 2.0 collective-permute-start.11
  423.7 3.9 collective-permute-done.9
  429.1 2.6 collective-permute-done.11
  433.1 5.7 %collective-permute-done.10 = bf16[64,1536]{1,0:T(8,128)(2,1)} collective-permute-done((bf16[64,1536]{1,0:T(8,128)(2,1)S(1)}, bf16[64,1536]{1,0:T(8,128)(2,1)}, u32[]{:S(2)}, u32[]{:S(2)}) %collective-permute-start.10) | collective-permute-done | bytes 196640 | tf_op jit(solution)/shard_map/ppermute | solution.py:590
  441.4 5.0 add_convert_fusion.1
  446.4 4.4 all-to-all-start.4
  451.7 2.3 collective-permute-done.24
  454.0 23.4 %collective-permute-done.26 = bf16[4,128,1024]{2,1,0:T(8,128)(2,1)} collective-permute-done((bf16[4,128,1024]{2,1,0:T(8,128)(2,1)}, bf16[4,128,1024]{2,1,0:T(8,128)(2,1)}, u32[]{:S(2)}, u32[]{:S(2)}) %collective-permute-start.26) | collective-permute-done | bytes 1048608 | tf_op jit(solution)/shard_map/ppermute | solution.py:590
  477.3 21.5 %collective-permute-done.25 = bf16[4,128,1024]{2,1,0:T(8,128)(2,1)} collective-permute-done((bf16[4,128,1024]{2,1,0:T(8,128)(2,1)}, bf16[4,128,1024]{2,1,0:T(8,128)(2,1)}, u32[]{:S(2)}, u32[]{:S(2)}) %collective-permute-start.25) | collective-permute-done | bytes 1048608 | tf_op jit(solution)/shard_map/ppermute | solution.py:590
  498.8 3.1 fusion.11
  506.3 3.8 add_convert_fusion.2
  510.1 4.5 all-to-all-start.3
  519.9 5.0 collective-permute-done.28
  524.9 2.1 fusion.19
  526.9 3.4 convert_reduce_fusion
  530.3 5.1 all-to-all-done.3
  535.4 4.6 fusion.5
  540.5 3.1 copy.99
  (209 shorter events, 67.2 us)
Async XLA Ops:
  7.2 111.8 %all-gather.4.cloned.1.call-start = ((), (), s32[]{:S(2)}) async-start(), calls=%async_computation.7 | async-start | bytes 4456448 | tf_op jit(solution)/shard_map/all_gather | solution.py:614
  11.7 1.7 collective-permute-start
  46.9 39.9 %copy-start.14 = (bf16[32]{0:T(256)(128)(2,1)S(1)}, bf16[32]{0:T(256)(128)(2,1)}, u32[]{:S(2)}) copy-start(bf16[32]{0:T(256)(128)(2,1)} %param.16) | copy-start | bytes 196
  46.9 39.9 %copy-start.15 = (bf16[32]{0:T(256)(128)(2,1)S(1)}, bf16[32]{0:T(256)(128)(2,1)}, u32[]{:S(2)}) copy-start(bf16[32]{0:T(256)(128)(2,1)} %param.17) | copy-start | bytes 196
  46.9 39.9 %copy-start.16 = (bf16[32]{0:T(256)(128)(2,1)S(1)}, bf16[32]{0:T(256)(128)(2,1)}, u32[]{:S(2)}) copy-start(bf16[32]{0:T(256)(128)(2,1)} %param.18) | copy-start | bytes 196
  46.9 39.9 %copy-start.17 = (bf16[32]{0:T(256)(128)(2,1)S(1)}, bf16[32]{0:T(256)(128)(2,1)}, u32[]{:S(2)}) copy-start(bf16[32]{0:T(256)(128)(2,1)} %param.22) | copy-start | bytes 196
  46.9 39.9 %copy-start.18 = (bf16[32]{0:T(256)(128)(2,1)S(1)}, bf16[32]{0:T(256)(128)(2,1)}, u32[]{:S(2)}) copy-start(bf16[32]{0:T(256)(128)(2,1)} %param.26) | copy-start | bytes 196
  47.0 39.9 %copy-start.19 = (bf16[96]{0:T(256)(128)(2,1)S(1)}, bf16[96]{0:T(256)(128)(2,1)}, u32[]{:S(2)}) copy-start(bf16[96]{0:T(256)(128)(2,1)} %param.20) | copy-start | bytes 580
  47.0 39.9 %copy-start.20 = (bf16[128]{0:T(256)(128)(2,1)S(1)}, bf16[128]{0:T(256)(128)(2,1)}, u32[]{:S(2)}) copy-start(bf16[128]{0:T(256)(128)(2,1)} %param.24) | copy-start | bytes 772
  47.0 39.8 %all-to-all-start.2 = ((bf16[8,128,1024]{2,1,0:T(8,128)(2,1)}), bf16[8,128,1024]{2,1,0:T(8,128)(2,1)}, u32[]{:S(2)}, u32[]{:S(2)}) async-start(bf16[8,128,1024]{2,1,0:T(8,128)(2,1)} %param.27), calls=%async_computation.2 | async-start | bytes 4194304 | tf_op jit(solution)/shard_map/all_to_all | solution.py:646
  51.6 237.3 %all-gather.6.cloned.1.call-start = ((), (), s32[]{:S(2)}) async-start(), calls=%async_computation.8 | async-start | bytes 8912896 | tf_op jit(solution)/shard_map/all_gather | solution.py:639
  52.5 50.0 %collective-permute-start.1 = (bf16[8,128,1024]{2,1,0:T(8,128)(2,1)}, bf16[8,128,1024]{2,1,0:T(8,128)(2,1)}, u32[]{:S(2)}, u32[]{:S(2)}) collective-permute-start(bf16[8,128,1024]{2,1,0:T(8,128)(2,1)} %all_to_all.43.mine_ref), channel_id=1, source_target_pairs={{0,1},{1,0},{2,3},{3,2},{4,5},{5,4},{6,7},{7,6},{8,9},{9,8},{10,11... | collective-permute-start | bytes 6291464 | tf_op jit(solution)/shard_map/ppermute | solution.py:590
  86.8 25.4 %collective-permute-start.2 = (bf16[8,128,1024]{2,1,0:T(8,128)(2,1)}, bf16[8,128,1024]{2,1,0:T(8,128)(2,1)}, u32[]{:S(2)}, u32[]{:S(2)}) collective-permute-start(bf16[8,128,1024]{2,1,0:T(8,128)(2,1)} %all-to-all-done.2.mine_ref), channel_id=1, source_target_pairs={{0,1},{1,0},{2,3},{3,2},{4,5},{5,4},{6,7},{7,6},{8,9},{9,8},{10,11... | collective-permute-start | bytes 6291464 | tf_op jit(solution)/shard_map/ppermute | solution.py:590
  88.9 12.2 %all-to-all-start.1 = ((bf16[32,2,208]{2,1,0:T(2,128)(2,1)}), bf16[32,2,208]{2,1,0:T(2,128)(2,1)S(1)}, u32[]{:S(2)}, u32[]{:S(2)}) async-start(bf16[32,2,208]{2,1,0:T(2,128)(2,1)} %reshape.292), calls=%async_computation.1 | async-start | bytes 65536 | tf_op jit(solution)/shard_map/all_to_all | solution.py:620
  120.2 11.7 %collective-permute-start.3 = (bf16[512,512]{1,0:T(8,128)(2,1)S(1)}, bf16[512,512]{1,0:T(8,128)(2,1)S(1)}, u32[]{:S(2)}, u32[]{:S(2)}) collective-permute-start(bf16[512,512]{1,0:T(8,128)(2,1)S(1)} %get-tuple-element.70), channel_id=1, source_target_pairs={{0,1},{1,0},{2,3},{3,2},{4,5},{5,4},{6,7},{7,6},{8,9},{9,8},{10,11... | collective-permute-start | bytes 1572872 | tf_op jit(solution)/shard_map/ppermute | solution.py:590
  185.4 7.6 %collective-permute-start.19 = (bf16[512,512]{1,0:T(8,128)(2,1)S(1)}, bf16[512,512]{1,0:T(8,128)(2,1)S(1)}, u32[]{:S(2)}, u32[]{:S(2)}) collective-permute-start(bf16[512,512]{1,0:T(8,128)(2,1)S(1)} %get-tuple-element.84), channel_id=1, source_target_pairs={{0,1},{1,0},{2,3},{3,2},{4,5},{5,4},{6,7},{7,6},{8,9},{9,8},{10,11... | collective-permute-start | bytes 1572872 | tf_op jit(solution)/shard_map/ppermute | solution.py:590
  196.5 53.1 %all-to-all-start.6 = ((bf16[4,4,64,2048]{3,2,1,0:T(8,128)(2,1)}), bf16[4,4,64,2048]{3,2,1,0:T(8,128)(2,1)}, u32[]{:S(2)}, u32[]{:S(2)}) async-start(bf16[4,4,64,2048]{3,2,1,0:T(8,128)(2,1)} %bitcast.150), calls=%async_computation.6 | async-start | bytes 8388608 | tf_op jit(solution)/shard_map/all_to_all | solution.py:702
  215.4 41.6 %copy-start.11 = (f32[2,1024]{1,0:T(2,128)S(1)}, f32[2,1024]{1,0:T(2,128)}, u32[]{:S(2)}) copy-start(f32[2,1024]{1,0:T(2,128)} %get-tuple-element.53) | copy-start | bytes 24580
  253.5 15.5 %collective-permute-start.20 = (bf16[64,2048]{1,0:T(8,128)(2,1)}, bf16[64,2048]{1,0:T(8,128)(2,1)}, u32[]{:S(2)}, u32[]{:S(2)}) collective-permute-start(bf16[64,2048]{1,0:T(8,128)(2,1)} %get-tuple-element.80), channel_id=1, source_target_pairs={{0,8},{1,9},{2,10},{3,11},{4,12},{5,13},{6,14},{7,15},{8,0},{9,1},... | collective-permute-start | bytes 786440 | tf_op jit(solution)/shard_map/ppermute | solution.py:590
  253.8 15.3 %collective-permute-start.22 = (bf16[64,2048]{1,0:T(8,128)(2,1)}, bf16[64,2048]{1,0:T(8,128)(2,1)}, u32[]{:S(2)}, u32[]{:S(2)}) collective-permute-start(bf16[64,2048]{1,0:T(8,128)(2,1)} %get-tuple-element.81), channel_id=1, source_target_pairs={{0,24},{1,25},{2,26},{3,27},{4,28},{5,29},{6,30},{7,31},{8,16},{9,... | collective-permute-start | bytes 786440 | tf_op jit(solution)/shard_map/ppermute | solution.py:590
  255.4 24.6 %collective-permute-start.21 = (bf16[64,2048]{1,0:T(8,128)(2,1)S(1)}, bf16[64,2048]{1,0:T(8,128)(2,1)}, u32[]{:S(2)}, u32[]{:S(2)}) collective-permute-start(bf16[64,2048]{1,0:T(8,128)(2,1)S(1)} %get-tuple-element.82), channel_id=1, source_target_pairs={{0,16},{1,17},{2,18},{3,19},{4,20},{5,21},{6,22},{7,23},{8,24},{9,... | collective-permute-start | bytes 786440 | tf_op jit(solution)/shard_map/ppermute | solution.py:590
  258.0 24.7 %all-to-all-start.5 = ((f32[32,1,192]{2,1,0:T(1,128)}), f32[32,1,192]{2,1,0:T(1,128)S(1)}, u32[]{:S(2)}, u32[]{:S(2)}) async-start(f32[32,1,192]{2,1,0:T(1,128)} %all_to_all.33), calls=%async_computation.5 | async-start | bytes 65536 | tf_op jit(solution)/shard_map/all_to_all | solution.py:723
  281.3 2.6 collective-permute-start.23
  283.9 256.0 %copy-start.21 = (f32[32]{0:T(128)}, f32[32]{0:T(128)S(1)}, u32[]{:S(2)}) copy-start(f32[32]{0:T(128)S(1)} %get-tuple-element.161) | copy-start | bytes 388
  357.5 19.8 %collective-permute-start.12 = (bf16[4,64,640]{2,1,0:T(8,128)(2,1)S(1)}, bf16[4,64,640]{2,1,0:T(8,128)(2,1)S(1)}, u32[]{:S(2)}, u32[]{:S(2)}) collective-permute-start(bf16[4,64,640]{2,1,0:T(8,128)(2,1)S(1)} %get-tuple-element.74), channel_id=1, source_target_pairs={{0,8},{1,9},{2,10},{3,11},{4,12},{5,13},{6,14},{7,15},{8,0},{9,1},... | collective-permute-start | bytes 983048 | tf_op jit(solution)/shard_map/ppermute | solution.py:590
  357.5 21.3 %collective-permute-start.14 = (bf16[4,64,640]{2,1,0:T(8,128)(2,1)S(1)}, bf16[4,64,640]{2,1,0:T(8,128)(2,1)S(1)}, u32[]{:S(2)}, u32[]{:S(2)}) collective-permute-start(bf16[4,64,640]{2,1,0:T(8,128)(2,1)S(1)} %get-tuple-element.75), channel_id=1, source_target_pairs={{0,24},{1,25},{2,26},{3,27},{4,28},{5,29},{6,30},{7,31},{8,16},{9,... | collective-permute-start | bytes 983048 | tf_op jit(solution)/shard_map/ppermute | solution.py:590
  372.0 28.0 %collective-permute-start.13 = (bf16[4,64,640]{2,1,0:T(8,128)(2,1)}, bf16[4,64,640]{2,1,0:T(8,128)(2,1)}, u32[]{:S(2)}, u32[]{:S(2)}) collective-permute-start(bf16[4,64,640]{2,1,0:T(8,128)(2,1)} %get-tuple-element.76), channel_id=1, source_target_pairs={{0,16},{1,17},{2,18},{3,19},{4,20},{5,21},{6,22},{7,23},{8,24},{9,... | collective-permute-start | bytes 983048 | tf_op jit(solution)/shard_map/ppermute | solution.py:590
  374.4 67.0 %collective-permute-start.5 = (bf16[4,2,128,1024]{3,2,1,0:T(8,128)(2,1)}, bf16[4,2,128,1024]{3,2,1,0:T(8,128)(2,1)}, u32[]{:S(2)}, u32[]{:S(2)}) collective-permute-start(bf16[4,2,128,1024]{3,2,1,0:T(8,128)(2,1)} %get-tuple-element.52), channel_id=1, source_target_pairs={{0,1},{1,0},{2,3},{3,2},{4,5},{5,4},{6,7},{7,6},{8,9},{9,8},{10,11... | collective-permute-start | bytes 6291464 | tf_op jit(solution)/shard_map/ppermute | solution.py:590
  375.9 25.4 %collective-permute-start.6 = (bf16[4,64,1536]{2,1,0:T(8,128)(2,1)}, bf16[4,64,1536]{2,1,0:T(8,128)(2,1)}, u32[]{:S(2)}, u32[]{:S(2)}) collective-permute-start(bf16[4,64,1536]{2,1,0:T(8,128)(2,1)} %get-tuple-element.71), channel_id=1, source_target_pairs={{0,2},{1,3},{2,0},{3,1},{4,6},{5,7},{6,4},{7,5},{8,10},{9,11},{10,... | collective-permute-start | bytes 2359304 | tf_op jit(solution)/shard_map/ppermute | solution.py:590
  377.3 37.1 %collective-permute-start.8 = (bf16[4,64,1536]{2,1,0:T(8,128)(2,1)}, bf16[4,64,1536]{2,1,0:T(8,128)(2,1)}, u32[]{:S(2)}, u32[]{:S(2)}) collective-permute-start(bf16[4,64,1536]{2,1,0:T(8,128)(2,1)} %get-tuple-element.72), channel_id=1, source_target_pairs={{0,6},{1,7},{2,4},{3,5},{4,2},{5,3},{6,0},{7,1},{8,14},{9,15},{10,... | collective-permute-start | bytes 2359304 | tf_op jit(solution)/shard_map/ppermute | solution.py:590
  378.8 37.0 %collective-permute-start.7 = (bf16[4,64,1536]{2,1,0:T(8,128)(2,1)}, bf16[4,64,1536]{2,1,0:T(8,128)(2,1)}, u32[]{:S(2)}, u32[]{:S(2)}) collective-permute-start(bf16[4,64,1536]{2,1,0:T(8,128)(2,1)} %get-tuple-element.73), channel_id=1, source_target_pairs={{0,4},{1,5},{2,6},{3,7},{4,0},{5,1},{6,2},{7,3},{8,12},{9,13},{10,... | collective-permute-start | bytes 2359304 | tf_op jit(solution)/shard_map/ppermute | solution.py:590
  400.0 106.3 %collective-permute-start.4 = (bf16[4,2,128,1024]{3,2,1,0:T(8,128)(2,1)}, bf16[4,2,128,1024]{3,2,1,0:T(8,128)(2,1)}, u32[]{:S(2)}, u32[]{:S(2)}) collective-permute-start(bf16[4,2,128,1024]{3,2,1,0:T(8,128)(2,1)} %get-tuple-element.45), channel_id=1, source_target_pairs={{0,1},{1,0},{2,3},{3,2},{4,5},{5,4},{6,7},{7,6},{8,9},{9,8},{10,11... | collective-permute-start | bytes 6291464 | tf_op jit(solution)/shard_map/ppermute | solution.py:590
  401.2 18.2 %collective-permute-start.15 = (bf16[64,640]{1,0:T(8,128)(2,1)S(1)}, bf16[64,640]{1,0:T(8,128)(2,1)S(1)}, u32[]{:S(2)}, u32[]{:S(2)}) collective-permute-start(bf16[64,640]{1,0:T(8,128)(2,1)S(1)} %get-tuple-element.94), channel_id=1, source_target_pairs={{0,2},{1,3},{2,0},{3,1},{4,6},{5,7},{6,4},{7,5},{8,10},{9,11},{10,... | collective-permute-start | bytes 245768 | tf_op jit(solution)/shard_map/ppermute | solution.py:590
  414.4 5.9 %collective-permute-start.17 = (bf16[64,640]{1,0:T(8,128)(2,1)S(1)}, bf16[64,640]{1,0:T(8,128)(2,1)S(1)}, u32[]{:S(2)}, u32[]{:S(2)}) collective-permute-start(bf16[64,640]{1,0:T(8,128)(2,1)S(1)} %get-tuple-element.95), channel_id=1, source_target_pairs={{0,6},{1,7},{2,4},{3,5},{4,2},{5,3},{6,0},{7,1},{8,14},{9,15},{10,... | collective-permute-start | bytes 245768 | tf_op jit(solution)/shard_map/ppermute | solution.py:590
  415.8 6.5 %collective-permute-start.16 = (bf16[64,640]{1,0:T(8,128)(2,1)S(1)}, bf16[64,640]{1,0:T(8,128)(2,1)S(1)}, u32[]{:S(2)}, u32[]{:S(2)}) collective-permute-start(bf16[64,640]{1,0:T(8,128)(2,1)S(1)} %get-tuple-element.96), channel_id=1, source_target_pairs={{0,4},{1,5},{2,6},{3,7},{4,0},{5,1},{6,2},{7,3},{8,12},{9,13},{10,... | collective-permute-start | bytes 245768 | tf_op jit(solution)/shard_map/ppermute | solution.py:590
  419.4 8.2 %collective-permute-start.9 = (bf16[64,1536]{1,0:T(8,128)(2,1)}, bf16[64,1536]{1,0:T(8,128)(2,1)}, u32[]{:S(2)}, u32[]{:S(2)}) collective-permute-start(bf16[64,1536]{1,0:T(8,128)(2,1)} %get-tuple-element.85), channel_id=1, source_target_pairs={{0,8},{1,9},{2,10},{3,11},{4,12},{5,13},{6,14},{7,15},{8,0},{9,1},... | collective-permute-start | bytes 589832 | tf_op jit(solution)/shard_map/ppermute | solution.py:590
  420.3 11.3 %collective-permute-start.11 = (bf16[64,1536]{1,0:T(8,128)(2,1)S(1)}, bf16[64,1536]{1,0:T(8,128)(2,1)}, u32[]{:S(2)}, u32[]{:S(2)}) collective-permute-start(bf16[64,1536]{1,0:T(8,128)(2,1)S(1)} %get-tuple-element.86), channel_id=1, source_target_pairs={{0,24},{1,25},{2,26},{3,27},{4,28},{5,29},{6,30},{7,31},{8,16},{9,... | collective-permute-start | bytes 589832 | tf_op jit(solution)/shard_map/ppermute | solution.py:590
  422.3 16.5 %collective-permute-start.10 = (bf16[64,1536]{1,0:T(8,128)(2,1)S(1)}, bf16[64,1536]{1,0:T(8,128)(2,1)}, u32[]{:S(2)}, u32[]{:S(2)}) collective-permute-start(bf16[64,1536]{1,0:T(8,128)(2,1)S(1)} %get-tuple-element.87), channel_id=1, source_target_pairs={{0,16},{1,17},{2,18},{3,19},{4,20},{5,21},{6,22},{7,23},{8,24},{9,... | collective-permute-start | bytes 589832 | tf_op jit(solution)/shard_map/ppermute | solution.py:590
  427.6 26.3 %collective-permute-start.24 = (bf16[4,128,1024]{2,1,0:T(8,128)(2,1)}, bf16[4,128,1024]{2,1,0:T(8,128)(2,1)}, u32[]{:S(2)}, u32[]{:S(2)}) collective-permute-start(bf16[4,128,1024]{2,1,0:T(8,128)(2,1)} %get-tuple-element.66), channel_id=1, source_target_pairs={{0,2},{1,3},{2,0},{3,1},{4,6},{5,7},{6,4},{7,5},{8,10},{9,11},{10,... | collective-permute-start | bytes 3145736 | tf_op jit(solution)/shard_map/ppermute | solution.py:590
  431.6 45.7 %collective-permute-start.26 = (bf16[4,128,1024]{2,1,0:T(8,128)(2,1)}, bf16[4,128,1024]{2,1,0:T(8,128)(2,1)}, u32[]{:S(2)}, u32[]{:S(2)}) collective-permute-start(bf16[4,128,1024]{2,1,0:T(8,128)(2,1)} %get-tuple-element.67), channel_id=1, source_target_pairs={{0,6},{1,7},{2,4},{3,5},{4,2},{5,3},{6,0},{7,1},{8,14},{9,15},{10,... | collective-permute-start | bytes 3145736 | tf_op jit(solution)/shard_map/ppermute | solution.py:590
  438.8 60.1 %collective-permute-start.25 = (bf16[4,128,1024]{2,1,0:T(8,128)(2,1)}, bf16[4,128,1024]{2,1,0:T(8,128)(2,1)}, u32[]{:S(2)}, u32[]{:S(2)}) collective-permute-start(bf16[4,128,1024]{2,1,0:T(8,128)(2,1)} %get-tuple-element.68), channel_id=1, source_target_pairs={{0,4},{1,5},{2,6},{3,7},{4,0},{5,1},{6,2},{7,3},{8,12},{9,13},{10,... | collective-permute-start | bytes 3145736 | tf_op jit(solution)/shard_map/ppermute | solution.py:590
  446.4 63.7 %all-to-all-start.4 = ((bf16[8,128,1024]{2,1,0:T(8,128)(2,1)}), bf16[8,128,1024]{2,1,0:T(8,128)(2,1)}, u32[]{:S(2)}, u32[]{:S(2)}) async-start(bf16[8,128,1024]{2,1,0:T(8,128)(2,1)} %bitcast.155), calls=%async_computation.4 | async-start | bytes 4194304 | tf_op jit(solution)/shard_map/all_to_all | solution.py:652
  450.9 55.4 %copy-start.3 = (f32[4,2,128,1024]{3,2,1,0:T(8,128)S(1)}, f32[4,2,128,1024]{3,2,1,0:T(8,128)}, u32[]{:S(2)}) copy-start(f32[4,2,128,1024]{3,2,1,0:T(8,128)} %get-tuple-element.44) | copy-start | bytes 12582916
  451.7 62.9 %collective-permute-start.18 = (f32[32,2176]{1,0:T(8,128)}, f32[32,2176]{1,0:T(8,128)S(1)}, u32[]{:S(2)}, u32[]{:S(2)}) collective-permute-start(f32[32,2176]{1,0:T(8,128)} %dynamic-slice_bitcast_fusion.9), channel_id=1, source_target_pairs={{0,1},{1,0},{2,3},{3,2},{4,5},{5,4},{6,7},{7,6},{8,9},{9,8},{10,11... | collective-permute-start | bytes 835592 | tf_op jit(solution)/shard_map/ppermute | solution.py:590
  502.8 17.0 %collective-permute-start.27 = (bf16[128,1024]{1,0:T(8,128)(2,1)}, bf16[128,1024]{1,0:T(8,128)(2,1)}, u32[]{:S(2)}, u32[]{:S(2)}) collective-permute-start(bf16[128,1024]{1,0:T(8,128)(2,1)} %get-tuple-element.77), channel_id=1, source_target_pairs={{0,8},{1,9},{2,10},{3,11},{4,12},{5,13},{6,14},{7,15},{8,0},{9,1},... | collective-permute-start | bytes 786440 | tf_op jit(solution)/shard_map/ppermute | solution.py:590
  502.8 17.0 %collective-permute-start.29 = (bf16[128,1024]{1,0:T(8,128)(2,1)}, bf16[128,1024]{1,0:T(8,128)(2,1)}, u32[]{:S(2)}, u32[]{:S(2)}) collective-permute-start(bf16[128,1024]{1,0:T(8,128)(2,1)} %get-tuple-element.78), channel_id=1, source_target_pairs={{0,24},{1,25},{2,26},{3,27},{4,28},{5,29},{6,30},{7,31},{8,16},{9,... | collective-permute-start | bytes 786440 | tf_op jit(solution)/shard_map/ppermute | solution.py:590
  504.5 20.4 %collective-permute-start.28 = (bf16[128,1024]{1,0:T(8,128)(2,1)}, bf16[128,1024]{1,0:T(8,128)(2,1)}, u32[]{:S(2)}, u32[]{:S(2)}) collective-permute-start(bf16[128,1024]{1,0:T(8,128)(2,1)} %get-tuple-element.79), channel_id=1, source_target_pairs={{0,16},{1,17},{2,18},{3,19},{4,20},{5,21},{6,22},{7,23},{8,24},{9,... | collective-permute-start | bytes 786440 | tf_op jit(solution)/shard_map/ppermute | solution.py:590
  510.1 25.3 %all-to-all-start.3 = ((bf16[8,128,1024]{2,1,0:T(8,128)(2,1)}), bf16[8,128,1024]{2,1,0:T(8,128)(2,1)}, u32[]{:S(2)}, u32[]{:S(2)}) async-start(bf16[8,128,1024]{2,1,0:T(8,128)(2,1)} %bitcast.156), calls=%async_computation.3 | async-start | bytes 4194304 | tf_op jit(solution)/shard_map/all_to_all | solution.py:652
  (16 other events, 211.6 us)
Sparse Core Ops, SparseCore 0:
  14.3 91.6 all-gather.3
  109.4 110.5 all-gather.5

commit v3 on v2

--- a/solution.py
+++ b/solution.py
@@ -499,14 +499,14 @@
 
 
 def out_kernel(
-    core_ref, z_ref, down_ref, ctx_ref, out_ref, x_ref, bias_ref, kept_ref, sent_ref, value_s
+    core_ref, z_ref, down_ref, attended_ref, x_ref, bias_ref, kept_ref, sent_ref, value_s
 ):
     def product(here):
         down = stacked(down_ref, slice(0, z_ref.shape[1]), here)
-        return dot_nn(z_ref[...], down) + dot_nn(ctx_ref[...], out_ref[:, here])
+        return dot_nn(z_ref[...], down)
 
     def split(here, value):
-        value_s[...] = value
+        value_s[...] = value + attended_ref[:, here].astype(F32)
         split_rows(
             core_ref[0],
             value_s,
@@ -516,12 +516,12 @@
             lambda p: x_ref[p, 0, :, here].astype(F32) + bias_ref[:, here],
         )
 
-    pipelined(starts(out_ref.shape[1]), product, split)
-
-
-def out_project(core, z, shared, context, w_out, x_mine, bias, planes, per_chip, rows):
+    pipelined(starts(attended_ref.shape[1]), product, split)
+
+
+def out_project(core, z, shared, attended, x_mine, bias, planes, per_chip, rows):
     count, hidden = z.shape
-    inner, width = w_out.shape
+    width = attended.shape[1]
     group = math.gcd(planes, 2)
     grid, piece, block = token_specs(planes, per_chip, rows, width, group)
     shape = (planes, per_chip, rows, width)
@@ -534,8 +534,7 @@
             in_specs=[
                 block(hidden),
                 shared_specs(shared)[2],
-                block(inner),
-                pl.BlockSpec((inner, width), lambda s, p, core: (0, 0)),
+                block(width),
                 piece,
                 pl.BlockSpec((1, width), lambda s, p, core: (0, 0)),
             ],
@@ -543,12 +542,12 @@
             scratch_shapes=[pltpu.VMEM((2 * group * rows, math.gcd(width, 512)), F32)],
         ),
         cost_estimate=pl.CostEstimate(
-            flops=2 * count * width * (hidden + inner),
-            bytes_accessed=2 * count * (hidden + inner + 4 * width),
+            flops=2 * count * width * hidden,
+            bytes_accessed=2 * count * (hidden + 5 * width),
             transcendentals=0,
         ),
         compiler_params=pltpu.CompilerParams(vmem_limit_bytes=60 << 20),
-    )(core.reshape(1), z, shared, context, w_out, x_mine.reshape(shape), bias)
+    )(core.reshape(1), z, shared, attended, x_mine.reshape(shape), bias)
 
 
 def ordered(value, *before):
@@ -723,6 +722,8 @@
     sums = lax.all_to_all(sums, AXES, split_axis=0, concat_axis=0, tiled=True)
     sums = jnp.sum(sums, 0)
 
+    attended = dot_nn(context, w_out).astype(BF)
+
     z, slope = up_project(a_two, shared, b_in[None], block)
     down_w_grad = dot_tn(z, dy).astype(BF)
     down_w_grad = plane_then_deep(down_w_grad)
@@ -738,9 +739,9 @@
     )
     in_w_grad = jnp.concatenate(
         [
-            plane_then_deep(in_w_grad[:, : 3 * hidden // 4]),
+            plane_then_deep(in_w_grad[:, : 15 * hidden // 16]),
             deep_then_plane(
-                jnp.concatenate([in_w_grad[:, 3 * hidden // 4 :], riders.astype(BF)], 1)
+                jnp.concatenate([in_w_grad[:, 15 * hidden // 16 :], riders.astype(BF)], 1)
             ),
         ],
         1,
@@ -750,7 +751,7 @@
     ln2_grads = (in_w_own + in_w_other)[:, hidden : hidden + 2]
     in_w_grad = weave(first_core, in_w_own, in_w_other, chips, hidden)
     kept, sent = out_project(
-        core, z, shared, context, w_out, x_mine, (b_out + b_down)[None], planes, per_chip, rows_here
+        core, z, shared, attended, x_mine, (b_out + b_down)[None], planes, per_chip, rows_here
     )
     output = to_tokens(kept, sent)
 

time: 560 us -> 581 us (1.038)
  waiting for transfers between devices: 165 us -> 198 us
  starting transfers between devices: 60.8 us -> 52.2 us
    ppermute x30, waiting for transfers between devices: 88.2 us -> 109 us  [swap(): return lax.ppermute(value, AXES, [(i, i ^ mask) for i in range(n)])]
    all_to_all x2, waiting for transfers between devices: 5.07 us -> 18.1 us  [to_tokens(): return lax.all_to_all(value, 'pl', split_axis=0, concat_axis=0, tiled=True)]
    all_to_all x1, starting transfers between devices: 11 us -> 2.57 us  [local(): sums = lax.all_to_all(sums, AXES, split_axis=0, concat_axis=0, tiled=True)]
    dot_general x1 -> x2, matrix products: 11.6 us -> 18.2 us  [dot_nn(): lax.dot_general(left, right, (((1,), (0,)), ((), ())), preferred_element_...]
  transfers between devices with their start and end apart: 38 -> 38, of which waited for: 14 -> 15; matrix products, arithmetic and copies ran while one was open for 19% -> 18% of each run, Pallas kernels for 16% -> 15%
where the time goes in v3:
time: 581 us; the launch traced here: 573 us
  waiting for transfers between devices  198 us (34%)
  Pallas kernels  138 us (24%)
  matrix products  59.3 us (10%)
  starting transfers between devices  52.2 us (9%)
  other arithmetic  39.8 us (7%)
  local copies, waits for them, and re-layouts  37.7 us (6%)
  blocking collectives  32.7 us (6%)
  between operations  15.1 us (3%)
    ppermute x30, waiting for transfers between devices, swap(): return lax.ppermute(value, AXES, [(i, i ^ mask) for i in range(n)])  109 us
    pallas_call x1, Pallas kernels, attention(): pl.pallas_call(functools.partial(attention_kernel, math.gcd(length, 256))...  43.8 us
    dot_general x4, matrix products, dot_tn(): lax.dot_general(left, right, (((0,), (0,)), ((), ())), preferred_element_...  37.2 us
    all_to_all x1, waiting for transfers between devices, to_chip(): mine = lax.all_to_all(value, 'pl', split_axis=0, concat_axis=0, tiled=True)  34.2 us
    all_to_all x1, blocking collectives, to_chip(): mine = lax.all_to_all(value, 'pl', split_axis=0, concat_axis=0, tiled=True)  32.7 us
    all_to_all x1, waiting for transfers between devices, local(): lax.all_to_all(first_grad, 'pl', split_axis=0, concat_axis=0, tiled=True)  32 us
    ppermute x30, starting transfers between devices, swap(): return lax.ppermute(value, AXES, [(i, i ^ mask) for i in range(n)])  25.9 us
    pallas_call x1, Pallas kernels, up_project(): pl.pallas_call(up_kernel, out_shape=(shape, shape), grid=(count // block,...  19.5 us
  transfers between devices with their start and end apart: 38, of which 15 were waited for; matrix products, arithmetic and copies ran while one was open for 18% of the time, Pallas kernels for 15%

profile of v3, /device:TPU:0, one launch (start us, length us, event | category | flops | bytes accessed | tf_op | source)
XLA Modules:
  0.0 572.5 jit_solution(8646871803643610707)
XLA Ops:
  14.2 32.7 %all_to_all.43.mine_ref = bf16[8,128,1024]{2,1,0:T(8,128)(2,1)} all-to-all(bf16[8,128,1024]{2,1,0:T(8,128)(2,1)S(1)} %copy-done), channel_id=1, replica_groups=mesh['dp'=4,'pl'=4,'core'=2] {'pl'}, dimensions={0} | all-to-all | bytes 4194304 | tf_op jit(solution)/shard_map/all_to_all | solution.py:645
  47.0 4.6 all-to-all-start.2
  52.6 34.2 %all-to-all-done.2.mine_ref = bf16[8,128,1024]{2,1,0:T(8,128)(2,1)} async-done(((bf16[8,128,1024]{2,1,0:T(8,128)(2,1)}), bf16[8,128,1024]{2,1,0:T(8,128)(2,1)}, u32[]{:S(2)}, u32[]{:S(2)}) %all-to-all-start.2) | async-done | bytes 2097184 | tf_op jit(solution)/shard_map/all_to_all | solution.py:645
  88.9 4.7 all-to-all-start.1
  93.6 3.0 fusion.20
  96.6 4.5 all-to-all-done.1
  102.6 9.7 %shard_map.245 = (bf16[2048,1024]{1,0:T(8,128)(2,1)}, bf16[2048,1024]{1,0:T(8,128)(2,1)}, bf16[2048,1024]{1,0:T(8,128)(2,1)}) custom-call(s32[1]{0:T(128)} %bitcast.core_ref, bf16[8,128,1024]{2,1,0:T(8,128)(2,1)} %all_to_all.43.mine_ref, bf16[8,128,1024]{2,1,0:T(8,128)(2,1)} %collective-permute-done.1.theirs_ref, f32[4,1024]{1,0:T(4,128)} %pad_maximum_fusion.5.gains_ref), custom_call_target="tpu_custom_call" | custom-call | flops 20971520 | bytes 16777216 | tf_op jit(solution)/shard_map/pallas_call | solution.py:193
  112.3 6.7 %shard_map.247 = (bf16[2048,1024]{1,0:T(8,128)(2,1)}, f32[1,1024]{1,0:T(1,128)}) custom-call(s32[1]{0:T(128)} %bitcast.core_ref, bf16[8,128,1024]{2,1,0:T(8,128)(2,1)} %all-to-all-done.2.mine_ref, bf16[8,128,1024]{2,1,0:T(8,128)(2,1)} %collective-permute-done.2.theirs_ref), custom_call_target="tpu_custom_call" | custom-call | flops 20971520 | bytes 8388608 | tf_op jit(solution)/shard_map/pallas_call | solution.py:193
  120.5 11.7 %add_convert_fusion = bf16[2048,1536]{1,0:T(8,128)(2,1)} fusion(bf16[2048,1024]{1,0:T(8,128)(2,1)} %get-tuple-element.40, f32[1536]{0:T(1024)S(1)} %add.227, bf16[1024,2048]{1,0:T(8,128)(2,1)} %all-gather.4.cloned.1.call-done.w_ref), kind=kOutput, calls=%fused_computation | convolution fusion | flops 6448742400 | bytes 13637632 | tf_op jit(solution)/shard_map/dot_general | solution.py:26
  132.1 3.8 convolution_convert_fusion.4
  136.0 43.8 %shard_map.248 = (bf16[2,1024,512]{2,1,0:T(8,128)(2,1)}, bf16[2,1024,1536]{2,1,0:T(8,128)(2,1)}) custom-call(bf16[2,1024,1536]{2,1,0:T(8,128)(2,1)} %bitcast.179, bf16[2,1024,512]{2,1,0:T(8,128)(2,1)} %bitcast.182, f32[1024,128]{1,0:T(8,128)} %get-tuple-element.107.cos_ref, f32[1024,128]{1,0:T(8,128)} %get-tuple-element.106.sin_a_ref, ...), custom_call_target="tpu_custom_call" | custom-call | flops 15032385536 | bytes 18874368 | tf_op jit(solution)/shard_map/pallas_call | solution.py:139
  179.7 5.4 convolution_convert_fusion.5
  185.7 7.1 %convolution_convert_fusion = bf16[1024,1536]{1,0:T(8,128)(2,1)S(1)} fusion(bf16[2048,1024]{1,0:T(8,128)(2,1)S(1)} %copy-done.29, bf16[2048,1536]{1,0:T(8,128)(2,1)S(1)} %bitcast.178), kind=kOutput, calls=%fused_computation.18 | convolution fusion | flops 6444023808 | bytes 13631488 | tf_op jit(solution)/shard_map/dot_general | solution.py:34
  193.9 2.3 copy.91
  196.2 5.1 all-to-all-start.6
  205.1 11.5 %shard_map.251 = (bf16[2048,1024]{1,0:T(8,128)(2,1)}, f32[2,1024]{1,0:T(2,128)}, f32[1,1536]{1,0:T(1,128)}) custom-call(bf16[2048,1536]{1,0:T(8,128)(2,1)} %bitcast.177, bf16[1024,2048]{1,0:T(8,128)(2,1)} %all-gather.4.cloned.1.call-done.w_ref, bf16[2048,1024]{1,0:T(8,128)(2,1)} %get-tuple-element.48.normed_ref, f32[1,1024]{1,0:T(1,128)} %copy-done.14), custom_call_target="tpu_custom_call" | custom-call | flops 6442450944 | bytes 14680064 | tf_op jit(solution)/shard_map/pallas_call | solution.py:382
  217.6 32.0 %all-to-all-done.6 = bf16[4,4,64,2048]{3,2,1,0:T(8,128)(2,1)} async-done(((bf16[4,4,64,2048]{3,2,1,0:T(8,128)(2,1)}), bf16[4,4,64,2048]{3,2,1,0:T(8,128)(2,1)}, u32[]{:S(2)}, u32[]{:S(2)}) %all-to-all-start.6) | async-done | bytes 4194336 | tf_op jit(solution)/shard_map/all_to_all | solution.py:701
  249.5 3.1 reduce_sum.62
  258.0 2.6 all-to-all-start.5
  260.6 5.9 %collective-permute-done.20 = bf16[64,2048]{1,0:T(8,128)(2,1)} collective-permute-done((bf16[64,2048]{1,0:T(8,128)(2,1)}, bf16[64,2048]{1,0:T(8,128)(2,1)}, u32[]{:S(2)}, u32[]{:S(2)}) %collective-permute-start.20) | collective-permute-done | bytes 262176 | tf_op jit(solution)/shard_map/ppermute | solution.py:589
  268.5 11.6 %collective-permute-done.21 = bf16[64,2048]{1,0:T(8,128)(2,1)} collective-permute-done((bf16[64,2048]{1,0:T(8,128)(2,1)S(1)}, bf16[64,2048]{1,0:T(8,128)(2,1)}, u32[]{:S(2)}, u32[]{:S(2)}) %collective-permute-start.21) | collective-permute-done | bytes 262176 | tf_op jit(solution)/shard_map/ppermute | solution.py:589
  281.5 6.5 %convolution_convert_fusion.2.attended_ref = bf16[2048,1024]{1,0:T(8,128)(2,1)} fusion(bf16[2048,512]{1,0:T(8,128)(2,1)} %bitcast.181, bf16[512,512]{1,0:T(8,128)(2,1)} %copy-done.30, bf16[512,512]{1,0:T(8,128)(2,1)} %copy-done.11, pred[]{:T(512)S(6)} %eq.6), kind=kOutput, calls=%fused_computation.20 | convolution fusion | flops 2154299392 | bytes 7340033 | tf_op jit(solution)/shard_map/dot_general | solution.py:26
  294.2 19.5 %shard_map.246 = (bf16[2048,2048]{1,0:T(8,128)(2,1)}, bf16[2048,2048]{1,0:T(8,128)(2,1)}) custom-call(bf16[2048,1024]{1,0:T(8,128)(2,1)} %get-tuple-element.38.a_ref, bf16[16,256,1024]{2,1,0:T(8,128)(2,1)} %bitcast.144, bf16[16,256,1024]{2,1,0:T(8,128)(2,1)} %bitcast.145, f32[1,2048]{1,0:T(1,128)} %fusion.28.bias_ref), custom_call_target="tpu_custom_call" | custom-call | flops 8589934592 | bytes 25165824 | tf_op jit(solution)/shard_map/pallas_call | solution.py:294
  313.7 15.0 %shard_map.250 = (bf16[2048,2048]{1,0:T(8,128)(2,1)}, f32[1,2048]{1,0:T(1,128)}) custom-call(bf16[2048,1024]{1,0:T(8,128)(2,1)} %get-tuple-element.42.dy_ref, bf16[16,256,1024]{2,1,0:T(8,128)(2,1)} %bitcast.146, bf16[2048,2048]{1,0:T(8,128)(2,1)} %get-tuple-element.46.slope_ref), custom_call_target="tpu_custom_call" | custom-call | flops 8589934592 | bytes 25165824 | tf_op jit(solution)/shard_map/pallas_call | solution.py:337
  328.7 13.1 %convolution_convert_fusion.1 = bf16[1024,2048]{1,0:T(8,128)(2,1)S(1)} fusion(bf16[2048,1024]{1,0:T(8,128)(2,1)} %get-tuple-element.38.a_ref, bf16[2048,2048]{1,0:T(8,128)(2,1)} %get-tuple-element.47.d_ref), kind=kOutput, calls=%fused_computation.19 | convolution fusion | flops 8592031744 | bytes 16777216 | tf_op jit(solution)/shard_map/dot_general | solution.py:34
  341.8 2.5 slice.115
  345.0 15.7 %shard_map.252 = (f32[4,2,128,1024]{3,2,1,0:T(8,128)}, bf16[4,2,128,1024]{3,2,1,0:T(8,128)(2,1)}, f32[2,1024]{1,0:T(2,128)}) custom-call(s32[1]{0:T(128)} %bitcast.core_ref, bf16[2048,2048]{1,0:T(8,128)(2,1)} %get-tuple-element.47.d_ref, bf16[16,256,1024]{2,1,0:T(8,128)(2,1)} %bitcast.147, bf16[16,256,1024]{2,1,0:T(8,128)(2,1)} %bitcast.148, ...), custom_call_target="tpu_custom_call" | custom-call | flops 8589934592 | bytes 25165824 | tf_op jit(solution)/shard_map/pallas_call | solution.py:471
  363.9 2.2 collective-permute-start.13
  366.0 3.0 dynamic-slice_bitcast_fusion.5
  372.0 11.7 %convolution_convert_fusion.3 = bf16[2048,1024]{1,0:T(8,128)(2,1)S(1)} fusion(bf16[2048,2048]{1,0:T(8,128)(2,1)} %get-tuple-element.39.z_ref, bf16[2048,1024]{1,0:T(8,128)(2,1)S(1)} %copy-done.28), kind=kOutput, calls=%fused_computation.21 | convolution fusion | flops 8592031744 | bytes 16777216 | tf_op jit(solution)/shard_map/dot_general | solution.py:34
  389.0 25.5 %collective-permute-done.15 = bf16[64,256]{1,0:T(8,128)(2,1)S(1)} collective-permute-done((bf16[64,256]{1,0:T(8,128)(2,1)S(1)}, bf16[64,256]{1,0:T(8,128)(2,1)S(1)}, u32[]{:S(2)}, u32[]{:S(2)}) %collective-permute-start.15) | collective-permute-done | bytes 32800 | tf_op jit(solution)/shard_map/ppermute | solution.py:589
  420.2 14.6 %shard_map.249 = (f32[4,2,128,1024]{3,2,1,0:T(8,128)}, bf16[4,2,128,1024]{3,2,1,0:T(8,128)(2,1)}) custom-call(s32[1]{0:T(128)} %bitcast.core_ref, bf16[2048,2048]{1,0:T(8,128)(2,1)} %get-tuple-element.39.z_ref, bf16[16,256,1024]{2,1,0:T(8,128)(2,1)} %bitcast.149, bf16[2048,1024]{1,0:T(8,128)(2,1)} %convolution_convert_fusion.2.attended_ref, ...), custom_call_target="tpu_custom_call" | custom-call | flops 8589934592 | bytes 29360128 | tf_op jit(solution)/shard_map/pallas_call | solution.py:528
  435.5 6.3 %collective-permute-done.7 = bf16[4,64,1920]{2,1,0:T(8,128)(2,1)} collective-permute-done((bf16[4,64,1920]{2,1,0:T(8,128)(2,1)}, bf16[4,64,1920]{2,1,0:T(8,128)(2,1)}, u32[]{:S(2)}, u32[]{:S(2)}) %collective-permute-start.7) | collective-permute-done | bytes 983072 | tf_op jit(solution)/shard_map/ppermute | solution.py:589
  441.8 2.6 fusion.14
  446.5 17.6 %collective-permute-done.26 = bf16[4,128,1024]{2,1,0:T(8,128)(2,1)} collective-permute-done((bf16[4,128,1024]{2,1,0:T(8,128)(2,1)}, bf16[4,128,1024]{2,1,0:T(8,128)(2,1)}, u32[]{:S(2)}, u32[]{:S(2)}) %collective-permute-start.26) | collective-permute-done | bytes 1048608 | tf_op jit(solution)/shard_map/ppermute | solution.py:589
  465.4 18.6 %collective-permute-done.25 = bf16[4,128,1024]{2,1,0:T(8,128)(2,1)} collective-permute-done((bf16[4,128,1024]{2,1,0:T(8,128)(2,1)S(1)}, bf16[4,128,1024]{2,1,0:T(8,128)(2,1)}, u32[]{:S(2)}, u32[]{:S(2)}) %collective-permute-start.25) | collective-permute-done | bytes 1048608 | tf_op jit(solution)/shard_map/ppermute | solution.py:589
  484.9 3.1 fusion.11
  489.8 3.8 add_convert_fusion.1
  493.5 4.5 all-to-all-start.4
  498.0 2.7 collective-permute-start.29
  503.1 6.0 %collective-permute-done.29 = bf16[128,1024]{1,0:T(8,128)(2,1)S(1)} collective-permute-done((bf16[128,1024]{1,0:T(8,128)(2,1)}, bf16[128,1024]{1,0:T(8,128)(2,1)S(1)}, u32[]{:S(2)}, u32[]{:S(2)}) %collective-permute-start.29) | collective-permute-done | bytes 262176 | tf_op jit(solution)/shard_map/ppermute | solution.py:589
  509.1 12.8 %collective-permute-done.28 = bf16[128,1024]{1,0:T(8,128)(2,1)S(1)} collective-permute-done((bf16[128,1024]{1,0:T(8,128)(2,1)}, bf16[128,1024]{1,0:T(8,128)(2,1)S(1)}, u32[]{:S(2)}, u32[]{:S(2)}) %collective-permute-start.28) | collective-permute-done | bytes 262176 | tf_op jit(solution)/shard_map/ppermute | solution.py:589
  523.8 3.8 add_convert_fusion.2
  527.6 4.8 all-to-all-start.3
  535.8 3.4 convert_reduce_fusion
  539.2 18.1 %all-to-all-done.3 = bf16[8,128,1024]{2,1,0:T(8,128)(2,1)} async-done(((bf16[8,128,1024]{2,1,0:T(8,128)(2,1)}), bf16[8,128,1024]{2,1,0:T(8,128)(2,1)}, u32[]{:S(2)}, u32[]{:S(2)}) %all-to-all-start.3) | async-done | bytes 2097184 | tf_op jit(solution)/shard_map/all_to_all | solution.py:651
  557.3 4.6 fusion.5
  562.4 3.1 copy.99
  (222 shorter events, 66.8 us)
Async XLA Ops:
  7.2 111.8 %all-gather.4.cloned.1.call-start = ((), (), s32[]{:S(2)}) async-start(), calls=%async_computation.7 | async-start | bytes 4456448 | tf_op jit(solution)/shard_map/all_gather | solution.py:613
  11.7 1.7 collective-permute-start
  46.9 39.9 %copy-start.19 = (bf16[32]{0:T(256)(128)(2,1)S(1)}, bf16[32]{0:T(256)(128)(2,1)}, u32[]{:S(2)}) copy-start(bf16[32]{0:T(256)(128)(2,1)} %param.16) | copy-start | bytes 196
  46.9 39.9 %copy-start.20 = (bf16[32]{0:T(256)(128)(2,1)S(1)}, bf16[32]{0:T(256)(128)(2,1)}, u32[]{:S(2)}) copy-start(bf16[32]{0:T(256)(128)(2,1)} %param.17) | copy-start | bytes 196
  46.9 39.9 %copy-start.21 = (bf16[32]{0:T(256)(128)(2,1)S(1)}, bf16[32]{0:T(256)(128)(2,1)}, u32[]{:S(2)}) copy-start(bf16[32]{0:T(256)(128)(2,1)} %param.18) | copy-start | bytes 196
  46.9 39.9 %copy-start.22 = (bf16[32]{0:T(256)(128)(2,1)S(1)}, bf16[32]{0:T(256)(128)(2,1)}, u32[]{:S(2)}) copy-start(bf16[32]{0:T(256)(128)(2,1)} %param.22) | copy-start | bytes 196
  46.9 39.9 %copy-start.23 = (bf16[32]{0:T(256)(128)(2,1)S(1)}, bf16[32]{0:T(256)(128)(2,1)}, u32[]{:S(2)}) copy-start(bf16[32]{0:T(256)(128)(2,1)} %param.26) | copy-start | bytes 196
  47.0 39.9 %copy-start.24 = (bf16[96]{0:T(256)(128)(2,1)S(1)}, bf16[96]{0:T(256)(128)(2,1)}, u32[]{:S(2)}) copy-start(bf16[96]{0:T(256)(128)(2,1)} %param.20) | copy-start | bytes 580
  47.0 39.9 %copy-start.25 = (bf16[128]{0:T(256)(128)(2,1)S(1)}, bf16[128]{0:T(256)(128)(2,1)}, u32[]{:S(2)}) copy-start(bf16[128]{0:T(256)(128)(2,1)} %param.24) | copy-start | bytes 772
  47.0 39.8 %all-to-all-start.2 = ((bf16[8,128,1024]{2,1,0:T(8,128)(2,1)}), bf16[8,128,1024]{2,1,0:T(8,128)(2,1)}, u32[]{:S(2)}, u32[]{:S(2)}) async-start(bf16[8,128,1024]{2,1,0:T(8,128)(2,1)} %param.27), calls=%async_computation.2 | async-start | bytes 4194304 | tf_op jit(solution)/shard_map/all_to_all | solution.py:645
  51.6 242.6 %all-gather.6.cloned.1.call-start = ((), (), s32[]{:S(2)}) async-start(), calls=%async_computation.8 | async-start | bytes 8912896 | tf_op jit(solution)/shard_map/all_gather | solution.py:638
  52.6 50.0 %collective-permute-start.1 = (bf16[8,128,1024]{2,1,0:T(8,128)(2,1)}, bf16[8,128,1024]{2,1,0:T(8,128)(2,1)}, u32[]{:S(2)}, u32[]{:S(2)}) collective-permute-start(bf16[8,128,1024]{2,1,0:T(8,128)(2,1)} %all_to_all.43.mine_ref), channel_id=1, source_target_pairs={{0,1},{1,0},{2,3},{3,2},{4,5},{5,4},{6,7},{7,6},{8,9},{9,8},{10,11... | collective-permute-start | bytes 6291464 | tf_op jit(solution)/shard_map/ppermute | solution.py:589
  86.8 25.5 %collective-permute-start.2 = (bf16[8,128,1024]{2,1,0:T(8,128)(2,1)}, bf16[8,128,1024]{2,1,0:T(8,128)(2,1)}, u32[]{:S(2)}, u32[]{:S(2)}) collective-permute-start(bf16[8,128,1024]{2,1,0:T(8,128)(2,1)} %all-to-all-done.2.mine_ref), channel_id=1, source_target_pairs={{0,1},{1,0},{2,3},{3,2},{4,5},{5,4},{6,7},{7,6},{8,9},{9,8},{10,11... | collective-permute-start | bytes 6291464 | tf_op jit(solution)/shard_map/ppermute | solution.py:589
  88.9 12.2 %all-to-all-start.1 = ((bf16[32,2,208]{2,1,0:T(2,128)(2,1)}), bf16[32,2,208]{2,1,0:T(2,128)(2,1)S(1)}, u32[]{:S(2)}, u32[]{:S(2)}) async-start(bf16[32,2,208]{2,1,0:T(2,128)(2,1)} %reshape.292), calls=%async_computation.1 | async-start | bytes 65536 | tf_op jit(solution)/shard_map/all_to_all | solution.py:619
  120.3 11.8 %collective-permute-start.3 = (bf16[512,512]{1,0:T(8,128)(2,1)S(1)}, bf16[512,512]{1,0:T(8,128)(2,1)S(1)}, u32[]{:S(2)}, u32[]{:S(2)}) collective-permute-start(bf16[512,512]{1,0:T(8,128)(2,1)S(1)} %get-tuple-element.70), channel_id=1, source_target_pairs={{0,1},{1,0},{2,3},{3,2},{4,5},{5,4},{6,7},{7,6},{8,9},{9,8},{10,11... | collective-permute-start | bytes 1572872 | tf_op jit(solution)/shard_map/ppermute | solution.py:589
  185.2 7.6 %collective-permute-start.19 = (bf16[512,512]{1,0:T(8,128)(2,1)S(1)}, bf16[512,512]{1,0:T(8,128)(2,1)S(1)}, u32[]{:S(2)}, u32[]{:S(2)}) collective-permute-start(bf16[512,512]{1,0:T(8,128)(2,1)S(1)} %get-tuple-element.81), channel_id=1, source_target_pairs={{0,1},{1,0},{2,3},{3,2},{4,5},{5,4},{6,7},{7,6},{8,9},{9,8},{10,11... | collective-permute-start | bytes 1572872 | tf_op jit(solution)/shard_map/ppermute | solution.py:589
  196.2 53.3 %all-to-all-start.6 = ((bf16[4,4,64,2048]{3,2,1,0:T(8,128)(2,1)}), bf16[4,4,64,2048]{3,2,1,0:T(8,128)(2,1)}, u32[]{:S(2)}, u32[]{:S(2)}) async-start(bf16[4,4,64,2048]{3,2,1,0:T(8,128)(2,1)} %bitcast.150), calls=%async_computation.6 | async-start | bytes 8388608 | tf_op jit(solution)/shard_map/all_to_all | solution.py:701
  216.7 40.4 %copy-start.16 = (f32[2,1024]{1,0:T(2,128)S(1)}, f32[2,1024]{1,0:T(2,128)}, u32[]{:S(2)}) copy-start(f32[2,1024]{1,0:T(2,128)} %get-tuple-element.53) | copy-start | bytes 24580
  253.5 12.9 %collective-permute-start.20 = (bf16[64,2048]{1,0:T(8,128)(2,1)}, bf16[64,2048]{1,0:T(8,128)(2,1)}, u32[]{:S(2)}, u32[]{:S(2)}) collective-permute-start(bf16[64,2048]{1,0:T(8,128)(2,1)} %get-tuple-element.77), channel_id=1, source_target_pairs={{0,8},{1,9},{2,10},{3,11},{4,12},{5,13},{6,14},{7,15},{8,0},{9,1},... | collective-permute-start | bytes 786440 | tf_op jit(solution)/shard_map/ppermute | solution.py:589
  253.7 14.8 %collective-permute-start.22 = (bf16[64,2048]{1,0:T(8,128)(2,1)}, bf16[64,2048]{1,0:T(8,128)(2,1)}, u32[]{:S(2)}, u32[]{:S(2)}) collective-permute-start(bf16[64,2048]{1,0:T(8,128)(2,1)} %get-tuple-element.78), channel_id=1, source_target_pairs={{0,24},{1,25},{2,26},{3,27},{4,28},{5,29},{6,30},{7,31},{8,16},{9,... | collective-permute-start | bytes 786440 | tf_op jit(solution)/shard_map/ppermute | solution.py:589
  255.3 24.8 %collective-permute-start.21 = (bf16[64,2048]{1,0:T(8,128)(2,1)S(1)}, bf16[64,2048]{1,0:T(8,128)(2,1)}, u32[]{:S(2)}, u32[]{:S(2)}) collective-permute-start(bf16[64,2048]{1,0:T(8,128)(2,1)S(1)} %get-tuple-element.79), channel_id=1, source_target_pairs={{0,16},{1,17},{2,18},{3,19},{4,20},{5,21},{6,22},{7,23},{8,24},{9,... | collective-permute-start | bytes 786440 | tf_op jit(solution)/shard_map/ppermute | solution.py:589
  258.0 30.1 %all-to-all-start.5 = ((f32[32,1,192]{2,1,0:T(1,128)}), f32[32,1,192]{2,1,0:T(1,128)S(1)}, u32[]{:S(2)}, u32[]{:S(2)}) async-start(f32[32,1,192]{2,1,0:T(1,128)} %all_to_all.33), calls=%async_computation.5 | async-start | bytes 65536 | tf_op jit(solution)/shard_map/all_to_all | solution.py:722
  281.4 7.9 %collective-permute-start.23 = (f32[32,2048]{1,0:T(8,128)S(1)}, f32[32,2048]{1,0:T(8,128)S(1)}, u32[]{:S(2)}, u32[]{:S(2)}) collective-permute-start(f32[32,2048]{1,0:T(8,128)S(1)} %get-tuple-element.86), channel_id=1, source_target_pairs={{0,1},{1,0},{2,3},{3,2},{4,5},{5,4},{6,7},{7,6},{8,9},{9,8},{10,11... | collective-permute-start | bytes 786440 | tf_op jit(solution)/shard_map/ppermute | solution.py:589
  289.3 272.6 %copy-start.26 = (f32[32]{0:T(128)}, f32[32]{0:T(128)S(1)}, u32[]{:S(2)}) copy-start(f32[32]{0:T(128)S(1)} %get-tuple-element.161) | copy-start | bytes 388
  362.5 21.2 %collective-permute-start.12 = (bf16[4,64,256]{2,1,0:T(8,128)(2,1)S(1)}, bf16[4,64,256]{2,1,0:T(8,128)(2,1)S(1)}, u32[]{:S(2)}, u32[]{:S(2)}) collective-permute-start(bf16[4,64,256]{2,1,0:T(8,128)(2,1)S(1)} %get-tuple-element.87), channel_id=1, source_target_pairs={{0,8},{1,9},{2,10},{3,11},{4,12},{5,13},{6,14},{7,15},{8,0},{9,1},... | collective-permute-start | bytes 393224 | tf_op jit(solution)/shard_map/ppermute | solution.py:589
  362.6 21.1 %collective-permute-start.14 = (bf16[4,64,256]{2,1,0:T(8,128)(2,1)S(1)}, bf16[4,64,256]{2,1,0:T(8,128)(2,1)S(1)}, u32[]{:S(2)}, u32[]{:S(2)}) collective-permute-start(bf16[4,64,256]{2,1,0:T(8,128)(2,1)S(1)} %get-tuple-element.88), channel_id=1, source_target_pairs={{0,24},{1,25},{2,26},{3,27},{4,28},{5,29},{6,30},{7,31},{8,16},{9,... | collective-permute-start | bytes 393224 | tf_op jit(solution)/shard_map/ppermute | solution.py:589
  363.9 19.8 %collective-permute-start.13 = (bf16[4,64,256]{2,1,0:T(8,128)(2,1)S(1)}, bf16[4,64,256]{2,1,0:T(8,128)(2,1)S(1)}, u32[]{:S(2)}, u32[]{:S(2)}) collective-permute-start(bf16[4,64,256]{2,1,0:T(8,128)(2,1)S(1)} %get-tuple-element.89), channel_id=1, source_target_pairs={{0,16},{1,17},{2,18},{3,19},{4,20},{5,21},{6,22},{7,23},{8,24},{9,... | collective-permute-start | bytes 393224 | tf_op jit(solution)/shard_map/ppermute | solution.py:589
  369.1 48.7 %collective-permute-start.6 = (bf16[4,64,1920]{2,1,0:T(8,128)(2,1)S(1)}, bf16[4,64,1920]{2,1,0:T(8,128)(2,1)S(1)}, u32[]{:S(2)}, u32[]{:S(2)}) collective-permute-start(bf16[4,64,1920]{2,1,0:T(8,128)(2,1)S(1)} %get-tuple-element.71), channel_id=1, source_target_pairs={{0,2},{1,3},{2,0},{3,1},{4,6},{5,7},{6,4},{7,5},{8,10},{9,11},{10,... | collective-permute-start | bytes 2949128 | tf_op jit(solution)/shard_map/ppermute | solution.py:589
  370.5 48.8 %collective-permute-start.8 = (bf16[4,64,1920]{2,1,0:T(8,128)(2,1)S(1)}, bf16[4,64,1920]{2,1,0:T(8,128)(2,1)S(1)}, u32[]{:S(2)}, u32[]{:S(2)}) collective-permute-start(bf16[4,64,1920]{2,1,0:T(8,128)(2,1)S(1)} %get-tuple-element.72), channel_id=1, source_target_pairs={{0,6},{1,7},{2,4},{3,5},{4,2},{5,3},{6,0},{7,1},{8,14},{9,15},{10,... | collective-permute-start | bytes 2949128 | tf_op jit(solution)/shard_map/ppermute | solution.py:589
  383.8 30.7 %collective-permute-start.15 = (bf16[64,256]{1,0:T(8,128)(2,1)S(1)}, bf16[64,256]{1,0:T(8,128)(2,1)S(1)}, u32[]{:S(2)}, u32[]{:S(2)}) collective-permute-start(bf16[64,256]{1,0:T(8,128)(2,1)S(1)} %get-tuple-element.94), channel_id=1, source_target_pairs={{0,2},{1,3},{2,0},{3,1},{4,6},{5,7},{6,4},{7,5},{8,10},{9,11},{10,... | collective-permute-start | bytes 98312 | tf_op jit(solution)/shard_map/ppermute | solution.py:589
  384.5 31.3 %collective-permute-start.17 = (bf16[64,256]{1,0:T(8,128)(2,1)S(1)}, bf16[64,256]{1,0:T(8,128)(2,1)S(1)}, u32[]{:S(2)}, u32[]{:S(2)}) collective-permute-start(bf16[64,256]{1,0:T(8,128)(2,1)S(1)} %get-tuple-element.95), channel_id=1, source_target_pairs={{0,6},{1,7},{2,4},{3,5},{4,2},{5,3},{6,0},{7,1},{8,14},{9,15},{10,... | collective-permute-start | bytes 98312 | tf_op jit(solution)/shard_map/ppermute | solution.py:589
  385.9 30.4 %collective-permute-start.16 = (bf16[64,256]{1,0:T(8,128)(2,1)S(1)}, bf16[64,256]{1,0:T(8,128)(2,1)S(1)}, u32[]{:S(2)}, u32[]{:S(2)}) collective-permute-start(bf16[64,256]{1,0:T(8,128)(2,1)S(1)} %get-tuple-element.96), channel_id=1, source_target_pairs={{0,4},{1,5},{2,6},{3,7},{4,0},{5,1},{6,2},{7,3},{8,12},{9,13},{10,... | collective-permute-start | bytes 98312 | tf_op jit(solution)/shard_map/ppermute | solution.py:589
  414.5 74.5 %collective-permute-start.5 = (bf16[4,2,128,1024]{3,2,1,0:T(8,128)(2,1)}, bf16[4,2,128,1024]{3,2,1,0:T(8,128)(2,1)}, u32[]{:S(2)}, u32[]{:S(2)}) collective-permute-start(bf16[4,2,128,1024]{3,2,1,0:T(8,128)(2,1)} %get-tuple-element.52), channel_id=1, source_target_pairs={{0,1},{1,0},{2,3},{3,2},{4,5},{5,4},{6,7},{7,6},{8,9},{9,8},{10,11... | collective-permute-start | bytes 6291464 | tf_op jit(solution)/shard_map/ppermute | solution.py:589
  415.7 26.1 %collective-permute-start.7 = (bf16[4,64,1920]{2,1,0:T(8,128)(2,1)}, bf16[4,64,1920]{2,1,0:T(8,128)(2,1)}, u32[]{:S(2)}, u32[]{:S(2)}) collective-permute-start(bf16[4,64,1920]{2,1,0:T(8,128)(2,1)} %get-tuple-element.73), channel_id=1, source_target_pairs={{0,4},{1,5},{2,6},{3,7},{4,0},{5,1},{6,2},{7,3},{8,12},{9,13},{10,... | collective-permute-start | bytes 2949128 | tf_op jit(solution)/shard_map/ppermute | solution.py:589
  416.3 28.9 %collective-permute-start.24 = (bf16[4,128,1024]{2,1,0:T(8,128)(2,1)}, bf16[4,128,1024]{2,1,0:T(8,128)(2,1)}, u32[]{:S(2)}, u32[]{:S(2)}) collective-permute-start(bf16[4,128,1024]{2,1,0:T(8,128)(2,1)} %get-tuple-element.66), channel_id=1, source_target_pairs={{0,2},{1,3},{2,0},{3,1},{4,6},{5,7},{6,4},{7,5},{8,10},{9,11},{10,... | collective-permute-start | bytes 3145736 | tf_op jit(solution)/shard_map/ppermute | solution.py:589
  417.7 46.4 %collective-permute-start.26 = (bf16[4,128,1024]{2,1,0:T(8,128)(2,1)}, bf16[4,128,1024]{2,1,0:T(8,128)(2,1)}, u32[]{:S(2)}, u32[]{:S(2)}) collective-permute-start(bf16[4,128,1024]{2,1,0:T(8,128)(2,1)} %get-tuple-element.67), channel_id=1, source_target_pairs={{0,6},{1,7},{2,4},{3,5},{4,2},{5,3},{6,0},{7,1},{8,14},{9,15},{10,... | collective-permute-start | bytes 3145736 | tf_op jit(solution)/shard_map/ppermute | solution.py:589
  419.2 64.7 %collective-permute-start.25 = (bf16[4,128,1024]{2,1,0:T(8,128)(2,1)S(1)}, bf16[4,128,1024]{2,1,0:T(8,128)(2,1)}, u32[]{:S(2)}, u32[]{:S(2)}) collective-permute-start(bf16[4,128,1024]{2,1,0:T(8,128)(2,1)S(1)} %get-tuple-element.68), channel_id=1, source_target_pairs={{0,4},{1,5},{2,6},{3,7},{4,0},{5,1},{6,2},{7,3},{8,12},{9,13},{10,... | collective-permute-start | bytes 3145736 | tf_op jit(solution)/shard_map/ppermute | solution.py:589
  441.8 82.0 %collective-permute-start.4 = (bf16[4,2,128,1024]{3,2,1,0:T(8,128)(2,1)}, bf16[4,2,128,1024]{3,2,1,0:T(8,128)(2,1)}, u32[]{:S(2)}, u32[]{:S(2)}) collective-permute-start(bf16[4,2,128,1024]{3,2,1,0:T(8,128)(2,1)} %get-tuple-element.45), channel_id=1, source_target_pairs={{0,1},{1,0},{2,3},{3,2},{4,5},{5,4},{6,7},{7,6},{8,9},{9,8},{10,11... | collective-permute-start | bytes 6291464 | tf_op jit(solution)/shard_map/ppermute | solution.py:589
  444.4 45.4 %copy-start.1 = (f32[4,2,128,1024]{3,2,1,0:T(8,128)S(1)}, f32[4,2,128,1024]{3,2,1,0:T(8,128)}, u32[]{:S(2)}) copy-start(f32[4,2,128,1024]{3,2,1,0:T(8,128)} %get-tuple-element.51) | copy-start | bytes 12582916
  445.2 52.8 %collective-permute-start.9 = (bf16[64,1920]{1,0:T(8,128)(2,1)}, bf16[64,1920]{1,0:T(8,128)(2,1)}, u32[]{:S(2)}, u32[]{:S(2)}) collective-permute-start(bf16[64,1920]{1,0:T(8,128)(2,1)} %get-tuple-element.82), channel_id=1, source_target_pairs={{0,8},{1,9},{2,10},{3,11},{4,12},{5,13},{6,14},{7,15},{8,0},{9,1},... | collective-permute-start | bytes 737288 | tf_op jit(solution)/shard_map/ppermute | solution.py:589
  464.1 36.6 %collective-permute-start.11 = (bf16[64,1920]{1,0:T(8,128)(2,1)}, bf16[64,1920]{1,0:T(8,128)(2,1)}, u32[]{:S(2)}, u32[]{:S(2)}) collective-permute-start(bf16[64,1920]{1,0:T(8,128)(2,1)} %get-tuple-element.83), channel_id=1, source_target_pairs={{0,24},{1,25},{2,26},{3,27},{4,28},{5,29},{6,30},{7,31},{8,16},{9,... | collective-permute-start | bytes 737288 | tf_op jit(solution)/shard_map/ppermute | solution.py:589
  483.9 16.9 %collective-permute-start.10 = (bf16[64,1920]{1,0:T(8,128)(2,1)S(1)}, bf16[64,1920]{1,0:T(8,128)(2,1)}, u32[]{:S(2)}, u32[]{:S(2)}) collective-permute-start(bf16[64,1920]{1,0:T(8,128)(2,1)S(1)} %get-tuple-element.84), channel_id=1, source_target_pairs={{0,16},{1,17},{2,18},{3,19},{4,20},{5,21},{6,22},{7,23},{8,24},{9,... | collective-permute-start | bytes 737288 | tf_op jit(solution)/shard_map/ppermute | solution.py:589
  489.0 14.1 %collective-permute-start.27 = (bf16[128,1024]{1,0:T(8,128)(2,1)}, bf16[128,1024]{1,0:T(8,128)(2,1)}, u32[]{:S(2)}, u32[]{:S(2)}) collective-permute-start(bf16[128,1024]{1,0:T(8,128)(2,1)} %get-tuple-element.74), channel_id=1, source_target_pairs={{0,8},{1,9},{2,10},{3,11},{4,12},{5,13},{6,14},{7,15},{8,0},{9,1},... | collective-permute-start | bytes 786440 | tf_op jit(solution)/shard_map/ppermute | solution.py:589
  493.5 34.1 %all-to-all-start.4 = ((bf16[8,128,1024]{2,1,0:T(8,128)(2,1)}), bf16[8,128,1024]{2,1,0:T(8,128)(2,1)}, u32[]{:S(2)}, u32[]{:S(2)}) async-start(bf16[8,128,1024]{2,1,0:T(8,128)(2,1)} %bitcast.155), calls=%async_computation.4 | async-start | bytes 4194304 | tf_op jit(solution)/shard_map/all_to_all | solution.py:651
  498.0 11.1 %collective-permute-start.29 = (bf16[128,1024]{1,0:T(8,128)(2,1)}, bf16[128,1024]{1,0:T(8,128)(2,1)S(1)}, u32[]{:S(2)}, u32[]{:S(2)}) collective-permute-start(bf16[128,1024]{1,0:T(8,128)(2,1)} %get-tuple-element.75), channel_id=1, source_target_pairs={{0,24},{1,25},{2,26},{3,27},{4,28},{5,29},{6,30},{7,31},{8,16},{9,... | collective-permute-start | bytes 786440 | tf_op jit(solution)/shard_map/ppermute | solution.py:589
  500.7 21.2 %collective-permute-start.28 = (bf16[128,1024]{1,0:T(8,128)(2,1)}, bf16[128,1024]{1,0:T(8,128)(2,1)S(1)}, u32[]{:S(2)}, u32[]{:S(2)}) collective-permute-start(bf16[128,1024]{1,0:T(8,128)(2,1)} %get-tuple-element.76), channel_id=1, source_target_pairs={{0,16},{1,17},{2,18},{3,19},{4,20},{5,21},{6,22},{7,23},{8,24},{9,... | collective-permute-start | bytes 786440 | tf_op jit(solution)/shard_map/ppermute | solution.py:589
  503.1 29.3 %collective-permute-start.18 = (f32[32,2176]{1,0:T(8,128)}, f32[32,2176]{1,0:T(8,128)S(1)}, u32[]{:S(2)}, u32[]{:S(2)}) collective-permute-start(f32[32,2176]{1,0:T(8,128)} %dynamic-slice_bitcast_fusion.6), channel_id=1, source_target_pairs={{0,1},{1,0},{2,3},{3,2},{4,5},{5,4},{6,7},{7,6},{8,9},{9,8},{10,11... | collective-permute-start | bytes 835592 | tf_op jit(solution)/shard_map/ppermute | solution.py:589
  527.6 29.6 %all-to-all-start.3 = ((bf16[8,128,1024]{2,1,0:T(8,128)(2,1)}), bf16[8,128,1024]{2,1,0:T(8,128)(2,1)}, u32[]{:S(2)}, u32[]{:S(2)}) async-start(bf16[8,128,1024]{2,1,0:T(8,128)(2,1)} %bitcast.156), calls=%async_computation.3 | async-start | bytes 4194304 | tf_op jit(solution)/shard_map/all_to_all | solution.py:651
  (23 other events, 306.4 us)
Sparse Core Ops, SparseCore 0:
  14.3 91.7 all-gather.3
  109.5 110.5 all-gather.5
